TPU v7x, 128 devices: a whole 4x4x4 slice. The times are simulated.
128 devices in a mesh: dp: 16 (over y, z), fsdp: 8 (over x, core).
Axes of the slice: x: 4, y: 4, z: 4, core: 2. Of those that a mesh axis runs over, the one named last changes fastest.
Arguments:
- tokens: bfloat16 [128, 8, 64, 768], P(('dp', 'fsdp')), may hold values from -6 to 6
- cotangent: bfloat16 [128, 8, 64, 768], P(('dp', 'fsdp')), may hold values from -6 to 6
- lengths: int32 [128], P(('dp', 'fsdp')), may hold values from 32 to 64
- row_offset: int32 [128], P(('dp', 'fsdp')), may hold values from 0 to 1016
- col_offset: int32 [128], P(('dp', 'fsdp')), may hold values from 0 to 960
- norm_gain: bfloat16 [3, 768], P(None, ('dp', 'fsdp')), may hold values from 0.099609375 to 1.8984375
- norm_bias: bfloat16 [3, 768], P(None, ('dp', 'fsdp')), may hold values from -1.75 to 1.75
- row_qkv: bfloat16 [3, 768, 768], P(None, ('dp', 'fsdp')), may hold values from -0.21875 to 0.21875
- row_out: bfloat16 [768, 768], P(('dp', 'fsdp')), may hold values from -1.25 to 1.25
- row_bias: bfloat16 [3, 768], P(None, ('dp', 'fsdp')), may hold values from -1.75 to 1.75
- col_qkv: bfloat16 [3, 768, 768], P(None, ('dp', 'fsdp')), may hold values from -0.21875 to 0.21875
- col_out: bfloat16 [768, 768], P(('dp', 'fsdp')), may hold values from -0.4375 to 0.4375
- col_bias: bfloat16 [3, 768], P(None, ('dp', 'fsdp')), may hold values from -1.75 to 1.75
- ffn_up: bfloat16 [768, 3072], P(('dp', 'fsdp')), may hold values from -0.21875 to 0.21875
- up_bias: bfloat16 [3072], P(('dp', 'fsdp')), may hold values from -1.75 to 1.75
- ffn_down: bfloat16 [3072, 768], P(('dp', 'fsdp')), may hold values from -0.15625 to 0.15625
- down_bias: bfloat16 [768], P(('dp', 'fsdp')), may hold values from -1.75 to 1.75
- pos_tables: bfloat16 [2, 1024, 768], P(None, ('dp', 'fsdp')), may hold values from -3 to 3
Outputs:
- activations: bfloat16 [128, 8, 64, 768], P(('dp', 'fsdp'))
- tokens_grad: float32 [128, 8, 64, 768], P(('dp', 'fsdp'))
- norm_gain_grad: float32 [3, 768], P(None, ('dp', 'fsdp'))
- norm_bias_grad: float32 [3, 768], P(None, ('dp', 'fsdp'))
- row_qkv_grad: float32 [3, 768, 768], P(None, ('dp', 'fsdp'))
- row_out_grad: float32 [768, 768], P(('dp', 'fsdp'))
- row_bias_grad: float32 [3, 768], P(None, ('dp', 'fsdp'))
- col_qkv_grad: float32 [3, 768, 768], P(None, ('dp', 'fsdp'))
- col_out_grad: float32 [768, 768], P(('dp', 'fsdp'))
- col_bias_grad: float32 [3, 768], P(None, ('dp', 'fsdp'))
- ffn_up_grad: float32 [768, 3072], P(('dp', 'fsdp'))
- up_bias_grad: float32 [3072], P(('dp', 'fsdp'))
- ffn_down_grad: float32 [3072, 768], P(('dp', 'fsdp'))
- down_bias_grad: float32 [768], P(('dp', 'fsdp'))
- pos_tables_grad: float32 [2, 1024, 768], P(None, ('dp', 'fsdp'))
All inputs are finite; a program needn't handle non-finite values.
Results may differ from a plain program's by a relative error of at most 0.018.
Values may be sent and summed in bfloat16 or wider, within the bound.
No kernel may reach another device: no remote copies, remote signals or barrier semaphores. Data moves between devices by JAX's collectives and lax.ppermute only.
A program may use at most 256 MiB of HBM per device.

v0:
```python
import math

import jax
import jax.numpy as jnp
from jax import lax
from jax.experimental import pallas as pl
from jax.experimental.pallas import tpu as pltpu
from jax.sharding import Mesh, PartitionSpec as P

AXES = ("y", "z", "x", "c")
DEVICES = 128
GROUPS = 32
MEMBERS = 4
D = 768
FF = 3072
HEAD_DIM = 64
POSITIONS = 1024
ROWS = 8
COLS = 64
TOKENS = ROWS * COLS
SLAB = 24
PACK = 112
PAIRS = 6
EPS = 1e-05
MASKED = -1e30
ROW_SCALE = 1.0 / math.sqrt(HEAD_DIM * ROWS)
COL_SCALE = 1.0 / math.sqrt(HEAD_DIM)
BF16 = jnp.bfloat16
F32 = jnp.float32
GAIN, SHIFT, ROW_BIAS, COL_BIAS, DOWN_BIAS = 0, 3, 6, 9, 12
A1, Q1, K1, V1, M1, A2, Q2, K2, V2, M2 = range(10)


def dot(left, right):
    return jnp.dot(left, right, preferred_element_type=F32)


def dot_nt(left, right):
    return lax.dot_general(left, right, (((1,), (1,)), ((), ())), preferred_element_type=F32)


def dot_tn(left, right):
    return lax.dot_general(left, right, (((0,), (0,)), ((), ())), preferred_element_type=F32)


def chunk(index, size):
    return pl.ds(pl.multiple_of(index * size, size), size)


def loop(count, body, unroll=1):
    def step(index, carry):
        body(index)
        return carry

    lax.fori_loop(0, count, step, 0, unroll=unroll)


def unit_of(hidden):
    centred = hidden - jnp.mean(hidden, axis=-1, keepdims=True)
    inverse = lax.rsqrt(jnp.mean(centred * centred, axis=-1, keepdims=True) + EPS)
    return centred * inverse, inverse


def norm(hidden, small, which):
    unit, _ = unit_of(hidden)
    gain, shift = small[GAIN + which : GAIN + which + 1, :], small[SHIFT + which : SHIFT + which + 1, :]
    return (unit * gain + shift).astype(BF16)


def norm_back(grad, hidden, gain):
    unit, inverse = unit_of(hidden)
    inner = grad * gain
    mean = jnp.mean(inner, axis=-1, keepdims=True)
    cross = jnp.mean(inner * unit, axis=-1, keepdims=True)
    return inverse * (inner - mean - unit * cross), grad * unit


def total(value):
    return jnp.sum(value, axis=0, keepdims=True)


def first_head(shape):
    return (lax.broadcasted_iota(jnp.int32, shape, 1) & 127) < HEAD_DIM


def stack_heads(value):
    keep = jnp.where(first_head(value.shape), 1.0, 0.0)
    return jnp.concatenate([value * keep.astype(BF16), value * (1.0 - keep).astype(BF16)], axis=0)


def merge_heads(value):
    half = value.shape[0] // 2
    return jnp.where(first_head((half, value.shape[1])), value[:half], value[half:])


def softmax(scores):
    top = jnp.max(scores, axis=-1, keepdims=True)
    raised = jnp.exp(scores - top)
    return raised / jnp.sum(raised, axis=-1, keepdims=True)


class RowHeads:
    scale = ROW_SCALE
    steps = 2

    def __init__(self, length):
        self.length = length

    def blocks(self, step):
        return [chunk(3 * step + i, 128) for i in range(3)]

    def load(self, ref, plane, lanes):
        return jnp.concatenate(
            [ref[plane, r * COLS : (r + 1) * COLS, lanes] for r in range(ROWS)], axis=1
        )

    def store(self, ref, plane, lanes, value):
        for r in range(ROWS):
            ref[plane, r * COLS : (r + 1) * COLS, lanes] = value[:, r * 128 : (r + 1) * 128]

    def mask(self):
        shape = (2 * COLS, COLS)
        return lax.broadcasted_iota(jnp.int32, shape, 1) < self.length


class ColHeads:
    scale = COL_SCALE
    steps = PAIRS

    def blocks(self, step):
        return [(i * 16, chunk(step, 128)) for i in range(4)]

    def load(self, ref, plane, block):
        start, lanes = block
        return jnp.concatenate(
            [ref[plane, r * COLS + start : r * COLS + start + 16, lanes] for r in range(ROWS)], axis=0
        )

    def store(self, ref, plane, block, value):
        start, lanes = block
        for r in range(ROWS):
            ref[plane, r * COLS + start : r * COLS + start + 16, lanes] = value[16 * r : 16 * r + 16]

    def mask(self):
        row = lax.broadcasted_iota(jnp.int32, (256, 128), 0) & 15
        return row == (lax.broadcasted_iota(jnp.int32, (256, 128), 1) & 15)


def each(function, *lists):
    return [function(*values) for values in zip(*lists)]


def weights_of(heads, queries, keys):
    mask = heads.mask()
    scores = each(dot_nt, queries, keys)
    return each(lambda s: softmax(jnp.where(mask, s * heads.scale, MASKED)), scores)


def attend(heads, ref, q, k, v, m):
    def body(step):
        blocks = heads.blocks(step)
        queries, keys, values = (
            [heads.load(ref, plane, block) for block in blocks] for plane in (q, k, v)
        )
        probs = weights_of(heads, each(stack_heads, queries), keys)
        mixed = each(lambda p, value: dot(p.astype(BF16), value), probs, values)
        for block, value in zip(blocks, mixed):
            heads.store(ref, m, block, merge_heads(value).astype(BF16))

    loop(heads.steps, body)


def attend_back(heads, ref, q, k, v, dm):
    def body(step):
        blocks = heads.blocks(step)
        queries, keys, values, mixed = (
            [heads.load(ref, plane, block) for block in blocks] for plane in (q, k, v, dm)
        )
        queries, mixed = each(stack_heads, queries), each(stack_heads, mixed)
        probs = weights_of(heads, queries, keys)
        grad = each(dot_nt, mixed, values)
        grad_values = each(lambda p, value: dot_tn(p.astype(BF16), value), probs, mixed)
        inner = each(
            lambda p, g: (p * (g - jnp.sum(g * p, axis=-1, keepdims=True))).astype(BF16), probs, grad
        )
        grad_queries = each(lambda i, key: merge_heads(dot(i, key)) * heads.scale, inner, keys)
        grad_keys = each(lambda i, query: dot_tn(i, query) * heads.scale, inner, queries)
        for i, block in enumerate(blocks):
            heads.store(ref, q, block, grad_queries[i].astype(BF16))
            heads.store(ref, k, block, grad_keys[i].astype(BF16))
            heads.store(ref, v, block, grad_values[i].astype(BF16))

    loop(heads.steps, body)


def whole(ref, index):
    return ref[index].reshape(D, D)


def project(ref, source, planes, weights, first, small, bias_row):
    def body(index):
        rows = chunk(index, 256)
        normed = ref[source, rows, :]
        for i, plane in enumerate(planes):
            value = dot(normed, whole(weights, first + i))
            if i != 1:
                row = bias_row + (0 if i == 0 else 1)
                value = value + small[row : row + 1, :]
            ref[plane, rows, :] = value.astype(BF16)

    loop(2, body)


def by_halves(grads, which, index, value):
    value = value.astype(BF16).reshape(8, 2, SLAB, D)
    for half in range(2):
        grads[which, pl.ds(16 * half + 8 * index, 8)] = value[:, half]


class Copies:
    def __init__(self, sems):
        self.sems, self.used = sems, 0

    def start(self, source, target):
        copy = pltpu.make_async_copy(source, target, self.sems.at[self.used])
        self.used += 1
        copy.start()
        return copy

    def send(self, core, parity, source, own, other):
        sem = self.sems.at[self.used]
        self.used += 1
        here = pltpu.make_async_copy(source, own, sem)
        there = pltpu.make_async_copy(source, other, sem)
        pl.when(core == parity)(here.start)
        pl.when(core != parity)(there.start)
        return here


def position_rows(window, offset, count):
    shape = (count, window.shape[0])
    pick = lax.broadcasted_iota(jnp.int32, shape, 1) == (
        lax.broadcasted_iota(jnp.int32, shape, 0) + offset % 8
    )
    return dot(jnp.where(pick, 1.0, 0.0).astype(BF16), window)


def forward_kernel(
    ints, tokens, cotangent, small, up_bias, gathered,
    act_out, g2_out, saved_out, hidden_out, shares, sums,
    weights, down, window, act, hidden, h2, a3, gy, wide, y, da, sems,
):
    grads = weights
    length, row_offset, col_offset = ints[0], ints[1], ints[2]
    copies = Copies(sems)
    near = []
    for i in range(2):
        dev = jnp.minimum(row_offset // 8 + i, DEVICES - 1)
        near.append(
            copies.start(gathered.at[dev // 4, dev % 4, 96:104, :], window.at[8 * i : 8 * i + 8, :])
        )
    for i in range(9):
        dev = jnp.minimum(col_offset // 8 + i, DEVICES - 1)
        near.append(
            copies.start(
                gathered.at[dev // 4, dev % 4, 104:112, :], window.at[16 + 8 * i : 24 + 8 * i, :]
            )
        )
    loads = [
        copies.start(gathered.at[:, i % 4, 24 * (i // 4) : 24 * (i // 4) + 24, :], weights.at[i])
        for i in range(12)
    ]
    loads += [
        copies.start(gathered.at[8 * f : 8 * f + 8, :, 72:96, :], down.at[f]) for f in range(4)
    ]
    for copy in near:
        copy.wait()
    row_pos = position_rows(window[0:16, :], row_offset, ROWS)
    col_pos = position_rows(window[16:88, :], col_offset, COLS)
    for r in range(ROWS):
        rows = slice(r * COLS, (r + 1) * COLS)
        value = tokens[rows, :].astype(F32) + row_pos[r : r + 1, :] + col_pos
        hidden[0, rows, :] = value
        act[A1, rows, :] = norm(value, small, 0)
    stores = [copies.start(hidden.at[0], hidden_out.at[0]), copies.start(act.at[A1], saved_out.at[A1])]

    def branch(first, source, planes, heads, bias, target, which, last):
        for i in range(3):
            loads[first + i].wait()
        project(act, source, planes[:3], weights, first, small, bias)
        for plane in planes[:3]:
            stores.append(copies.start(act.at[plane], saved_out.at[plane]))
        attend(heads, act, *planes)
        stores.append(copies.start(act.at[planes[3]], saved_out.at[planes[3]]))
        loads[first + 3].wait()

        def body(index):
            rows = chunk(index, 256)
            branch_out = dot(act[planes[3], rows, :], whole(weights, first + 3))
            before = hidden[which - 1, rows, :]
            after = before + (branch_out + small[bias + 2 : bias + 3, :])
            if last:
                h2[rows, :] = after
                a3[rows, :] = norm(after, small, which)
            else:
                hidden[which, rows, :] = after
                act[target, rows, :] = norm(after, small, which)

        loop(2, body)

    branch(0, A1, (Q1, K1, V1, M1), RowHeads(length), ROW_BIAS, A2, 1, False)
    stores.append(copies.start(hidden.at[1], hidden_out.at[1]))
    stores.append(copies.start(act.at[A2], saved_out.at[A2]))
    branch(4, A2, (Q2, K2, V2, M2), ColHeads(), COL_BIAS, None, 2, True)

    in_use = lax.broadcasted_iota(jnp.int32, (COLS, D), 0) < length
    for r in range(ROWS):
        rows = slice(r * COLS, (r + 1) * COLS)
        gy[rows, :] = jnp.where(in_use, cotangent[rows, :].astype(F32), 0.0).astype(BF16)
    for copy in loads[8:]:
        copy.wait()

    def ffn(f):
        up, low = whole(weights, 8 + f), down[f].reshape(D, D)
        bias = up_bias[pl.ds(f, 1), :]

        def body(index):
            rows = chunk(index, 256)
            z = dot(a3[rows, :], up) + bias
            cdf = 0.5 * (1.0 + lax.erf(z * math.sqrt(0.5)))
            slope = cdf + z * (jnp.exp(-0.5 * z * z) * (1.0 / math.sqrt(2.0 * math.pi)))
            u = (z * cdf).astype(BF16)
            wide[0, rows, :] = u
            du = dot_nt(gy[rows, :], low).astype(BF16).astype(F32)
            dz = (du * slope).astype(BF16)
            wide[1, rows, :] = dz
            more, more_da = dot(u, low), dot_nt(dz, up)

            @pl.when(f == 0)
            def _():
                y[rows, :] = more
                da[rows, :] = more_da

            @pl.when(f != 0)
            def _():
                y[rows, :] += more
                da[rows, :] += more_da

        loop(2, body)
        sums[pl.ds(f, 1), :] = total(wide[1].astype(F32))

        def back(index):
            cols = chunk(index, 384)
            value = dot_tn(wide[0, :, cols], gy[...]).astype(BF16).reshape(2, 8, SLAB, D)
            for k in range(8):
                grads[4 + f, pl.ds(4 * k + 2 * index, 2)] = value[:, k]
            by_halves(grads, f, index, dot_tn(a3[:, cols], wide[1]))

        loop(2, back)
        for copy in ffn_sends(f):
            copy.start()

    first_sem = copies.used

    def ffn_sends(f):
        sends = []
        for half in range(2):
            place = (4 * half + f, slice(None), slice(0, SLAB))
            sends.append((grads.at[f, 16 * half : 16 * half + 16], shares.at[place]))
        for k in range(8):
            place = (k, pl.ds(4 * f, 4), slice(SLAB, 2 * SLAB))
            sends.append((grads.at[4 + f, 4 * k : 4 * k + 4], shares.at[place]))
        return [
            pltpu.make_async_copy(source, target, sems.at[first_sem + 10 * f + i])
            for i, (source, target) in enumerate(sends)
        ]

    loop(4, ffn)
    gain = small[GAIN + 2 : GAIN + 3, :]

    def finish(index, carry):
        rows = chunk(index, 64)
        late = h2[rows, :]
        act_out[rows, :] = (late + (y[rows, :] + small[DOWN_BIAS : DOWN_BIAS + 1, :])).astype(BF16)
        grad = da[rows, :]
        inner, unit = norm_back(grad, late, gain)
        cot = gy[rows, :].astype(F32)
        g2_out[rows, :] = cot + inner
        return carry[0] + total(unit), carry[1] + total(grad), carry[2] + total(cot)

    zero = jnp.zeros((1, D), F32)
    gain_sum, shift_sum, down_sum = lax.fori_loop(0, 8, finish, (zero, zero, zero))
    sums[4:5, :] = down_sum
    sums[5:6, :] = gain_sum
    sums[6:7, :] = shift_sum
    sums[7:8, :] = zero
    for copy in stores + [copy for f in range(4) for copy in ffn_sends(f)]:
        copy.wait()


def heads_kernel(column, ints, grad_in, gathered, saved, grads_out, weight, act, sems):
    first, planes = (24, (Q2, K2, V2)) if column else (0, (Q1, K1, V1))
    heads = ColHeads() if column else RowHeads(ints[0])
    copies = Copies(sems)
    load = copies.start(gathered.at[:, 3, first : first + SLAB, :], weight.at[0])
    act_loads = [copies.start(saved.at[plane], act.at[i]) for i, plane in enumerate(planes)]
    load.wait()

    def mixed_back(index):
        rows = chunk(index, 256)
        act[3, rows, :] = dot_nt(grad_in[rows, :].astype(BF16), whole(weight, 0)).astype(BF16)

    loop(2, mixed_back)
    for copy in act_loads:
        copy.wait()
    attend_back(heads, act, 0, 1, 2, 3)
    stores = [copies.start(act.at[i], grads_out.at[i]) for i in range(3)]
    for copy in stores:
        copy.wait()


class Shares:
    def __init__(self, core, copies, own, other):
        self.core, self.copies, self.own, self.other, self.sent = core, copies, own, other, []

    def send(self, grads, member):
        every, parity = slice(None), member % 2
        for half in range(2):
            x = 2 * half + member // 2
            place = (x,) if parity == 0 else (every, x)
            self.sent.append(
                self.copies.send(
                    self.core, parity, grads.at[member, half], self.own.at[place], self.other.at[place]
                )
            )

    def wait(self):
        for copy in self.sent:
            copy.wait()


def keep(grads, which, part, value):
    value = value.astype(BF16).reshape(2, 4, 2, SLAB, D)
    for half in range(2):
        grads[which, half, pl.ds(2 * part, 2)] = value[:, :, half]


def weight_grads(loads, grad_in, act, out_grad, normed, mixed, grads, shares):
    def low(index):
        rows = chunk(index, 128)
        out_grad[rows, :] = grad_in[rows, :].astype(BF16)

    loop(4, low)
    loads["mixed"].wait()

    def out_back(index):
        keep(grads, 3, index, dot_tn(mixed[:, chunk(index, 384)], out_grad[...]))

    loop(2, out_back)
    shares.send(grads, 3)
    loads["normed"].wait()
    for i in range(3):
        loads[i].wait()

    def weight_back(index):
        which, part = index // 2, index % 2
        keep(grads, which, part, dot_tn(normed[:, chunk(part, 384)], act[which]))

    loop(6, weight_back)
    for member in range(3):
        shares.send(grads, member)


def input_grads(loads, grad_in, gain, act, weights, hidden, da, grad_out, sums, lines=None):
    for i in range(3):
        for copy in loads["inputs"][i]:
            copy.wait()

        def input_back(index):
            rows = chunk(index, 256)
            value = dot_nt(act[i, rows, :], whole(weights, i))
            da[rows, :] = value if i == 0 else da[rows, :] + value

        loop(2, input_back)
    loads["hidden"].wait()

    def finish(index, carry):
        rows = chunk(index, 64)
        grad, before = da[rows, :], grad_in[rows, :]
        inner, unit = norm_back(grad, hidden[rows, :], gain)
        value = before + inner
        grad_out[rows, :] = value
        added = [unit, grad, act[0, rows, :], act[2, rows, :], before.astype(BF16)]
        added = [total(extra.astype(F32)) for extra in added]
        if lines is not None:
            lines[pl.ds(index, 1), :] = total(value)
            added.append(value)
        return tuple(a + b for a, b in zip(carry, added))

    carry = (jnp.zeros((1, D), F32),) * 5
    if lines is not None:
        carry = carry + (jnp.zeros((COLS, D), F32),)
    carry = lax.fori_loop(0, 8, finish, carry)
    for i in range(5):
        sums[i : i + 1, :] = carry[i]
    sums[5:8, :] = jnp.zeros((3, D), F32)
    return carry[-1]


def column_kernel(
    ints, grad_in, small, gathered, saved, hidden_saved, grads_in,
    grad_out, own, other, sums,
    weights, act, out_grad, normed, mixed, hidden, da, grads, sems,
):
    copies = Copies(sems)
    shares = Shares(ints[3], copies, own, other)
    loads = {"mixed": copies.start(saved.at[M2], mixed), "normed": copies.start(saved.at[A2], normed)}
    for i in range(3):
        loads[i] = copies.start(grads_in.at[i], act.at[i])
    loads["inputs"] = [
        [copies.start(gathered.at[:, i, SLAB : 2 * SLAB, :], weights.at[i])] for i in range(3)
    ]
    loads["hidden"] = copies.start(hidden_saved.at[1], hidden)
    weight_grads(loads, grad_in, act, out_grad, normed, mixed, grads, shares)
    input_grads(loads, grad_in, small[GAIN + 1 : GAIN + 2, :], act, weights, hidden, da, grad_out, sums)
    shares.wait()


def row_weights_kernel(
    ints, grad_in, saved, grads_in, own, other, act, out_grad, normed, mixed, grads, sems
):
    copies = Copies(sems)
    shares = Shares(ints[3], copies, own, other)
    loads = {"mixed": copies.start(saved.at[M1], mixed), "normed": copies.start(saved.at[A1], normed)}
    for i in range(3):
        loads[i] = copies.start(grads_in.at[i], act.at[i])
    weight_grads(loads, grad_in, act, out_grad, normed, mixed, grads, shares)
    shares.wait()


def row_input_kernel(
    ints, grad_in, small, gathered, hidden_saved, grads_in,
    grad_out, own, other, sums,
    weights, act, hidden, da, zeros, table, lines, sems,
):
    copies = Copies(sems)
    loads = {"inputs": []}
    for i in range(3):
        slab = gathered.at[:, i, 0:SLAB, :]
        loads["inputs"].append(
            [copies.start(grads_in.at[i], act.at[i]), copies.start(slab, weights.at[i])]
        )
    loads["hidden"] = copies.start(hidden_saved.at[0], hidden)
    zeros[...] = jnp.zeros_like(zeros)
    fills = [copies.start(zeros, out) for out in (own, other)]
    gain = small[GAIN : GAIN + 1, :]
    col_lines = input_grads(loads, grad_in, gain, act, weights, hidden, da, grad_out, sums, lines)
    send_tables(ints, copies, fills, lines[...], col_lines, table, own, other)


def send_tables(ints, copies, fills, row_lines, col_lines, table, own, other):
    core = ints[3]

    def placed(values, offset, count):
        shape = (count, values.shape[0])
        here = lax.broadcasted_iota(jnp.int32, shape, 0) == (
            lax.broadcasted_iota(jnp.int32, shape, 1) + offset % 8
        )
        return dot(jnp.where(here, 1.0, 0.0).astype(BF16), values.astype(BF16)).astype(BF16)

    spots = []
    for first, count, values, offset, start in (
        (0, 2, row_lines, ints[1], 0),
        (2, 9, col_lines, ints[2], 8),
    ):
        table[first : first + count] = placed(values, offset, 8 * count).reshape(count, 8, D)
        spots += [(first + i, offset // 8 + i, start) for i in range(count)]
    for copy in fills:
        copy.wait()
    waits = []
    for slot, owner, start in spots:
        real, dev = owner < DEVICES, jnp.minimum(owner, DEVICES - 1)
        x, y, z = (dev // 2) % 4, dev // 32, (dev // 8) % 4
        odd = dev % 2 == 1
        place = (jnp.where(odd, y, x), jnp.where(odd, x, y), z, slice(start, start + 8))
        sem = copies.sems.at[copies.used]
        copies.used += 1
        here = pltpu.make_async_copy(table.at[slot], own.at[place], sem)
        there = pltpu.make_async_copy(table.at[slot], other.at[place], sem)
        pl.when(real & (dev % 2 == core))(here.start)
        pl.when(real & (dev % 2 != core))(there.start)
        waits.append((real, here))
    for real, copy in waits:
        pl.when(real)(copy.wait)


VMEM = pl.BlockSpec(memory_space=pltpu.VMEM)
ANY = pl.BlockSpec(memory_space=pl.ANY)
SMEM = pl.BlockSpec(memory_space=pltpu.SMEM)
SHAPE = jax.ShapeDtypeStruct


def params():
    return pltpu.CompilerParams(vmem_limit_bytes=62 * 1024 * 1024)


def cost(flops, traffic):
    return pl.CostEstimate(flops=flops, transcendentals=0, bytes_accessed=traffic)


def forward_call(ints, tokens, cotangent, small, up_bias, gathered):
    plane = (TOKENS, D)
    return pl.pallas_call(
        forward_kernel,
        name="forward",
        in_specs=[SMEM, VMEM, VMEM, VMEM, VMEM, ANY],
        out_shape=(
            SHAPE(plane, BF16),
            SHAPE(plane, F32),
            SHAPE((10,) + plane, BF16),
            SHAPE((2,) + plane, F32),
            SHAPE((8, 16, 2 * SLAB, D), BF16),
            SHAPE((8, D), F32),
        ),
        out_specs=(VMEM, VMEM, ANY, ANY, ANY, VMEM),
        scratch_shapes=[
            pltpu.VMEM((12, GROUPS, SLAB, D), BF16),
            pltpu.VMEM((4, 8, MEMBERS, SLAB, D), BF16),
            pltpu.VMEM((88, D), BF16),
            pltpu.VMEM((10,) + plane, BF16),
            pltpu.VMEM((2,) + plane, F32),
            pltpu.VMEM(plane, F32),
            pltpu.VMEM(plane, BF16),
            pltpu.VMEM(plane, BF16),
            pltpu.VMEM((2,) + plane, BF16),
            pltpu.VMEM(plane, F32),
            pltpu.VMEM(plane, F32),
            pltpu.SemaphoreType.DMA((96,)),
        ],
        compiler_params=params(),
        cost_estimate=cost(24 * 10**9, 50 * 10**6),
    )(ints, tokens, cotangent, small, up_bias, gathered)


def heads_call(column, ints, grad, gathered, saved):
    plane = (TOKENS, D)
    return pl.pallas_call(
        lambda *refs: heads_kernel(column, *refs),
        name="column_heads" if column else "row_heads",
        in_specs=[SMEM, VMEM, ANY, ANY],
        out_shape=SHAPE((3,) + plane, BF16),
        out_specs=ANY,
        scratch_shapes=[
            pltpu.VMEM((1, GROUPS, SLAB, D), BF16),
            pltpu.VMEM((4,) + plane, BF16),
            pltpu.SemaphoreType.DMA((8,)),
        ],
        compiler_params=params(),
        cost_estimate=cost(10**10, 10**7),
    )(ints, grad, gathered, saved)


PLANE = (TOKENS, D)


def share_of(rows):
    return SHAPE((4, 4, 4, rows, D), BF16)


def column_call(ints, grad, small, gathered, saved, hidden, grads):
    return pl.pallas_call(
        column_kernel,
        name="column_weights",
        in_specs=[SMEM, VMEM, VMEM, ANY, ANY, ANY, ANY],
        out_shape=(SHAPE(PLANE, F32), share_of(SLAB), share_of(SLAB), SHAPE((8, D), F32)),
        out_specs=(VMEM, ANY, ANY, VMEM),
        scratch_shapes=[
            pltpu.VMEM((3, GROUPS, SLAB, D), BF16),
            pltpu.VMEM((3,) + PLANE, BF16),
            pltpu.VMEM(PLANE, BF16),
            pltpu.VMEM(PLANE, BF16),
            pltpu.VMEM(PLANE, BF16),
            pltpu.VMEM(PLANE, F32),
            pltpu.VMEM(PLANE, F32),
            pltpu.VMEM((4, 2, 4, 4, SLAB, D), BF16),
            pltpu.SemaphoreType.DMA((32,)),
        ],
        compiler_params=params(),
        cost_estimate=cost(10**10, 10**7),
    )(ints, grad, small, gathered, saved, hidden, grads)


def row_weights_call(ints, grad, saved, grads):
    return pl.pallas_call(
        row_weights_kernel,
        name="row_weights",
        in_specs=[SMEM, VMEM, ANY, ANY],
        out_shape=(share_of(SLAB), share_of(SLAB)),
        out_specs=(ANY, ANY),
        scratch_shapes=[
            pltpu.VMEM((3,) + PLANE, BF16),
            pltpu.VMEM(PLANE, BF16),
            pltpu.VMEM(PLANE, BF16),
            pltpu.VMEM(PLANE, BF16),
            pltpu.VMEM((4, 2, 4, 4, SLAB, D), BF16),
            pltpu.SemaphoreType.DMA((32,)),
        ],
        compiler_params=params(),
        cost_estimate=cost(10**10, 10**7),
    )(ints, grad, saved, grads)


def row_input_call(ints, grad, small, gathered, hidden, grads):
    return pl.pallas_call(
        row_input_kernel,
        name="row_input",
        in_specs=[SMEM, VMEM, VMEM, ANY, ANY, ANY],
        out_shape=(SHAPE(PLANE, F32), share_of(16), share_of(16), SHAPE((8, D), F32)),
        out_specs=(VMEM, ANY, ANY, VMEM),
        scratch_shapes=[
            pltpu.VMEM((3, GROUPS, SLAB, D), BF16),
            pltpu.VMEM((3,) + PLANE, BF16),
            pltpu.VMEM(PLANE, F32),
            pltpu.VMEM(PLANE, F32),
            pltpu.VMEM((4, 4, 4, 16, D), BF16),
            pltpu.VMEM((11, 8, D), BF16),
            pltpu.VMEM((ROWS, D), F32),
            pltpu.SemaphoreType.DMA((32,)),
        ],
        compiler_params=params(),
        cost_estimate=cost(10**10, 10**7),
    )(ints, grad, small, gathered, hidden, grads)


def take(value, index, dim):
    return lax.squeeze(lax.dynamic_slice_in_dim(value, index, 1, dim), (dim,))


def add(*values):
    total_value = values[0].astype(F32)
    for value in values[1:]:
        total_value = total_value + value.astype(F32)
    return total_value.astype(BF16)


def exchange(blocks):
    me = (lax.axis_index("x") % 2) * 2 + lax.axis_index("c")
    parts = []
    for flip in range(4):
        part = take(blocks, me ^ flip, 0)
        if flip:
            pairs = [(i, (i // 4) * 4 + ((i % 4) ^ flip)) for i in range(8)]
            part = lax.ppermute(part, ("x", "c"), pairs)
        parts.append(part)
    odd, high = (me & 1) == 1, (me & 2) == 2
    pairs = [jnp.where(odd, parts[i ^ 1], parts[i]) for i in range(4)]
    return [jnp.where(high, pairs[i ^ 2], pairs[i]) for i in range(4)]


def swap(value):
    return lax.ppermute(value, "c", [(0, 1), (1, 0)])


def scatter_chip_rows(shares):
    return lax.psum_scatter(shares, ("x", "c"), scatter_dimension=0, tiled=False)


STAGES = (("x", "y"), ("y", "x"), ("z", "z"))
STRIDES = {"y": 32, "z": 8, "x": 2}


def direct(value, axes):
    place = jnp.where(lax.axis_index("c") == 0, lax.axis_index(axes[0]), lax.axis_index(axes[1]))
    parts = [take(value, place, 0)]
    for hop in range(1, 4):
        pairs = []
        for dev in range(DEVICES):
            stride = STRIDES[axes[dev % 2]]
            at = dev // stride % 4
            pairs.append((dev, dev + ((at + hop) % 4 - at) * stride))
        parts.append(lax.ppermute(take(value, (place + hop) % 4, 0), AXES, pairs))
    return add(*parts)


def small_shares(*sums):
    sixes = jnp.concatenate([part[first:last] for part, first, last in sums[:-1]], axis=0)
    sixes = sixes.reshape(-1, DEVICES, 6).transpose(1, 0, 2).reshape(DEVICES, -1)
    values = jnp.concatenate([sixes, sums[-1].reshape(DEVICES, SLAB)], axis=1).astype(BF16)
    values = jnp.pad(values, ((0, 0), (0, 128 - values.shape[1]))).reshape(4, 4, 4, 2, 1, 128)
    even, odd = values[:, :, :, 0].transpose(2, 0, 1, 3, 4), values[:, :, :, 1].transpose(0, 2, 1, 3, 4)
    first = lax.axis_index("c") == 0
    both = add(jnp.where(first, even, odd), swap(jnp.where(first, odd, even)))
    return jnp.pad(both, ((0, 0), (0, 0), (0, 0), (0, 7), (0, D - 128)))


def gather(norm_gain, norm_bias, row_qkv, row_out, row_bias, col_qkv, col_out, col_bias,
           ffn_up, up_bias, ffn_down, down_bias, pos_tables):
    row = jnp.concatenate([row_qkv, row_out[None]], axis=0)
    col = jnp.concatenate([col_qkv, col_out[None]], axis=0)
    up = ffn_up.reshape(6, MEMBERS, D).transpose(1, 0, 2)
    slabs = jnp.stack(exchange(jnp.stack([row, col, up], axis=1)), axis=1)
    packed = jnp.concatenate(
        [slabs.reshape(3 * SLAB, D), ffn_down, pos_tables[0], pos_tables[1]], axis=0
    )
    gathered = lax.all_gather(packed, AXES, axis=0, tiled=False)
    sixes = jnp.concatenate([norm_gain, norm_bias, row_bias, col_bias, down_bias[None]], axis=0)
    line = jnp.pad(jnp.concatenate([sixes.reshape(-1), up_bias]), (0, 26))
    lines = lax.all_gather(line, AXES, axis=0, tiled=False).astype(F32)
    small = lines[:, :78].reshape(DEVICES, 13, 6).transpose(1, 0, 2).reshape(13, D)
    small = jnp.pad(small, ((0, 3), (0, 0)))
    return gathered.reshape(GROUPS, MEMBERS, PACK, D), small, lines[:, 78:102].reshape(4, D)


def on_device(tokens, cotangent, lengths, row_offset, col_offset, *weights):
    gathered, small, up_bias = gather(*weights)
    core = lax.axis_index("c").astype(jnp.int32)
    ints = jnp.concatenate([lengths, row_offset, col_offset, core[None]])
    act, g2, saved, hidden, ffn_shares, ffn_sums = forward_call(
        ints, tokens.reshape(TOKENS, D), cotangent.reshape(TOKENS, D), small, up_bias, gathered
    )
    barrier = lax.optimization_barrier
    ffn = scatter_chip_rows(ffn_shares)
    col_heads = heads_call(True, ints, g2, gathered, saved)
    g1, own, other, col_sums = column_call(ints, g2, small, gathered, saved, hidden, col_heads)
    row_heads = heads_call(False, ints, g1, gathered, saved)
    col, row_heads = barrier((add(own, swap(other)), row_heads))
    col = direct(col, STAGES[0])
    g0, table_own, table_other, row_sums = row_input_call(ints, g1, small, gathered, hidden, row_heads)
    own, other = row_weights_call(ints, g1, saved, row_heads)
    table_other, col = barrier((table_other, col))
    other, table_other = barrier((other, swap(table_other)))
    extra = small_shares((row_sums, 0, 5), (col_sums, 0, 5), (ffn_sums, 4, 7), ffn_sums[:4])
    other = swap(other)
    table = jnp.concatenate([add(table_own, table_other), extra], axis=3)
    table = direct(table, STAGES[0])
    other, ffn = barrier((other, ffn))
    ffn = lax.psum_scatter(ffn.reshape(4, 4, 2 * SLAB, D), "y", scatter_dimension=0, tiled=False)
    row = direct(add(own, other), STAGES[0])
    rows = direct(jnp.concatenate([row, table, col], axis=2), STAGES[1])
    rows = direct(jnp.concatenate([rows, ffn], axis=1), STAGES[2])
    return (act.reshape(tokens.shape), g0.reshape(tokens.shape)) + owned(rows)


def rows_of(*slabs):
    blocks = jnp.stack(slabs, axis=0).reshape(len(slabs), MEMBERS, 6, D)
    return jnp.stack(exchange(blocks.transpose(1, 0, 2, 3)), axis=0).astype(F32)


def owned(rows):
    row, table, col, up, down = (rows[i * SLAB : (i + 1) * SLAB] for i in range(5))
    mine = rows_of(row, col, up)
    line = table[16, :128].astype(F32)
    sixes = line[:78].reshape(13, 6)
    row_sums, col_sums, ffn_sums = sixes[0:5], sixes[5:10], sixes[10:13]
    gain = jnp.stack([row_sums[0], col_sums[0], ffn_sums[1]])
    shift_grad = jnp.stack([row_sums[1], col_sums[1], ffn_sums[2]])
    return (
        gain,
        shift_grad,
        mine[:3, 0],
        mine[3, 0],
        row_sums[2:5],
        mine[:3, 1],
        mine[3, 1],
        col_sums[2:5],
        mine[:, 2].transpose(1, 0, 2).reshape(6, FF),
        line[78:102],
        down.astype(F32),
        ffn_sums[0],
        table[:16].reshape(2, 8, D).astype(F32),
    )


def solution(mesh):
    mesh = Mesh(mesh.devices.reshape(4, 4, 4, 2), AXES)
    first, second = P(AXES), P(None, AXES)
    weights = (second, second, second, first, second, second, first, second) + (first,) * 4 + (second,)
    return jax.shard_map(
        on_device,
        mesh=mesh,
        in_specs=(first,) * 5 + weights,
        out_specs=(first, first) + weights,
        check_vma=False,
    )
```

profile of v0, /device:TPU:24, one launch (start us, length us, event | category | flops | bytes accessed | tf_op | source)
XLA Modules:
  0.0 320.4 jit_solution(6223004018664095535)
XLA Ops:
  9.1 1.6 collective-permute-start.1
  18.1 31.4 %all-gather.2 = bf16[128,1,128]{2,1,0:T(2,128)(2,1)S(1)} all-gather(bf16[1,1,128]{2,1,0:T(2,128)(2,1)S(1)} %fusion.30), channel_id=2, replica_groups=mesh['y'=4,'z'=4,'x'=4,'c'=2] {'y','z','x','c'}, dimensions={0}, use_global_device_ids=true | all-gather | bytes 33024 | tf_op jit(solution)/shard_map/all_gather | solution.py:808
  52.5 53.4 %all-gather.5.cloned.1.call-done = bf16[14336,768]{1,0:T(8,128)(2,1)} async-done(((bf16[112,768]{1,0:T(8,128)(2,1)}), bf16[14336,768]{1,0:T(8,128)(2,1)}) %all-gather.5.cloned.1.call-update) | async-done | bytes 22020112 | tf_op jit(solution)/shard_map/all_gather | solution.py:805
  105.9 41.7 %forward.1 = (bf16[512,768]{1,0:T(8,128)(2,1)}, f32[512,768]{1,0:T(8,128)}, bf16[10,512,768]{2,1,0:T(8,128)(2,1)}, f32[2,512,768]{2,1,0:T(8,128)}, bf16[8,16,48,768]{3,2,1,0:T(8,128)(2,1)}, /*index=5*/f32[8,768]{1,0:T(8,128)}) custom-call(s32[4]{0:T(128)} %pad_add_fusion.ints.refs_0_, bf16[512,768]{1,0:T(8,128)(2,1)} %bitcast.189, ...), custom_call_target="tpu_custom_call" | custom-call | flops 24000000000 | bytes 50000000 | tf_op jit(solution)/shard_map/forward/pallas_call | solution.py:613
  147.9 11.3 %column_heads.1.grads_in = bf16[3,512,768]{2,1,0:T(8,128)(2,1)} custom-call(s32[4]{0:T(128)} %pad_add_fusion.ints.refs_0_, f32[512,768]{1,0:T(8,128)} %get-tuple-element.40.refs_1_.grad_in, bf16[32,4,112,768]{3,2,1,0:T(8,128)(2,1)} %bitcast.168, bf16[10,512,768]{2,1,0:T(8,128)(2,1)} %get-tuple-element.41.refs_3_.saved), custom_call_target="tpu_custom_call" | custom-call | flops 10000000000 | bytes 10000000 | tf_op jit(solution)/shard_map/column_heads/pallas_call | solution.py:647
  159.2 13.8 %column_weights.1 = (f32[512,768]{1,0:T(8,128)}, bf16[4,4,4,24,768]{4,3,2,1,0:T(8,128)(2,1)}, bf16[4,4,4,24,768]{4,3,2,1,0:T(8,128)(2,1)}, f32[8,768]{1,0:T(8,128)}) custom-call(s32[4]{0:T(128)} %pad_add_fusion.ints.refs_0_, f32[512,768]{1,0:T(8,128)} %get-tuple-element.40.refs_1_.grad_in, f32[16,768]{1,0:T(8,128)} %pad.17.small, ...), custom_call_target="tpu_custom_call" | custom-call | flops 10000000000 | bytes 10000000 | tf_op jit(solution)/shard_map/column_weights/pallas_call | solution.py:671
  173.4 7.8 %row_heads.1.grads_in = bf16[3,512,768]{2,1,0:T(8,128)(2,1)} custom-call(s32[4]{0:T(128)} %pad_add_fusion.ints.refs_0_, f32[512,768]{1,0:T(8,128)} %get-tuple-element.43.refs_1_.grad_in, bf16[32,4,112,768]{3,2,1,0:T(8,128)(2,1)} %bitcast.170, bf16[10,512,768]{2,1,0:T(8,128)(2,1)} %get-tuple-element.41.refs_3_.saved), custom_call_target="tpu_custom_call" | custom-call | flops 10000000000 | bytes 10000000 | tf_op jit(solution)/shard_map/row_heads/pallas_call | solution.py:647
  181.2 3.2 add_convert_fusion.1
  186.9 1.5 collective-permute-start.4
  188.4 1.7 collective-permute-start.6
  190.1 1.8 collective-permute-start.5
  191.9 12.4 %row_input.1 = (f32[512,768]{1,0:T(8,128)}, bf16[4,4,4,16,768]{4,3,2,1,0:T(8,128)(2,1)}, bf16[4,4,4,16,768]{4,3,2,1,0:T(8,128)(2,1)}, f32[8,768]{1,0:T(8,128)}) custom-call(s32[4]{0:T(128)} %pad_add_fusion.ints.refs_0_, f32[512,768]{1,0:T(8,128)} %get-tuple-element.43.refs_1_.grad_in, f32[16,768]{1,0:T(8,128)} %pad.17.small, ...), custom_call_target="tpu_custom_call" | custom-call | flops 10000000000 | bytes 10000000 | tf_op jit(solution)/shard_map/row_input/pallas_call | solution.py:714
  204.9 11.3 %collective-permute-done.5 = bf16[4,4,24,768]{3,2,1,0:T(8,128)(2,1)} collective-permute-done((bf16[4,4,24,768]{3,2,1,0:T(8,128)(2,1)S(1)}, bf16[4,4,24,768]{3,2,1,0:T(8,128)(2,1)}, u32[]{:S(2)}, u32[]{:S(2)}) %collective-permute-start.5) | collective-permute-done | bytes 589856 | tf_op jit(solution)/shard_map/ppermute | solution.py:781
  216.2 1.5 fusion.10
  217.9 8.8 %row_weights.1 = (bf16[4,4,4,24,768]{4,3,2,1,0:T(8,128)(2,1)}, bf16[4,4,4,24,768]{4,3,2,1,0:T(8,128)(2,1)}) custom-call(s32[4]{0:T(128)} %pad_add_fusion.ints.refs_0_, f32[512,768]{1,0:T(8,128)} %get-tuple-element.43.refs_1_.grad_in, bf16[10,512,768]{2,1,0:T(8,128)(2,1)} %get-tuple-element.41.refs_3_.saved, bf16[3,512,768]{2,1,0:T(8,128)(2,1)} %row_heads.1.grads_in), custom_call_target="tpu_custom_call" | custom-call | flops 10000000000 | bytes 10000000 | tf_op jit(solution)/shard_map/row_weights/pallas_call | solution.py:694
  229.2 2.5 collective-permute-done.12
  231.8 2.4 add_convert_fusion.2
  234.4 1.5 copy-done.1
  238.2 2.3 collective-permute-start.15
  241.9 3.1 add_convert_fusion
  247.4 2.0 collective-permute-start.11
  249.4 5.4 %collective-permute-done.13 = bf16[4,4,24,768]{3,2,1,0:T(8,128)(2,1)S(1)} collective-permute-done((bf16[4,4,24,768]{3,2,1,0:T(8,128)(2,1)}, bf16[4,4,24,768]{3,2,1,0:T(8,128)(2,1)S(1)}, u32[]{:S(2)}, u32[]{:S(2)}) %collective-permute-start.13) | collective-permute-done | bytes 589856 | tf_op jit(solution)/shard_map/ppermute | solution.py:781
  254.8 1.7 fusion.4
  256.6 11.0 %collective-permute-done.9 = bf16[4,4,24,768]{3,2,1,0:T(8,128)(2,1)} collective-permute-done((bf16[4,4,24,768]{3,2,1,0:T(8,128)(2,1)}, bf16[4,4,24,768]{3,2,1,0:T(8,128)(2,1)}, u32[]{:S(2)}, u32[]{:S(2)}) %collective-permute-start.9) | collective-permute-done | bytes 589856 | tf_op jit(solution)/shard_map/ppermute | solution.py:781
  267.6 1.7 fusion.7
  271.0 1.5 collective-permute-start.18
  273.9 6.0 %collective-permute-done.16 = bf16[4,72,768]{2,1,0:T(8,128)(2,1)S(1)} collective-permute-done((bf16[4,72,768]{2,1,0:T(8,128)(2,1)}, bf16[4,72,768]{2,1,0:T(8,128)(2,1)S(1)}, u32[]{:S(2)}, u32[]{:S(2)}) %collective-permute-start.16) | collective-permute-done | bytes 442400 | tf_op jit(solution)/shard_map/ppermute | solution.py:781
  279.9 6.1 %collective-permute-done.18 = bf16[4,72,768]{2,1,0:T(8,128)(2,1)S(1)} collective-permute-done((bf16[4,72,768]{2,1,0:T(8,128)(2,1)}, bf16[4,72,768]{2,1,0:T(8,128)(2,1)S(1)}, u32[]{:S(2)}, u32[]{:S(2)}) %collective-permute-start.18) | collective-permute-done | bytes 442400 | tf_op jit(solution)/shard_map/ppermute | solution.py:781
  287.3 1.6 collective-permute-start.19
  288.9 2.9 collective-permute-start.20
  294.1 3.1 collective-permute-done.20
  301.0 6.2 %collective-permute-start.24 = (bf16[3,6,768]{2,1,0:T(8,128)(2,1)S(1)}, bf16[3,6,768]{2,1,0:T(8,128)(2,1)S(1)}, u32[]{:S(2)}, u32[]{:S(2)}) collective-permute-start(bf16[3,6,768]{2,1,0:T(8,128)(2,1)S(1)} %get-tuple-element.96), channel_id=1, source_target_pairs={{0,1},{1,0},{2,3},{3,2},{4,5},{5,4},{6,7},{7,6},{8,9},{9,8},{10,11... | collective-permute-start | bytes 82952 | tf_op jit(solution)/shard_map/ppermute | solution.py:753
  (135 shorter events, 39.7 us)
Async XLA Ops:
  7.2 10.6 %copy-start.10 = (bf16[6]{0:T(256)(128)(2,1)S(1)}, bf16[6]{0:T(256)(128)(2,1)}, u32[]{:S(2)}) copy-start(bf16[6]{0:T(256)(128)(2,1)} %param.34) | copy-start | bytes 40
  7.2 10.6 %copy-start.9 = (bf16[3,6]{1,0:T(4,128)(2,1)S(1)}, bf16[3,6]{1,0:T(4,128)(2,1)}, u32[]{:S(2)}) copy-start(bf16[3,6]{1,0:T(4,128)(2,1)} %param.30) | copy-start | bytes 112
  7.2 10.6 %copy-start.8 = (bf16[3,6]{1,0:T(4,128)(2,1)S(1)}, bf16[3,6]{1,0:T(4,128)(2,1)}, u32[]{:S(2)}) copy-start(bf16[3,6]{1,0:T(4,128)(2,1)} %param.27) | copy-start | bytes 112
  7.2 10.8 %copy-start.11 = (bf16[24]{0:T(256)(128)(2,1)S(1)}, bf16[24]{0:T(256)(128)(2,1)}, u32[]{:S(2)}) copy-start(bf16[24]{0:T(256)(128)(2,1)} %param.32) | copy-start | bytes 148
  7.2 98.6 %all-gather.5.cloned.1.call-start = ((), (), s32[]{:S(2)}) async-start(), calls=%async_computation.4 | async-start | bytes 22192128 | tf_op jit(solution)/shard_map/all_gather | solution.py:805
  9.0 2.7 collective-permute-start.2
  9.1 4.0 %collective-permute-start.1 = (bf16[3,6,768]{2,1,0:T(8,128)(2,1)S(1)}, bf16[3,6,768]{2,1,0:T(8,128)(2,1)S(1)}, u32[]{:S(2)}, u32[]{:S(2)}) collective-permute-start(bf16[3,6,768]{2,1,0:T(8,128)(2,1)S(1)} %get-tuple-element.100), channel_id=1, source_target_pairs={{0,2},{1,3},{2,0},{3,1},{4,6},{5,7},{6,4},{7,5},{8,10},{9,11},{10,... | collective-permute-start | bytes 82952 | tf_op jit(solution)/shard_map/ppermute | solution.py:753
  10.7 3.4 %collective-permute-start = (bf16[3,6,768]{2,1,0:T(8,128)(2,1)S(1)}, bf16[3,6,768]{2,1,0:T(8,128)(2,1)S(1)}, u32[]{:S(2)}, u32[]{:S(2)}) collective-permute-start(bf16[3,6,768]{2,1,0:T(8,128)(2,1)S(1)} %get-tuple-element.101), channel_id=1, source_target_pairs={{0,3},{1,2},{2,1},{3,0},{4,7},{5,6},{6,5},{7,4},{8,11},{9,10},{10,... | collective-permute-start | bytes 82952 | tf_op jit(solution)/shard_map/ppermute | solution.py:753
  15.8 224.7 %reduce-scatter.3.cloned.1.call-start = ((), (), s32[]{:S(2)}) async-start(), calls=%async_computation.2 | async-start | bytes 10616832 | tf_op jit(solution)/shard_map/reduce_scatter | solution.py:765
  147.6 138.6 %reduce-scatter.5.cloned.1.call-start = ((), (), s32[]{:S(2)}) async-start(), calls=%async_computation.3 | async-start | bytes 1474560 | tf_op jit(solution)/shard_map/reduce_scatter | solution.py:837
  173.0 8.1 %collective-permute-start.3 = (bf16[4,4,4,24,768]{4,3,2,1,0:T(8,128)(2,1)}, bf16[4,4,4,24,768]{4,3,2,1,0:T(8,128)(2,1)}, u32[]{:S(2)}, u32[]{:S(2)}) collective-permute-start(bf16[4,4,4,24,768]{4,3,2,1,0:T(8,128)(2,1)} %get-tuple-element.45), channel_id=1, source_target_pairs={{0,1},{1,0},{2,3},{3,2},{4,5},{5,4},{6,7},{7,6},{8,9},{9,8},{10,11... | collective-permute-start | bytes 7077896 | tf_op jit(solution)/shard_map/ppermute | solution.py:761
  186.9 17.7 %collective-permute-start.4 = (bf16[4,4,24,768]{3,2,1,0:T(8,128)(2,1)}, bf16[4,4,24,768]{3,2,1,0:T(8,128)(2,1)S(1)}, u32[]{:S(2)}, u32[]{:S(2)}) collective-permute-start(bf16[4,4,24,768]{3,2,1,0:T(8,128)(2,1)} %get-tuple-element.71), channel_id=1, source_target_pairs={{0,2},{1,33},{2,4},{3,35},{4,6},{5,37},{6,0},{7,39},{8,10},{9,41},... | collective-permute-start | bytes 1769480 | tf_op jit(solution)/shard_map/ppermute | solution.py:781
  188.4 16.5 %collective-permute-start.6 = (bf16[4,4,24,768]{3,2,1,0:T(8,128)(2,1)}, bf16[4,4,24,768]{3,2,1,0:T(8,128)(2,1)S(1)}, u32[]{:S(2)}, u32[]{:S(2)}) collective-permute-start(bf16[4,4,24,768]{3,2,1,0:T(8,128)(2,1)} %get-tuple-element.72), channel_id=1, source_target_pairs={{0,6},{1,97},{2,0},{3,99},{4,2},{5,101},{6,4},{7,103},{8,14},{9,10... | collective-permute-start | bytes 1769480 | tf_op jit(solution)/shard_map/ppermute | solution.py:781
  190.1 26.1 %collective-permute-start.5 = (bf16[4,4,24,768]{3,2,1,0:T(8,128)(2,1)S(1)}, bf16[4,4,24,768]{3,2,1,0:T(8,128)(2,1)}, u32[]{:S(2)}, u32[]{:S(2)}) collective-permute-start(bf16[4,4,24,768]{3,2,1,0:T(8,128)(2,1)S(1)} %get-tuple-element.73), channel_id=1, source_target_pairs={{0,4},{1,65},{2,6},{3,67},{4,0},{5,69},{6,2},{7,71},{8,12},{9,73},... | collective-permute-start | bytes 1769480 | tf_op jit(solution)/shard_map/ppermute | solution.py:781
  217.8 8.9 %collective-permute-start.7 = (bf16[4,4,4,16,768]{4,3,2,1,0:T(8,128)(2,1)}, bf16[4,4,4,16,768]{4,3,2,1,0:T(8,128)(2,1)}, u32[]{:S(2)}, u32[]{:S(2)}) collective-permute-start(bf16[4,4,4,16,768]{4,3,2,1,0:T(8,128)(2,1)} %get-tuple-element.52), channel_id=1, source_target_pairs={{0,1},{1,0},{2,3},{3,2},{4,5},{5,4},{6,7},{7,6},{8,9},{9,8},{10,11... | collective-permute-start | bytes 4718600 | tf_op jit(solution)/shard_map/ppermute | solution.py:761
  226.7 13.7 %collective-permute-start.8 = (bf16[4,4,4,24,768]{4,3,2,1,0:T(8,128)(2,1)}, bf16[4,4,4,24,768]{4,3,2,1,0:T(8,128)(2,1)S(1)}, u32[]{:S(2)}, u32[]{:S(2)}) collective-permute-start(bf16[4,4,4,24,768]{4,3,2,1,0:T(8,128)(2,1)} %get-tuple-element.53), channel_id=1, source_target_pairs={{0,1},{1,0},{2,3},{3,2},{4,5},{5,4},{6,7},{7,6},{8,9},{9,8},{10,11... | collective-permute-start | bytes 7077896 | tf_op jit(solution)/shard_map/ppermute | solution.py:761
  229.1 2.6 collective-permute-start.12
  237.2 17.6 %collective-permute-start.13 = (bf16[4,4,24,768]{3,2,1,0:T(8,128)(2,1)}, bf16[4,4,24,768]{3,2,1,0:T(8,128)(2,1)S(1)}, u32[]{:S(2)}, u32[]{:S(2)}) collective-permute-start(bf16[4,4,24,768]{3,2,1,0:T(8,128)(2,1)} %get-tuple-element.68), channel_id=1, source_target_pairs={{0,2},{1,33},{2,4},{3,35},{4,6},{5,37},{6,0},{7,39},{8,10},{9,41},... | collective-permute-start | bytes 1769480 | tf_op jit(solution)/shard_map/ppermute | solution.py:781
  238.2 16.7 %collective-permute-start.15 = (bf16[4,4,24,768]{3,2,1,0:T(8,128)(2,1)}, bf16[4,4,24,768]{3,2,1,0:T(8,128)(2,1)}, u32[]{:S(2)}, u32[]{:S(2)}) collective-permute-start(bf16[4,4,24,768]{3,2,1,0:T(8,128)(2,1)} %get-tuple-element.69), channel_id=1, source_target_pairs={{0,6},{1,97},{2,0},{3,99},{4,2},{5,101},{6,4},{7,103},{8,14},{9,10... | collective-permute-start | bytes 1769480 | tf_op jit(solution)/shard_map/ppermute | solution.py:781
  240.4 14.4 %collective-permute-start.14 = (bf16[4,4,24,768]{3,2,1,0:T(8,128)(2,1)}, bf16[4,4,24,768]{3,2,1,0:T(8,128)(2,1)}, u32[]{:S(2)}, u32[]{:S(2)}) collective-permute-start(bf16[4,4,24,768]{3,2,1,0:T(8,128)(2,1)} %get-tuple-element.70), channel_id=1, source_target_pairs={{0,4},{1,65},{2,6},{3,67},{4,0},{5,69},{6,2},{7,71},{8,12},{9,73},... | collective-permute-start | bytes 1769480 | tf_op jit(solution)/shard_map/ppermute | solution.py:781
  246.2 21.4 %collective-permute-start.9 = (bf16[4,4,24,768]{3,2,1,0:T(8,128)(2,1)}, bf16[4,4,24,768]{3,2,1,0:T(8,128)(2,1)}, u32[]{:S(2)}, u32[]{:S(2)}) collective-permute-start(bf16[4,4,24,768]{3,2,1,0:T(8,128)(2,1)} %get-tuple-element.65), channel_id=1, source_target_pairs={{0,2},{1,33},{2,4},{3,35},{4,6},{5,37},{6,0},{7,39},{8,10},{9,41},... | collective-permute-start | bytes 1769480 | tf_op jit(solution)/shard_map/ppermute | solution.py:781
  247.4 20.1 %collective-permute-start.11 = (bf16[4,4,24,768]{3,2,1,0:T(8,128)(2,1)}, bf16[4,4,24,768]{3,2,1,0:T(8,128)(2,1)}, u32[]{:S(2)}, u32[]{:S(2)}) collective-permute-start(bf16[4,4,24,768]{3,2,1,0:T(8,128)(2,1)} %get-tuple-element.66), channel_id=1, source_target_pairs={{0,6},{1,97},{2,0},{3,99},{4,2},{5,101},{6,4},{7,103},{8,14},{9,10... | collective-permute-start | bytes 1769480 | tf_op jit(solution)/shard_map/ppermute | solution.py:781
  254.8 12.8 %collective-permute-start.10 = (bf16[4,4,24,768]{3,2,1,0:T(8,128)(2,1)}, bf16[4,4,24,768]{3,2,1,0:T(8,128)(2,1)}, u32[]{:S(2)}, u32[]{:S(2)}) collective-permute-start(bf16[4,4,24,768]{3,2,1,0:T(8,128)(2,1)} %get-tuple-element.67), channel_id=1, source_target_pairs={{0,4},{1,65},{2,6},{3,67},{4,0},{5,69},{6,2},{7,71},{8,12},{9,73},... | collective-permute-start | bytes 1769480 | tf_op jit(solution)/shard_map/ppermute | solution.py:781
  270.5 9.5 %collective-permute-start.16 = (bf16[4,72,768]{2,1,0:T(8,128)(2,1)}, bf16[4,72,768]{2,1,0:T(8,128)(2,1)S(1)}, u32[]{:S(2)}, u32[]{:S(2)}) collective-permute-start(bf16[4,72,768]{2,1,0:T(8,128)(2,1)} %get-tuple-element.74), channel_id=1, source_target_pairs={{0,32},{1,3},{2,34},{3,5},{4,36},{5,7},{6,38},{7,1},{8,40},{9,11},... | collective-permute-start | bytes 1327112 | tf_op jit(solution)/shard_map/ppermute | solution.py:781
  271.0 15.1 %collective-permute-start.18 = (bf16[4,72,768]{2,1,0:T(8,128)(2,1)}, bf16[4,72,768]{2,1,0:T(8,128)(2,1)S(1)}, u32[]{:S(2)}, u32[]{:S(2)}) collective-permute-start(bf16[4,72,768]{2,1,0:T(8,128)(2,1)} %get-tuple-element.75), channel_id=1, source_target_pairs={{0,96},{1,7},{2,98},{3,1},{4,100},{5,3},{6,102},{7,5},{8,104},{9,1... | collective-permute-start | bytes 1327112 | tf_op jit(solution)/shard_map/ppermute | solution.py:781
  272.5 13.5 %collective-permute-start.17 = (bf16[4,72,768]{2,1,0:T(8,128)(2,1)S(1)}, bf16[4,72,768]{2,1,0:T(8,128)(2,1)S(1)}, u32[]{:S(2)}, u32[]{:S(2)}) collective-permute-start(bf16[4,72,768]{2,1,0:T(8,128)(2,1)S(1)} %get-tuple-element.76), channel_id=1, source_target_pairs={{0,64},{1,5},{2,66},{3,7},{4,68},{5,1},{6,70},{7,3},{8,72},{9,13},... | collective-permute-start | bytes 1327112 | tf_op jit(solution)/shard_map/ppermute | solution.py:781
  287.3 6.8 %collective-permute-start.19 = (bf16[120,768]{1,0:T(8,128)(2,1)S(1)}, bf16[120,768]{1,0:T(8,128)(2,1)S(1)}, u32[]{:S(2)}, u32[]{:S(2)}) collective-permute-start(bf16[120,768]{1,0:T(8,128)(2,1)S(1)} %get-tuple-element.77), channel_id=1, source_target_pairs={{0,8},{1,9},{2,10},{3,11},{4,12},{5,13},{6,14},{7,15},{8,16},{9,17... | collective-permute-start | bytes 552968 | tf_op jit(solution)/shard_map/ppermute | solution.py:781
  288.9 8.3 %collective-permute-start.20 = (bf16[120,768]{1,0:T(8,128)(2,1)S(1)}, bf16[120,768]{1,0:T(8,128)(2,1)S(1)}, u32[]{:S(2)}, u32[]{:S(2)}) collective-permute-start(bf16[120,768]{1,0:T(8,128)(2,1)S(1)} %get-tuple-element.78), channel_id=1, source_target_pairs={{0,16},{1,17},{2,18},{3,19},{4,20},{5,21},{6,22},{7,23},{8,24},{9,... | collective-permute-start | bytes 552968 | tf_op jit(solution)/shard_map/ppermute | solution.py:781
  291.8 5.5 %collective-permute-start.21 = (bf16[120,768]{1,0:T(8,128)(2,1)S(1)}, bf16[120,768]{1,0:T(8,128)(2,1)S(1)}, u32[]{:S(2)}, u32[]{:S(2)}) collective-permute-start(bf16[120,768]{1,0:T(8,128)(2,1)S(1)} %get-tuple-element.79), channel_id=1, source_target_pairs={{0,24},{1,25},{2,26},{3,27},{4,28},{5,29},{6,30},{7,31},{8,0},{9,1... | collective-permute-start | bytes 552968 | tf_op jit(solution)/shard_map/ppermute | solution.py:781
  301.0 10.2 %collective-permute-start.24 = (bf16[3,6,768]{2,1,0:T(8,128)(2,1)S(1)}, bf16[3,6,768]{2,1,0:T(8,128)(2,1)S(1)}, u32[]{:S(2)}, u32[]{:S(2)}) collective-permute-start(bf16[3,6,768]{2,1,0:T(8,128)(2,1)S(1)} %get-tuple-element.96), channel_id=1, source_target_pairs={{0,1},{1,0},{2,3},{3,2},{4,5},{5,4},{6,7},{7,6},{8,9},{9,8},{10,11... | collective-permute-start | bytes 82952 | tf_op jit(solution)/shard_map/ppermute | solution.py:753
  307.2 4.1 %collective-permute-start.23 = (bf16[3,6,768]{2,1,0:T(8,128)(2,1)S(1)}, bf16[3,6,768]{2,1,0:T(8,128)(2,1)S(1)}, u32[]{:S(2)}, u32[]{:S(2)}) collective-permute-start(bf16[3,6,768]{2,1,0:T(8,128)(2,1)S(1)} %get-tuple-element.97), channel_id=1, source_target_pairs={{0,2},{1,3},{2,0},{3,1},{4,6},{5,7},{6,4},{7,5},{8,10},{9,11},{10,... | collective-permute-start | bytes 82952 | tf_op jit(solution)/shard_map/ppermute | solution.py:753
  308.1 3.8 %collective-permute-start.22 = (bf16[3,6,768]{2,1,0:T(8,128)(2,1)S(1)}, bf16[3,6,768]{2,1,0:T(8,128)(2,1)S(1)}, u32[]{:S(2)}, u32[]{:S(2)}) collective-permute-start(bf16[3,6,768]{2,1,0:T(8,128)(2,1)S(1)} %get-tuple-element.98), channel_id=1, source_target_pairs={{0,3},{1,2},{2,1},{3,0},{4,7},{5,6},{6,5},{7,4},{8,11},{9,10},{10,... | collective-permute-start | bytes 82952 | tf_op jit(solution)/shard_map/ppermute | solution.py:753
  (8 other events, 55.2 us)
Sparse Core Ops, SparseCore 0:
  15.9 89.9 all-gather.4
  147.8 66.9 reduce-scatter.2
  240.6 28.8 reduce-scatter.4
where the time goes:
time: 324 us; the launch traced here: 320 us
  waiting for transfers between devices  104 us (32%)
  Pallas kernels  95.9 us (30%)
  starting transfers between devices  32 us (10%)
  blocking collectives  31.4 us (10%)
  other arithmetic  23.5 us (7%)
  local copies, waits for them, and re-layouts  17.7 us (5%)
  between operations  16.3 us (5%)
    all_gather x1, waiting for transfers between devices, gather(): gathered = lax.all_gather(packed, AXES, axis=0, tiled=False)  53.4 us
    ppermute x15, waiting for transfers between devices, direct(): parts.append(lax.ppermute(take(value, (place + hop) % 4, 0), AXES, pairs))  44.5 us
    pallas_call x1, Pallas kernels, forward_call(): pl.pallas_call(forward_kernel, name='forward', in_specs=[SMEM, VMEM, VMEM...  41.7 us
    all_gather x1, blocking collectives, gather(): lines = lax.all_gather(line, AXES, axis=0, tiled=False).astype(F32)  31.4 us
    ppermute x15, starting transfers between devices, direct(): parts.append(lax.ppermute(take(value, (place + hop) % 4, 0), AXES, pairs))  20.8 us
    pallas_call x2, Pallas kernels, heads_call(): pl.pallas_call(lambda *refs: heads_kernel(column, *refs), name='column_he...  19 us
    convert_element_type x9, other arithmetic, add(): return total_value.astype(BF16)  14.9 us
    pallas_call x1, Pallas kernels, column_call(): pl.pallas_call(column_kernel, name='column_weights', in_specs=[SMEM, VMEM...  13.8 us
  transfers between devices with their start and end apart: 28, of which 16 were waited for; matrix products, arithmetic and copies ran while one was open for 8% of the time, Pallas kernels for 17%

commit v1 on v0

--- a/solution.py
+++ b/solution.py
@@ -427,12 +427,14 @@
         every, parity = slice(None), member % 2
         for half in range(2):
             x = 2 * half + member // 2
-            place = (x,) if parity == 0 else (every, x)
-            self.sent.append(
-                self.copies.send(
-                    self.core, parity, grads.at[member, half], self.own.at[place], self.other.at[place]
+            if parity == 0:
+                places = [(grads.at[member, half], (every, every, x))]
+            else:
+                places = [(grads.at[member, half, y], (every, y, x)) for y in range(4)]
+            for source, place in places:
+                self.sent.append(
+                    self.copies.send(self.core, parity, source, self.own.at[place], self.other.at[place])
                 )
-            )
 
     def wait(self):
         for copy in self.sent:
@@ -538,10 +540,31 @@
     shares.wait()
 
 
+def small_lines(sums, sums_col, sums_ffn):
+    lines = jnp.concatenate([sums[0:5, :], sums_col[0:5, :], sums_ffn[4:7, :], sums[5:8, :]], axis=0)
+    shape = (DEVICES, D)
+    dev, lane = (lax.broadcasted_iota(jnp.int32, shape, axis) for axis in (0, 1))
+    packed = jnp.zeros((DEVICES, 128), F32)
+    for j in range(6):
+        pick = jnp.where(lane == 6 * dev + j, 1.0, 0.0).astype(BF16)
+        blank = [jnp.zeros((16, D), F32)] * 8
+        blank[j] = lines
+        packed = packed + dot_nt(pick, jnp.concatenate(blank, axis=0).astype(BF16))
+    up = jnp.concatenate(
+        [jnp.broadcast_to(sums_ffn[f : f + 1, :], (32, D)) for f in range(4)], axis=0
+    )
+    first = 24 * (dev & 31)
+    up = jnp.where((lane >= first) & (lane < first + 24), up, 0.0).astype(BF16)
+    shape = (128, D)
+    to, lane = (lax.broadcasted_iota(jnp.int32, shape, axis) for axis in (0, 1))
+    fold = jnp.where(to - 96 == lane % 24, 1.0, 0.0).astype(BF16)
+    return (packed + dot_nt(up, fold)).astype(BF16)
+
+
 def row_input_kernel(
-    ints, grad_in, small, gathered, hidden_saved, grads_in,
-    grad_out, own, other, sums,
-    weights, act, hidden, da, zeros, table, lines, sems,
+    ints, grad_in, small, sums_col, sums_ffn, gathered, hidden_saved, grads_in,
+    grad_out, own, other,
+    weights, act, hidden, da, zeros, table, lines, sums, owned_lines, sems,
 ):
     copies = Copies(sems)
     loads = {"inputs": []}
@@ -555,10 +578,23 @@
     fills = [copies.start(zeros, out) for out in (own, other)]
     gain = small[GAIN : GAIN + 1, :]
     col_lines = input_grads(loads, grad_in, gain, act, weights, hidden, da, grad_out, sums, lines)
-    send_tables(ints, copies, fills, lines[...], col_lines, table, own, other)
-
-
-def send_tables(ints, copies, fills, row_lines, col_lines, table, own, other):
+    packed = small_lines(sums, sums_col, sums_ffn).astype(F32).reshape(4, 4, 4, 2, 1, 128)
+    owned_lines[...] = jnp.broadcast_to(packed, owned_lines.shape).astype(BF16)
+    for copy in fills:
+        copy.wait()
+    sent = []
+    every = slice(None)
+    places = [(0, owned_lines.at[:, :, :, 0], (every, every))]
+    places += [(1, owned_lines.at[y, :, :, 1], (every, y)) for y in range(4)]
+    for parity, source, place in places:
+        place = place + (every, slice(16, 24), slice(0, 128))
+        sent.append(copies.send(ints[3], parity, source, own.at[place], other.at[place]))
+    send_tables(ints, copies, lines[...], col_lines, table, own, other)
+    for copy in sent:
+        copy.wait()
+
+
+def send_tables(ints, copies, row_lines, col_lines, table, own, other):
     core = ints[3]
 
     def placed(values, offset, count):
@@ -575,14 +611,12 @@
     ):
         table[first : first + count] = placed(values, offset, 8 * count).reshape(count, 8, D)
         spots += [(first + i, offset // 8 + i, start) for i in range(count)]
-    for copy in fills:
-        copy.wait()
     waits = []
     for slot, owner, start in spots:
         real, dev = owner < DEVICES, jnp.minimum(owner, DEVICES - 1)
         x, y, z = (dev // 2) % 4, dev // 32, (dev // 8) % 4
         odd = dev % 2 == 1
-        place = (jnp.where(odd, y, x), jnp.where(odd, x, y), z, slice(start, start + 8))
+        place = (jnp.where(odd, z, y), jnp.where(odd, y, z), x, slice(start, start + 8))
         sem = copies.sems.at[copies.used]
         copies.used += 1
         here = pltpu.make_async_copy(table.at[slot], own.at[place], sem)
@@ -706,52 +740,186 @@
             pltpu.SemaphoreType.DMA((32,)),
         ],
         compiler_params=params(),
-        cost_estimate=cost(10**10, 10**7),
+        cost_estimate=cost(10**6, 10**5),
     )(ints, grad, saved, grads)
 
 
-def row_input_call(ints, grad, small, gathered, hidden, grads):
+def row_input_call(ints, grad, small, sums_col, sums_ffn, gathered, hidden, grads):
     return pl.pallas_call(
         row_input_kernel,
         name="row_input",
-        in_specs=[SMEM, VMEM, VMEM, ANY, ANY, ANY],
-        out_shape=(SHAPE(PLANE, F32), share_of(16), share_of(16), SHAPE((8, D), F32)),
-        out_specs=(VMEM, ANY, ANY, VMEM),
+        in_specs=[SMEM, VMEM, VMEM, VMEM, VMEM, ANY, ANY, ANY],
+        out_shape=(SHAPE(PLANE, F32), share_of(SLAB), share_of(SLAB)),
+        out_specs=(VMEM, ANY, ANY),
         scratch_shapes=[
             pltpu.VMEM((3, GROUPS, SLAB, D), BF16),
             pltpu.VMEM((3,) + PLANE, BF16),
             pltpu.VMEM(PLANE, F32),
             pltpu.VMEM(PLANE, F32),
-            pltpu.VMEM((4, 4, 4, 16, D), BF16),
+            pltpu.VMEM((4, 4, 4, SLAB, D), BF16),
             pltpu.VMEM((11, 8, D), BF16),
             pltpu.VMEM((ROWS, D), F32),
-            pltpu.SemaphoreType.DMA((32,)),
+            pltpu.VMEM((8, D), F32),
+            pltpu.VMEM((4, 4, 4, 2, 8, 128), BF16),
+            pltpu.SemaphoreType.DMA((48,)),
         ],
         compiler_params=params(),
-        cost_estimate=cost(10**10, 10**7),
-    )(ints, grad, small, gathered, hidden, grads)
+        cost_estimate=cost(2 * 10**10, 10**7),
+    )(ints, grad, small, sums_col, sums_ffn, gathered, hidden, grads)
+
+
+def split_kernel(place, own, other, *pieces):
+    for hop in range(4):
+        to = (place[0] + hop) & 3
+
+        def body(j):
+            pieces[hop][j] = (own[to, j].astype(F32) + other[to, j].astype(F32)).astype(BF16)
+
+        loop(4, body)
+
+
+def split(own, other, place):
+    return pl.pallas_call(
+        split_kernel,
+        name="split_shares",
+        in_specs=[SMEM, VMEM, VMEM],
+        out_shape=(SHAPE((4, 4, SLAB, D), BF16),) * 4,
+        out_specs=(VMEM,) * 4,
+        compiler_params=params(),
+        cost_estimate=cost(10**6, 10**6),
+    )(place, own, other)
+
+
+def sum_of(pieces, *index):
+    value = pieces[0][index].astype(F32)
+    for piece in pieces[1:]:
+        value = value + piece[index].astype(F32)
+    return value
+
+
+def second_kernel(place, *refs):
+    groups, pieces = [refs[4 * g : 4 * g + 4] for g in range(3)], refs[12:]
+    for hop in range(4):
+        to = (place[0] + hop) & 3
+
+        def body(j):
+            for g, group in enumerate(groups):
+                rows = slice(g * SLAB, (g + 1) * SLAB)
+                pieces[hop][j, rows, :] = sum_of(group, to, j).astype(BF16)
+
+        loop(4, body)
+
+
+def second_split(row, table, col, place):
+    return pl.pallas_call(
+        second_kernel,
+        name="second_split",
+        in_specs=[SMEM] + [VMEM] * 12,
+        out_shape=(SHAPE((4, 3 * SLAB, D), BF16),) * 4,
+        out_specs=(VMEM,) * 4,
+        compiler_params=params(),
+        cost_estimate=cost(10**6, 10**6),
+    )(place, *row, *table, *col)
+
+
+def third_kernel(place, *refs):
+    for hop in range(4):
+        refs[4 + hop][...] = sum_of(refs[:4], (place[0] + hop) & 3).astype(BF16)
+
+
+def third_split(rows, place):
+    return pl.pallas_call(
+        third_kernel,
+        name="third_split",
+        in_specs=[SMEM] + [VMEM] * 4,
+        out_shape=(SHAPE((3 * SLAB, D), BF16),) * 4,
+        out_specs=(VMEM,) * 4,
+        compiler_params=params(),
+        cost_estimate=cost(10**6, 10**6),
+    )(place, *rows)
+
+
+def last_kernel(me, *refs):
+    parts, ffn, (down, tables, line), pieces, held = refs[:4], refs[4:8], refs[8:11], refs[11:15], refs[15]
+    down[...] = sum_of(ffn, slice(SLAB, 2 * SLAB))
+    for i in range(2):
+        rows = slice(SLAB + 8 * i, SLAB + 8 * i + 8)
+        tables[i] = sum_of(parts, rows)
+    line[...] = sum_of(parts, slice(SLAB + 16, SLAB + 24))
+    for kind, (source, start) in enumerate(((parts, 0), (parts, 2 * SLAB), (ffn, 0))):
+        value = sum_of(source, slice(start, start + SLAB))
+        for member in range(MEMBERS):
+            held[member, kind] = value[6 * member : 6 * member + 6, :]
+    for flip in range(4):
+        pieces[flip][...] = held[me[0] ^ flip].astype(BF16)
+
+
+def last_split(me, rows, ffn):
+    return pl.pallas_call(
+        last_kernel,
+        name="last_split",
+        in_specs=[SMEM] + [VMEM] * 8,
+        out_shape=(
+            SHAPE((SLAB, D), F32),
+            SHAPE((2, 8, D), F32),
+            SHAPE((8, D), F32),
+        )
+        + (SHAPE((3, 6, D), BF16),) * 4,
+        out_specs=(VMEM,) * 7,
+        scratch_shapes=[pltpu.VMEM((MEMBERS, 3, 6, D), F32)],
+        compiler_params=params(),
+        cost_estimate=cost(10**6, 10**6),
+    )(me, *rows, *ffn)
+
+
+def outputs_kernel(me, one, two, three, four, row_qkv, row_out, col_qkv, col_out, up, held):
+    for flip, piece in enumerate((one, two, three, four)):
+        held[me[0] ^ flip] = piece[...].astype(F32)
+    for i in range(3):
+        row_qkv[i], col_qkv[i] = held[i, 0], held[i, 1]
+    row_out[...], col_out[...] = held[3, 0], held[3, 1]
+    for i in range(MEMBERS):
+        up[:, i * D : (i + 1) * D] = held[i, 2]
+
+
+def outputs(me, pieces):
+    return pl.pallas_call(
+        outputs_kernel,
+        name="outputs",
+        in_specs=[SMEM] + [VMEM] * 4,
+        out_shape=(
+            SHAPE((3, 6, D), F32),
+            SHAPE((6, D), F32),
+            SHAPE((3, 6, D), F32),
+            SHAPE((6, D), F32),
+            SHAPE((6, FF), F32),
+        ),
+        out_specs=(VMEM,) * 5,
+        scratch_shapes=[pltpu.VMEM((MEMBERS, 3, 6, D), F32)],
+        compiler_params=params(),
+        cost_estimate=cost(10**6, 10**6),
+    )(me, *pieces)
 
 
 def take(value, index, dim):
     return lax.squeeze(lax.dynamic_slice_in_dim(value, index, 1, dim), (dim,))
 
 
-def add(*values):
-    total_value = values[0].astype(F32)
-    for value in values[1:]:
-        total_value = total_value + value.astype(F32)
-    return total_value.astype(BF16)
+def member():
+    return (lax.axis_index("x") % 2) * 2 + lax.axis_index("c")
+
+
+def trade(pieces):
+    came = [pieces[0]]
+    for flip in range(1, 4):
+        pairs = [(i, (i // 4) * 4 + ((i % 4) ^ flip)) for i in range(8)]
+        came.append(lax.ppermute(pieces[flip], ("x", "c"), pairs))
+    return came
 
 
 def exchange(blocks):
-    me = (lax.axis_index("x") % 2) * 2 + lax.axis_index("c")
-    parts = []
-    for flip in range(4):
-        part = take(blocks, me ^ flip, 0)
-        if flip:
-            pairs = [(i, (i // 4) * 4 + ((i % 4) ^ flip)) for i in range(8)]
-            part = lax.ppermute(part, ("x", "c"), pairs)
-        parts.append(part)
+    me = member()
+    parts = trade([take(blocks, me ^ flip, 0) for flip in range(4)])
     odd, high = (me & 1) == 1, (me & 2) == 2
     pairs = [jnp.where(odd, parts[i ^ 1], parts[i]) for i in range(4)]
     return [jnp.where(high, pairs[i ^ 2], pairs[i]) for i in range(4)]
@@ -765,32 +933,25 @@
     return lax.psum_scatter(shares, ("x", "c"), scatter_dimension=0, tiled=False)
 
 
-STAGES = (("x", "y"), ("y", "x"), ("z", "z"))
+STAGES = (("y", "z"), ("z", "y"), ("x", "x"))
 STRIDES = {"y": 32, "z": 8, "x": 2}
 
 
-def direct(value, axes):
-    place = jnp.where(lax.axis_index("c") == 0, lax.axis_index(axes[0]), lax.axis_index(axes[1]))
-    parts = [take(value, place, 0)]
+def place_on(axes):
+    here = jnp.where(lax.axis_index("c") == 0, lax.axis_index(axes[0]), lax.axis_index(axes[1]))
+    return here.astype(jnp.int32)[None]
+
+
+def deliver(pieces, axes):
+    came = [pieces[0]]
     for hop in range(1, 4):
         pairs = []
         for dev in range(DEVICES):
             stride = STRIDES[axes[dev % 2]]
             at = dev // stride % 4
             pairs.append((dev, dev + ((at + hop) % 4 - at) * stride))
-        parts.append(lax.ppermute(take(value, (place + hop) % 4, 0), AXES, pairs))
-    return add(*parts)
-
-
-def small_shares(*sums):
-    sixes = jnp.concatenate([part[first:last] for part, first, last in sums[:-1]], axis=0)
-    sixes = sixes.reshape(-1, DEVICES, 6).transpose(1, 0, 2).reshape(DEVICES, -1)
-    values = jnp.concatenate([sixes, sums[-1].reshape(DEVICES, SLAB)], axis=1).astype(BF16)
-    values = jnp.pad(values, ((0, 0), (0, 128 - values.shape[1]))).reshape(4, 4, 4, 2, 1, 128)
-    even, odd = values[:, :, :, 0].transpose(2, 0, 1, 3, 4), values[:, :, :, 1].transpose(0, 2, 1, 3, 4)
-    first = lax.axis_index("c") == 0
-    both = add(jnp.where(first, even, odd), swap(jnp.where(first, odd, even)))
-    return jnp.pad(both, ((0, 0), (0, 0), (0, 0), (0, 7), (0, D - 128)))
+        came.append(lax.ppermute(pieces[hop], AXES, pairs))
+    return came
 
 
 def gather(norm_gain, norm_bias, row_qkv, row_out, row_bias, col_qkv, col_out, col_bias,
@@ -823,51 +984,48 @@
     col_heads = heads_call(True, ints, g2, gathered, saved)
     g1, own, other, col_sums = column_call(ints, g2, small, gathered, saved, hidden, col_heads)
     row_heads = heads_call(False, ints, g1, gathered, saved)
-    col, row_heads = barrier((add(own, swap(other)), row_heads))
-    col = direct(col, STAGES[0])
-    g0, table_own, table_other, row_sums = row_input_call(ints, g1, small, gathered, hidden, row_heads)
+    places = [place_on(axes) for axes in STAGES]
+    other, row_heads = barrier((swap(other), row_heads))
+    pieces, row_heads = barrier((split(own, other, places[0]), row_heads))
+    col = deliver(pieces, STAGES[0])
+    g0, table_own, table_other = row_input_call(
+        ints, g1, small, col_sums, ffn_sums, gathered, hidden, row_heads
+    )
     own, other = row_weights_call(ints, g1, saved, row_heads)
     table_other, col = barrier((table_other, col))
-    other, table_other = barrier((other, swap(table_other)))
-    extra = small_shares((row_sums, 0, 5), (col_sums, 0, 5), (ffn_sums, 4, 7), ffn_sums[:4])
-    other = swap(other)
-    table = jnp.concatenate([add(table_own, table_other), extra], axis=3)
-    table = direct(table, STAGES[0])
-    other, ffn = barrier((other, ffn))
+    other, table_other, ffn = barrier((other, swap(table_other), ffn))
     ffn = lax.psum_scatter(ffn.reshape(4, 4, 2 * SLAB, D), "y", scatter_dimension=0, tiled=False)
-    row = direct(add(own, other), STAGES[0])
-    rows = direct(jnp.concatenate([row, table, col], axis=2), STAGES[1])
-    rows = direct(jnp.concatenate([rows, ffn], axis=1), STAGES[2])
-    return (act.reshape(tokens.shape), g0.reshape(tokens.shape)) + owned(rows)
-
-
-def rows_of(*slabs):
-    blocks = jnp.stack(slabs, axis=0).reshape(len(slabs), MEMBERS, 6, D)
-    return jnp.stack(exchange(blocks.transpose(1, 0, 2, 3)), axis=0).astype(F32)
-
-
-def owned(rows):
-    row, table, col, up, down = (rows[i * SLAB : (i + 1) * SLAB] for i in range(5))
-    mine = rows_of(row, col, up)
-    line = table[16, :128].astype(F32)
-    sixes = line[:78].reshape(13, 6)
+    table = deliver(split(table_own, table_other, places[0]), STAGES[0])
+    row = deliver(split(own, swap(other), places[0]), STAGES[0])
+    rows = deliver(second_split(row, table, col, places[1]), STAGES[1])
+    z = lax.axis_index("z")
+    ffn = deliver([take(ffn, (z + hop) % 4, 0) for hop in range(4)], ("z", "z"))
+    rows = deliver(third_split(rows, places[2]), STAGES[2])
+    return (act.reshape(tokens.shape), g0.reshape(tokens.shape)) + owned(rows, ffn)
+
+
+def owned(rows, ffn):
+    me = member().astype(jnp.int32)[None]
+    down, tables, line, *pieces = last_split(me, rows, ffn)
+    row_qkv, row_out, col_qkv, col_out, up = outputs(me, trade(pieces))
+    sixes = line[0, :96].reshape(6, 16).T
     row_sums, col_sums, ffn_sums = sixes[0:5], sixes[5:10], sixes[10:13]
     gain = jnp.stack([row_sums[0], col_sums[0], ffn_sums[1]])
     shift_grad = jnp.stack([row_sums[1], col_sums[1], ffn_sums[2]])
     return (
         gain,
         shift_grad,
-        mine[:3, 0],
-        mine[3, 0],
+        row_qkv,
+        row_out,
         row_sums[2:5],
-        mine[:3, 1],
-        mine[3, 1],
+        col_qkv,
+        col_out,
         col_sums[2:5],
-        mine[:, 2].transpose(1, 0, 2).reshape(6, FF),
-        line[78:102],
-        down.astype(F32),
+        up,
+        line[0, 96:120],
+        down,
         ffn_sums[0],
-        table[:16].reshape(2, 8, D).astype(F32),
+        tables,
     )
 
 

time: 324 us -> 322 us (level)
  Pallas kernels: 95.9 us -> 122 us
  other arithmetic: 23.5 us -> 4.73 us
  waiting for transfers between devices: 104 us -> 97.4 us
    pallas_call x0 -> x7, Pallas kernels: none -> 24.8 us  [the longest x3 13.7 us: split(): pl.pallas_call(split_kernel, name='split_shares', in_specs=[SMEM, VMEM, V...]
    convert_element_type x13 -> x0, other arithmetic: 16.2 us -> none  [the longest x9 14.9 us: add(): return total_value.astype(BF16)]
    ppermute x21 -> x24, starting transfers between devices: 30.4 us -> 29.1 us  [the longest x18 25.3 us: deliver(): came.append(lax.ppermute(pieces[hop], AXES, pairs))]
    ppermute x21 -> x24, waiting for transfers between devices: 47.7 us -> 46.5 us  [the longest x18 44.1 us: deliver(): came.append(lax.ppermute(pieces[hop], AXES, pairs))]
  transfers between devices with their start and end apart: 28 -> 30, of which waited for: 16 -> 14; matrix products, arithmetic and copies ran while one was open for 8% -> 4% of each run, Pallas kernels for 17% -> 24%
where the time goes in v1:
time: 322 us; the launch traced here: 316 us
  Pallas kernels  122 us (38%)
  waiting for transfers between devices  97.4 us (30%)
  blocking collectives  31.4 us (10%)
  starting transfers between devices  30.2 us (9%)
  between operations  16 us (5%)
  local copies, waits for them, and re-layouts  14.7 us (5%)
  other arithmetic  4.73 us (1%)
    all_gather x1, waiting for transfers between devices, gather(): gathered = lax.all_gather(packed, AXES, axis=0, tiled=False)  50.8 us
    ppermute x18, waiting for transfers between devices, deliver(): came.append(lax.ppermute(pieces[hop], AXES, pairs))  44.1 us
    pallas_call x1, Pallas kernels, forward_call(): pl.pallas_call(forward_kernel, name='forward', in_specs=[SMEM, VMEM, VMEM...  41.7 us
    all_gather x1, blocking collectives, gather(): lines = lax.all_gather(line, AXES, axis=0, tiled=False).astype(F32)  31.4 us
    ppermute x18, starting transfers between devices, deliver(): came.append(lax.ppermute(pieces[hop], AXES, pairs))  25.3 us
    pallas_call x2, Pallas kernels, heads_call(): pl.pallas_call(lambda *refs: heads_kernel(column, *refs), name='column_he...  18.9 us
    pallas_call x1, Pallas kernels, column_call(): pl.pallas_call(column_kernel, name='column_weights', in_specs=[SMEM, VMEM...  13.9 us
    pallas_call x3, Pallas kernels, split(): pl.pallas_call(split_kernel, name='split_shares', in_specs=[SMEM, VMEM, V...  13.7 us
  transfers between devices with their start and end apart: 30, of which 14 were waited for; matrix products, arithmetic and copies ran while one was open for 4% of the time, Pallas kernels for 24%

profile of v1, /device:TPU:24, one launch (start us, length us, event | category | flops | bytes accessed | tf_op | source)
XLA Modules:
  0.0 316.3 jit_solution(3866377906008581365)
XLA Ops:
  17.7 2.2 concatenate.19
  20.7 31.4 %all-gather.2 = bf16[128,1,128]{2,1,0:T(2,128)(2,1)S(1)} all-gather(bf16[1,1,128]{2,1,0:T(2,128)(2,1)S(1)} %fusion.1), channel_id=2, replica_groups=mesh['y'=4,'z'=4,'x'=4,'c'=2] {'y','z','x','c'}, dimensions={0}, use_global_device_ids=true | all-gather | bytes 33024 | tf_op jit(solution)/shard_map/all_gather | solution.py:969
  55.0 50.8 %all-gather.5.cloned.1.call-done = bf16[14336,768]{1,0:T(8,128)(2,1)} async-done(((bf16[112,768]{1,0:T(8,128)(2,1)}), bf16[14336,768]{1,0:T(8,128)(2,1)}) %all-gather.5.cloned.1.call-update) | async-done | bytes 22020112 | tf_op jit(solution)/shard_map/all_gather | solution.py:966
  105.8 41.7 %forward.1 = (bf16[512,768]{1,0:T(8,128)(2,1)}, f32[512,768]{1,0:T(8,128)}, bf16[10,512,768]{2,1,0:T(8,128)(2,1)}, f32[2,512,768]{2,1,0:T(8,128)}, bf16[8,16,48,768]{3,2,1,0:T(8,128)(2,1)}, /*index=5*/f32[8,768]{1,0:T(8,128)}) custom-call(s32[4]{0:T(128)} %pad_add_fusion.ints.refs_0_, bf16[512,768]{1,0:T(8,128)(2,1)} %bitcast.92, bf16[512,768]{1,0:T(8,128)(2,1)} %bitcast.93, ...), custom_call_target="tpu_custom_call" | custom-call | flops 24000000000 | bytes 50000000 | tf_op jit(solution)/shard_map/forward/pallas_call | solution.py:647
  147.8 11.2 %column_heads.1.grads_in = bf16[3,512,768]{2,1,0:T(8,128)(2,1)} custom-call(s32[4]{0:T(128)} %pad_add_fusion.ints.refs_0_, f32[512,768]{1,0:T(8,128)} %get-tuple-element.78.refs_1_.grad_in, bf16[32,4,112,768]{3,2,1,0:T(8,128)(2,1)} %bitcast.78, bf16[10,512,768]{2,1,0:T(8,128)(2,1)} %get-tuple-element.79.refs_3_.saved), custom_call_target="tpu_custom_call" | custom-call | flops 10000000000 | bytes 10000000 | tf_op jit(solution)/shard_map/column_heads/pallas_call | solution.py:681
  159.0 13.9 %column_weights.1 = (f32[512,768]{1,0:T(8,128)}, bf16[4,4,4,24,768]{4,3,2,1,0:T(8,128)(2,1)}, bf16[4,4,4,24,768]{4,3,2,1,0:T(8,128)(2,1)}, f32[8,768]{1,0:T(8,128)}) custom-call(s32[4]{0:T(128)} %pad_add_fusion.ints.refs_0_, f32[512,768]{1,0:T(8,128)} %get-tuple-element.78.refs_1_.grad_in, f32[16,768]{1,0:T(8,128)} %pad.9.small, ...), custom_call_target="tpu_custom_call" | custom-call | flops 10000000000 | bytes 10000000 | tf_op jit(solution)/shard_map/column_weights/pallas_call | solution.py:705
  173.3 7.7 %row_heads.1.grads_in = bf16[3,512,768]{2,1,0:T(8,128)(2,1)} custom-call(s32[4]{0:T(128)} %pad_add_fusion.ints.refs_0_, f32[512,768]{1,0:T(8,128)} %get-tuple-element.81.refs_1_.grad_in, bf16[32,4,112,768]{3,2,1,0:T(8,128)(2,1)} %bitcast.80, bf16[10,512,768]{2,1,0:T(8,128)(2,1)} %get-tuple-element.79.refs_3_.saved), custom_call_target="tpu_custom_call" | custom-call | flops 10000000000 | bytes 10000000 | tf_op jit(solution)/shard_map/row_heads/pallas_call | solution.py:681
  181.0 4.5 %split_shares.3 = (bf16[4,4,24,768]{3,2,1,0:T(8,128)(2,1)}, bf16[4,4,24,768]{3,2,1,0:T(8,128)(2,1)}, bf16[4,4,24,768]{3,2,1,0:T(8,128)(2,1)}, bf16[4,4,24,768]{3,2,1,0:T(8,128)(2,1)}) custom-call(s32[1]{0:T(128)} %bitcast.29.place, bf16[4,4,4,24,768]{4,3,2,1,0:T(8,128)(2,1)} %get-tuple-element.84.own, bf16[4,4,4,24,768]{4,3,2,1,0:T(8,128)(2,1)} %collective-permute-done.3.other), custom_call_target="tpu_custom_call" | custom-call | flops 1000000 | bytes 1000000 | tf_op jit(solution)/shard_map/split_shares/pallas_call | solution.py:782
  186.1 2.4 collective-permute-start.5
  188.5 13.5 %row_input.1 = (f32[512,768]{1,0:T(8,128)}, bf16[4,4,4,24,768]{4,3,2,1,0:T(8,128)(2,1)}, bf16[4,4,4,24,768]{4,3,2,1,0:T(8,128)(2,1)}) custom-call(s32[4]{0:T(128)} %pad_add_fusion.ints.refs_0_, f32[512,768]{1,0:T(8,128)} %get-tuple-element.81.refs_1_.grad_in, f32[16,768]{1,0:T(8,128)} %pad.9.small, f32[8,768]{1,0:T(8,128)} %get-tuple-element.82.sums_col, ...), custom_call_target="tpu_custom_call" | custom-call | flops 20000000000 | bytes 10000000 | tf_op jit(solution)/shard_map/row_input/pallas_call | solution.py:748
  202.0 2.0 collective-permute-done.6.refs_11_
  204.0 9.0 %row_weights.1 = (bf16[4,4,4,24,768]{4,3,2,1,0:T(8,128)(2,1)}, bf16[4,4,4,24,768]{4,3,2,1,0:T(8,128)(2,1)}) custom-call(s32[4]{0:T(128)} %pad_add_fusion.ints.refs_0_, f32[512,768]{1,0:T(8,128)} %get-tuple-element.81.refs_1_.grad_in, bf16[10,512,768]{2,1,0:T(8,128)(2,1)} %get-tuple-element.79.refs_3_.saved, bf16[3,512,768]{2,1,0:T(8,128)(2,1)} %row_heads.1.grads_in), custom_call_target="tpu_custom_call" | custom-call | flops 1000000 | bytes 100000 | tf_op jit(solution)/shard_map/row_weights/pallas_call | solution.py:728
  213.6 4.4 %split_shares.5 = (bf16[4,4,24,768]{3,2,1,0:T(8,128)(2,1)}, bf16[4,4,24,768]{3,2,1,0:T(8,128)(2,1)}, bf16[4,4,24,768]{3,2,1,0:T(8,128)(2,1)}, bf16[4,4,24,768]{3,2,1,0:T(8,128)(2,1)}) custom-call(s32[1]{0:T(128)} %bitcast.29.place, bf16[4,4,4,24,768]{4,3,2,1,0:T(8,128)(2,1)} %get-tuple-element.108.own, bf16[4,4,4,24,768]{4,3,2,1,0:T(8,128)(2,1)} %collective-permute-done.7.other), custom_call_target="tpu_custom_call" | custom-call | flops 1000000 | bytes 1000000 | tf_op jit(solution)/shard_map/split_shares/pallas_call | solution.py:782
  221.5 4.7 %split_shares.4 = (bf16[4,4,24,768]{3,2,1,0:T(8,128)(2,1)}, bf16[4,4,24,768]{3,2,1,0:T(8,128)(2,1)}, bf16[4,4,24,768]{3,2,1,0:T(8,128)(2,1)}, bf16[4,4,24,768]{3,2,1,0:T(8,128)(2,1)}) custom-call(s32[1]{0:T(128)} %bitcast.29.place, bf16[4,4,4,24,768]{4,3,2,1,0:T(8,128)(2,1)} %get-tuple-element.94.own, bf16[4,4,4,24,768]{4,3,2,1,0:T(8,128)(2,1)} %collective-permute-done.8.other), custom_call_target="tpu_custom_call" | custom-call | flops 1000000 | bytes 1000000 | tf_op jit(solution)/shard_map/split_shares/pallas_call | solution.py:782
  226.2 2.6 collective-permute-start.9
  229.6 6.0 %collective-permute-done.12.refs_5_ = bf16[4,4,24,768]{3,2,1,0:T(8,128)(2,1)S(1)} collective-permute-done((bf16[4,4,24,768]{3,2,1,0:T(8,128)(2,1)}, bf16[4,4,24,768]{3,2,1,0:T(8,128)(2,1)S(1)}, u32[]{:S(2)}, u32[]{:S(2)}) %collective-permute-start.12) | collective-permute-done | bytes 589856 | tf_op jit(solution)/shard_map/ppermute | solution.py:953
  235.7 2.7 collective-permute-done.13.refs_6_
  238.3 7.1 %collective-permute-done.14.refs_7_ = bf16[4,4,24,768]{3,2,1,0:T(8,128)(2,1)S(1)} collective-permute-done((bf16[4,4,24,768]{3,2,1,0:T(8,128)(2,1)}, bf16[4,4,24,768]{3,2,1,0:T(8,128)(2,1)S(1)}, u32[]{:S(2)}, u32[]{:S(2)}) %collective-permute-start.14) | collective-permute-done | bytes 589856 | tf_op jit(solution)/shard_map/ppermute | solution.py:953
  245.4 4.9 %collective-permute-done.9.refs_1_ = bf16[4,4,24,768]{3,2,1,0:T(8,128)(2,1)} collective-permute-done((bf16[4,4,24,768]{3,2,1,0:T(8,128)(2,1)}, bf16[4,4,24,768]{3,2,1,0:T(8,128)(2,1)}, u32[]{:S(2)}, u32[]{:S(2)}) %collective-permute-start.9) | collective-permute-done | bytes 589856 | tf_op jit(solution)/shard_map/ppermute | solution.py:953
  250.4 2.8 collective-permute-done.10.refs_2_
  253.1 5.1 %collective-permute-done.11.refs_3_ = bf16[4,4,24,768]{3,2,1,0:T(8,128)(2,1)} collective-permute-done((bf16[4,4,24,768]{3,2,1,0:T(8,128)(2,1)}, bf16[4,4,24,768]{3,2,1,0:T(8,128)(2,1)}, u32[]{:S(2)}, u32[]{:S(2)}) %collective-permute-start.11) | collective-permute-done | bytes 589856 | tf_op jit(solution)/shard_map/ppermute | solution.py:953
  258.2 5.2 %second_split.1 = (bf16[4,72,768]{2,1,0:T(8,128)(2,1)}, bf16[4,72,768]{2,1,0:T(8,128)(2,1)}, bf16[4,72,768]{2,1,0:T(8,128)(2,1)}, bf16[4,72,768]{2,1,0:T(8,128)(2,1)}) custom-call(s32[1]{0:T(128)} %bitcast.33.place, bf16[4,4,24,768]{3,2,1,0:T(8,128)(2,1)} %get-tuple-element.104.refs_0_, bf16[4,4,24,768]{3,2,1,0:T(8,128)(2,1)} %collective-permute-done.9.refs_1_, ...), custom_call_target="tpu_custom_call" | custom-call | flops 1000000 | bytes 1000000 | tf_op jit(solution)/shard_map/second_split/pallas_call | solution.py:814
  263.4 1.8 collective-permute-start.15
  265.2 2.9 collective-permute-start.16
  271.1 2.1 collective-permute-done.15.refs_1_
  273.2 6.1 %collective-permute-done.16.refs_2_ = bf16[4,72,768]{2,1,0:T(8,128)(2,1)S(1)} collective-permute-done((bf16[4,72,768]{2,1,0:T(8,128)(2,1)}, bf16[4,72,768]{2,1,0:T(8,128)(2,1)S(1)}, u32[]{:S(2)}, u32[]{:S(2)}) %collective-permute-start.16) | collective-permute-done | bytes 442400 | tf_op jit(solution)/shard_map/ppermute | solution.py:953
  280.2 2.3 third_split.1
  283.7 3.4 %collective-permute-start.19 = (bf16[72,768]{1,0:T(8,128)(2,1)}, bf16[72,768]{1,0:T(8,128)(2,1)S(1)}, u32[]{:S(2)}, u32[]{:S(2)}) collective-permute-start(bf16[72,768]{1,0:T(8,128)(2,1)} %get-tuple-element.124), channel_id=1, source_target_pairs={{0,4},{1,5},{2,6},{3,7},{4,0},{5,1},{6,2},{7,3},{8,12},{9,13},{10,... | collective-permute-start | bytes 331784 | tf_op jit(solution)/shard_map/ppermute | solution.py:953
  288.5 3.3 %collective-permute-start.22 = (bf16[48,768]{1,0:T(8,128)(2,1)S(1)}, bf16[48,768]{1,0:T(8,128)(2,1)S(1)}, u32[]{:S(2)}, u32[]{:S(2)}) collective-permute-start(bf16[48,768]{1,0:T(8,128)(2,1)S(1)} %get-tuple-element.185), channel_id=1, source_target_pairs={{0,16},{1,17},{2,18},{3,19},{4,20},{5,21},{6,22},{7,23},{8,24},{9,... | collective-permute-start | bytes 221192 | tf_op jit(solution)/shard_map/ppermute | solution.py:953
  292.0 2.4 collective-permute-done.22.refs_6_
  294.4 3.0 collective-permute-done.21.refs_5_
  298.1 2.0 last_split.1
  (113 shorter events, 35.2 us)
Async XLA Ops:
  7.2 98.6 %all-gather.5.cloned.1.call-start = ((), (), s32[]{:S(2)}) async-start(), calls=%async_computation.4 | async-start | bytes 22192128 | tf_op jit(solution)/shard_map/all_gather | solution.py:966
  9.0 2.7 collective-permute-start.2
  9.1 4.0 %collective-permute-start.1 = (bf16[3,6,768]{2,1,0:T(8,128)(2,1)S(1)}, bf16[3,6,768]{2,1,0:T(8,128)(2,1)S(1)}, u32[]{:S(2)}, u32[]{:S(2)}) collective-permute-start(bf16[3,6,768]{2,1,0:T(8,128)(2,1)S(1)} %get-tuple-element.193), channel_id=1, source_target_pairs={{0,2},{1,3},{2,0},{3,1},{4,6},{5,7},{6,4},{7,5},{8,10},{9,11},{10,... | collective-permute-start | bytes 82952 | tf_op jit(solution)/shard_map/ppermute | solution.py:916
  10.6 3.4 %collective-permute-start = (bf16[3,6,768]{2,1,0:T(8,128)(2,1)S(1)}, bf16[3,6,768]{2,1,0:T(8,128)(2,1)S(1)}, u32[]{:S(2)}, u32[]{:S(2)}) collective-permute-start(bf16[3,6,768]{2,1,0:T(8,128)(2,1)S(1)} %get-tuple-element.194), channel_id=1, source_target_pairs={{0,3},{1,2},{2,1},{3,0},{4,7},{5,6},{6,5},{7,4},{8,11},{9,10},{10,... | collective-permute-start | bytes 82952 | tf_op jit(solution)/shard_map/ppermute | solution.py:916
  15.7 197.4 %reduce-scatter.3.cloned.1.call-start = ((), (), s32[]{:S(2)}) async-start(), calls=%async_computation.2 | async-start | bytes 10616832 | tf_op jit(solution)/shard_map/reduce_scatter | solution.py:933
  147.6 121.9 %reduce-scatter.5.cloned.1.call-start = ((), (), s32[]{:S(2)}) async-start(), calls=%async_computation.3 | async-start | bytes 1474560 | tf_op jit(solution)/shard_map/reduce_scatter | solution.py:997
  172.9 8.1 %collective-permute-start.3 = (bf16[4,4,4,24,768]{4,3,2,1,0:T(8,128)(2,1)}, bf16[4,4,4,24,768]{4,3,2,1,0:T(8,128)(2,1)}, u32[]{:S(2)}, u32[]{:S(2)}) collective-permute-start(bf16[4,4,4,24,768]{4,3,2,1,0:T(8,128)(2,1)} %get-tuple-element.85), channel_id=1, source_target_pairs={{0,1},{1,0},{2,3},{3,2},{4,5},{5,4},{6,7},{7,6},{8,9},{9,8},{10,11... | collective-permute-start | bytes 7077896 | tf_op jit(solution)/shard_map/ppermute | solution.py:929
  185.6 16.4 %collective-permute-start.4 = (bf16[4,4,24,768]{3,2,1,0:T(8,128)(2,1)}, bf16[4,4,24,768]{3,2,1,0:T(8,128)(2,1)S(1)}, u32[]{:S(2)}, u32[]{:S(2)}) collective-permute-start(bf16[4,4,24,768]{3,2,1,0:T(8,128)(2,1)} %get-tuple-element.98), channel_id=1, source_target_pairs={{0,32},{1,9},{2,34},{3,11},{4,36},{5,13},{6,38},{7,15},{8,40},{9,1... | collective-permute-start | bytes 1769480 | tf_op jit(solution)/shard_map/ppermute | solution.py:953
  186.1 15.9 %collective-permute-start.5 = (bf16[4,4,24,768]{3,2,1,0:T(8,128)(2,1)}, bf16[4,4,24,768]{3,2,1,0:T(8,128)(2,1)S(1)}, u32[]{:S(2)}, u32[]{:S(2)}) collective-permute-start(bf16[4,4,24,768]{3,2,1,0:T(8,128)(2,1)} %get-tuple-element.99), channel_id=1, source_target_pairs={{0,64},{1,17},{2,66},{3,19},{4,68},{5,21},{6,70},{7,23},{8,72},{9,... | collective-permute-start | bytes 1769480 | tf_op jit(solution)/shard_map/ppermute | solution.py:953
  188.5 15.5 %collective-permute-start.6 = (bf16[4,4,24,768]{3,2,1,0:T(8,128)(2,1)}, bf16[4,4,24,768]{3,2,1,0:T(8,128)(2,1)S(1)}, u32[]{:S(2)}, u32[]{:S(2)}) collective-permute-start(bf16[4,4,24,768]{3,2,1,0:T(8,128)(2,1)} %get-tuple-element.100), channel_id=1, source_target_pairs={{0,96},{1,25},{2,98},{3,27},{4,100},{5,29},{6,102},{7,31},{8,104},... | collective-permute-start | bytes 1769480 | tf_op jit(solution)/shard_map/ppermute | solution.py:953
  204.0 9.1 %collective-permute-start.7 = (bf16[4,4,4,24,768]{4,3,2,1,0:T(8,128)(2,1)}, bf16[4,4,4,24,768]{4,3,2,1,0:T(8,128)(2,1)}, u32[]{:S(2)}, u32[]{:S(2)}) collective-permute-start(bf16[4,4,4,24,768]{4,3,2,1,0:T(8,128)(2,1)} %get-tuple-element.101), channel_id=1, source_target_pairs={{0,1},{1,0},{2,3},{3,2},{4,5},{5,4},{6,7},{7,6},{8,9},{9,8},{10,11... | collective-permute-start | bytes 7077896 | tf_op jit(solution)/shard_map/ppermute | solution.py:929
  213.1 8.4 %collective-permute-start.8 = (bf16[4,4,4,24,768]{4,3,2,1,0:T(8,128)(2,1)}, bf16[4,4,4,24,768]{4,3,2,1,0:T(8,128)(2,1)}, u32[]{:S(2)}, u32[]{:S(2)}) collective-permute-start(bf16[4,4,4,24,768]{4,3,2,1,0:T(8,128)(2,1)} %get-tuple-element.103), channel_id=1, source_target_pairs={{0,1},{1,0},{2,3},{3,2},{4,5},{5,4},{6,7},{7,6},{8,9},{9,8},{10,11... | collective-permute-start | bytes 7077896 | tf_op jit(solution)/shard_map/ppermute | solution.py:929
  218.0 17.6 %collective-permute-start.12 = (bf16[4,4,24,768]{3,2,1,0:T(8,128)(2,1)}, bf16[4,4,24,768]{3,2,1,0:T(8,128)(2,1)S(1)}, u32[]{:S(2)}, u32[]{:S(2)}) collective-permute-start(bf16[4,4,24,768]{3,2,1,0:T(8,128)(2,1)} %get-tuple-element.111), channel_id=1, source_target_pairs={{0,32},{1,9},{2,34},{3,11},{4,36},{5,13},{6,38},{7,15},{8,40},{9,1... | collective-permute-start | bytes 1769480 | tf_op jit(solution)/shard_map/ppermute | solution.py:953
  219.4 18.9 %collective-permute-start.13 = (bf16[4,4,24,768]{3,2,1,0:T(8,128)(2,1)}, bf16[4,4,24,768]{3,2,1,0:T(8,128)(2,1)S(1)}, u32[]{:S(2)}, u32[]{:S(2)}) collective-permute-start(bf16[4,4,24,768]{3,2,1,0:T(8,128)(2,1)} %get-tuple-element.112), channel_id=1, source_target_pairs={{0,64},{1,17},{2,66},{3,19},{4,68},{5,21},{6,70},{7,23},{8,72},{9,... | collective-permute-start | bytes 1769480 | tf_op jit(solution)/shard_map/ppermute | solution.py:953
  221.1 24.3 %collective-permute-start.14 = (bf16[4,4,24,768]{3,2,1,0:T(8,128)(2,1)}, bf16[4,4,24,768]{3,2,1,0:T(8,128)(2,1)S(1)}, u32[]{:S(2)}, u32[]{:S(2)}) collective-permute-start(bf16[4,4,24,768]{3,2,1,0:T(8,128)(2,1)} %get-tuple-element.113), channel_id=1, source_target_pairs={{0,96},{1,25},{2,98},{3,27},{4,100},{5,29},{6,102},{7,31},{8,104},... | collective-permute-start | bytes 1769480 | tf_op jit(solution)/shard_map/ppermute | solution.py:953
  226.2 24.2 %collective-permute-start.9 = (bf16[4,4,24,768]{3,2,1,0:T(8,128)(2,1)}, bf16[4,4,24,768]{3,2,1,0:T(8,128)(2,1)}, u32[]{:S(2)}, u32[]{:S(2)}) collective-permute-start(bf16[4,4,24,768]{3,2,1,0:T(8,128)(2,1)} %get-tuple-element.105), channel_id=1, source_target_pairs={{0,32},{1,9},{2,34},{3,11},{4,36},{5,13},{6,38},{7,15},{8,40},{9,1... | collective-permute-start | bytes 1769480 | tf_op jit(solution)/shard_map/ppermute | solution.py:953
  228.8 24.3 %collective-permute-start.10 = (bf16[4,4,24,768]{3,2,1,0:T(8,128)(2,1)}, bf16[4,4,24,768]{3,2,1,0:T(8,128)(2,1)}, u32[]{:S(2)}, u32[]{:S(2)}) collective-permute-start(bf16[4,4,24,768]{3,2,1,0:T(8,128)(2,1)} %get-tuple-element.106), channel_id=1, source_target_pairs={{0,64},{1,17},{2,66},{3,19},{4,68},{5,21},{6,70},{7,23},{8,72},{9,... | collective-permute-start | bytes 1769480 | tf_op jit(solution)/shard_map/ppermute | solution.py:953
  235.6 22.5 %copy-start.3 = (bf16[4,4,24,768]{3,2,1,0:T(8,128)(2,1)}, bf16[4,4,24,768]{3,2,1,0:T(8,128)(2,1)S(1)}, u32[]{:S(2)}) copy-start(bf16[4,4,24,768]{3,2,1,0:T(8,128)(2,1)S(1)} %collective-permute-done.12.refs_5_) | copy-start | bytes 1769476
  235.6 22.5 %collective-permute-start.11 = (bf16[4,4,24,768]{3,2,1,0:T(8,128)(2,1)}, bf16[4,4,24,768]{3,2,1,0:T(8,128)(2,1)}, u32[]{:S(2)}, u32[]{:S(2)}) collective-permute-start(bf16[4,4,24,768]{3,2,1,0:T(8,128)(2,1)} %get-tuple-element.107), channel_id=1, source_target_pairs={{0,96},{1,25},{2,98},{3,27},{4,100},{5,29},{6,102},{7,31},{8,104},... | collective-permute-start | bytes 1769480 | tf_op jit(solution)/shard_map/ppermute | solution.py:953
  238.3 19.9 %copy-start.4 = (bf16[4,4,24,768]{3,2,1,0:T(8,128)(2,1)}, bf16[4,4,24,768]{3,2,1,0:T(8,128)(2,1)S(1)}, u32[]{:S(2)}) copy-start(bf16[4,4,24,768]{3,2,1,0:T(8,128)(2,1)S(1)} %collective-permute-done.13.refs_6_) | copy-start | bytes 1769476
  263.4 9.7 %collective-permute-start.15 = (bf16[4,72,768]{2,1,0:T(8,128)(2,1)}, bf16[4,72,768]{2,1,0:T(8,128)(2,1)S(1)}, u32[]{:S(2)}, u32[]{:S(2)}) collective-permute-start(bf16[4,72,768]{2,1,0:T(8,128)(2,1)} %get-tuple-element.119), channel_id=1, source_target_pairs={{0,8},{1,33},{2,10},{3,35},{4,12},{5,37},{6,14},{7,39},{8,16},{9,4... | collective-permute-start | bytes 1327112 | tf_op jit(solution)/shard_map/ppermute | solution.py:953
  265.2 14.1 %collective-permute-start.16 = (bf16[4,72,768]{2,1,0:T(8,128)(2,1)}, bf16[4,72,768]{2,1,0:T(8,128)(2,1)S(1)}, u32[]{:S(2)}, u32[]{:S(2)}) collective-permute-start(bf16[4,72,768]{2,1,0:T(8,128)(2,1)} %get-tuple-element.120), channel_id=1, source_target_pairs={{0,16},{1,65},{2,18},{3,67},{4,20},{5,69},{6,22},{7,71},{8,24},{9,... | collective-permute-start | bytes 1327112 | tf_op jit(solution)/shard_map/ppermute | solution.py:953
  268.1 11.2 %collective-permute-start.17 = (bf16[4,72,768]{2,1,0:T(8,128)(2,1)}, bf16[4,72,768]{2,1,0:T(8,128)(2,1)S(1)}, u32[]{:S(2)}, u32[]{:S(2)}) collective-permute-start(bf16[4,72,768]{2,1,0:T(8,128)(2,1)} %get-tuple-element.121), channel_id=1, source_target_pairs={{0,24},{1,97},{2,26},{3,99},{4,28},{5,101},{6,30},{7,103},{8,0},{9... | collective-permute-start | bytes 1327112 | tf_op jit(solution)/shard_map/ppermute | solution.py:953
  271.1 20.7 %collective-permute-start.23 = (bf16[48,768]{1,0:T(8,128)(2,1)S(1)}, bf16[48,768]{1,0:T(8,128)(2,1)S(1)}, u32[]{:S(2)}, u32[]{:S(2)}) collective-permute-start(bf16[48,768]{1,0:T(8,128)(2,1)S(1)} %get-tuple-element.184), channel_id=1, source_target_pairs={{0,24},{1,25},{2,26},{3,27},{4,28},{5,29},{6,30},{7,31},{8,0},{9,1... | collective-permute-start | bytes 221192 | tf_op jit(solution)/shard_map/ppermute | solution.py:953
  282.5 14.8 %collective-permute-start.18 = (bf16[72,768]{1,0:T(8,128)(2,1)}, bf16[72,768]{1,0:T(8,128)(2,1)S(1)}, u32[]{:S(2)}, u32[]{:S(2)}) collective-permute-start(bf16[72,768]{1,0:T(8,128)(2,1)} %get-tuple-element.123), channel_id=1, source_target_pairs={{0,2},{1,3},{2,4},{3,5},{4,6},{5,7},{6,0},{7,1},{8,10},{9,11},{10,... | collective-permute-start | bytes 331784 | tf_op jit(solution)/shard_map/ppermute | solution.py:953
  283.7 13.7 %collective-permute-start.19 = (bf16[72,768]{1,0:T(8,128)(2,1)}, bf16[72,768]{1,0:T(8,128)(2,1)S(1)}, u32[]{:S(2)}, u32[]{:S(2)}) collective-permute-start(bf16[72,768]{1,0:T(8,128)(2,1)} %get-tuple-element.124), channel_id=1, source_target_pairs={{0,4},{1,5},{2,6},{3,7},{4,0},{5,1},{6,2},{7,3},{8,12},{9,13},{10,... | collective-permute-start | bytes 331784 | tf_op jit(solution)/shard_map/ppermute | solution.py:953
  287.1 10.3 %collective-permute-start.20 = (bf16[72,768]{1,0:T(8,128)(2,1)}, bf16[72,768]{1,0:T(8,128)(2,1)S(1)}, u32[]{:S(2)}, u32[]{:S(2)}) collective-permute-start(bf16[72,768]{1,0:T(8,128)(2,1)} %get-tuple-element.125), channel_id=1, source_target_pairs={{0,6},{1,7},{2,0},{3,1},{4,2},{5,3},{6,4},{7,5},{8,14},{9,15},{10,... | collective-permute-start | bytes 331784 | tf_op jit(solution)/shard_map/ppermute | solution.py:953
  288.5 5.9 %collective-permute-start.22 = (bf16[48,768]{1,0:T(8,128)(2,1)S(1)}, bf16[48,768]{1,0:T(8,128)(2,1)S(1)}, u32[]{:S(2)}, u32[]{:S(2)}) collective-permute-start(bf16[48,768]{1,0:T(8,128)(2,1)S(1)} %get-tuple-element.185), channel_id=1, source_target_pairs={{0,16},{1,17},{2,18},{3,19},{4,20},{5,21},{6,22},{7,23},{8,24},{9,... | collective-permute-start | bytes 221192 | tf_op jit(solution)/shard_map/ppermute | solution.py:953
  291.8 5.6 %collective-permute-start.21 = (bf16[48,768]{1,0:T(8,128)(2,1)S(1)}, bf16[48,768]{1,0:T(8,128)(2,1)S(1)}, u32[]{:S(2)}, u32[]{:S(2)}) collective-permute-start(bf16[48,768]{1,0:T(8,128)(2,1)S(1)} %get-tuple-element.186), channel_id=1, source_target_pairs={{0,8},{1,9},{2,10},{3,11},{4,12},{5,13},{6,14},{7,15},{8,16},{9,17... | collective-permute-start | bytes 221192 | tf_op jit(solution)/shard_map/ppermute | solution.py:953
  302.9 4.7 %collective-permute-start.24 = (bf16[3,6,768]{2,1,0:T(8,128)(2,1)}, bf16[3,6,768]{2,1,0:T(8,128)(2,1)S(1)}, u32[]{:S(2)}, u32[]{:S(2)}) collective-permute-start(bf16[3,6,768]{2,1,0:T(8,128)(2,1)} %get-tuple-element.129), channel_id=1, source_target_pairs={{0,1},{1,0},{2,3},{3,2},{4,5},{5,4},{6,7},{7,6},{8,9},{9,8},{10,11... | collective-permute-start | bytes 82952 | tf_op jit(solution)/shard_map/ppermute | solution.py:916
  302.9 4.7 %collective-permute-start.25 = (bf16[3,6,768]{2,1,0:T(8,128)(2,1)}, bf16[3,6,768]{2,1,0:T(8,128)(2,1)S(1)}, u32[]{:S(2)}, u32[]{:S(2)}) collective-permute-start(bf16[3,6,768]{2,1,0:T(8,128)(2,1)} %get-tuple-element.130), channel_id=1, source_target_pairs={{0,2},{1,3},{2,0},{3,1},{4,6},{5,7},{6,4},{7,5},{8,10},{9,11},{10,... | collective-permute-start | bytes 82952 | tf_op jit(solution)/shard_map/ppermute | solution.py:916
  303.5 4.1 %collective-permute-start.26 = (bf16[3,6,768]{2,1,0:T(8,128)(2,1)}, bf16[3,6,768]{2,1,0:T(8,128)(2,1)S(1)}, u32[]{:S(2)}, u32[]{:S(2)}) collective-permute-start(bf16[3,6,768]{2,1,0:T(8,128)(2,1)} %get-tuple-element.131), channel_id=1, source_target_pairs={{0,3},{1,2},{2,1},{3,0},{4,7},{5,6},{6,5},{7,4},{8,11},{9,10},{10,... | collective-permute-start | bytes 82952 | tf_op jit(solution)/shard_map/ppermute | solution.py:916
  (16 other events, 65.0 us)
Sparse Core Ops, SparseCore 0:
  15.8 89.9 all-gather.4
  147.7 56.8 reduce-scatter.2
  213.7 31.7 reduce-scatter.4

commit v2 on v1

--- a/solution.py
+++ b/solution.py
@@ -19,6 +19,7 @@
 COLS = 64
 TOKENS = ROWS * COLS
 SLAB = 24
+WIDE = D + 128
 PACK = 112
 PAIRS = 6
 EPS = 1e-05
@@ -575,7 +576,7 @@
         )
     loads["hidden"] = copies.start(hidden_saved.at[0], hidden)
     zeros[...] = jnp.zeros_like(zeros)
-    fills = [copies.start(zeros, out) for out in (own, other)]
+    fills = [copies.start(zeros, out.at[:, :, :, :, 0:D]) for out in (own, other)]
     gain = small[GAIN : GAIN + 1, :]
     col_lines = input_grads(loads, grad_in, gain, act, weights, hidden, da, grad_out, sums, lines)
     packed = small_lines(sums, sums_col, sums_ffn).astype(F32).reshape(4, 4, 4, 2, 1, 128)
@@ -583,12 +584,10 @@
     for copy in fills:
         copy.wait()
     sent = []
-    every = slice(None)
-    places = [(0, owned_lines.at[:, :, :, 0], (every, every))]
-    places += [(1, owned_lines.at[y, :, :, 1], (every, y)) for y in range(4)]
-    for parity, source, place in places:
-        place = place + (every, slice(16, 24), slice(0, 128))
-        sent.append(copies.send(ints[3], parity, source, own.at[place], other.at[place]))
+    for parity in range(2):
+        for x in range(4):
+            source, place = owned_lines.at[:, :, x, parity], (x, slice(None), slice(None), slice(0, 16), slice(D, WIDE))
+            sent.append(copies.send(ints[3], parity, source, own.at[place], other.at[place]))
     send_tables(ints, copies, lines[...], col_lines, table, own, other)
     for copy in sent:
         copy.wait()
@@ -615,8 +614,7 @@
     for slot, owner, start in spots:
         real, dev = owner < DEVICES, jnp.minimum(owner, DEVICES - 1)
         x, y, z = (dev // 2) % 4, dev // 32, (dev // 8) % 4
-        odd = dev % 2 == 1
-        place = (jnp.where(odd, z, y), jnp.where(odd, y, z), x, slice(start, start + 8))
+        place = (x, y, z, slice(start, start + 8), slice(0, D))
         sem = copies.sems.at[copies.used]
         copies.used += 1
         here = pltpu.make_async_copy(table.at[slot], own.at[place], sem)
@@ -749,18 +747,18 @@
         row_input_kernel,
         name="row_input",
         in_specs=[SMEM, VMEM, VMEM, VMEM, VMEM, ANY, ANY, ANY],
-        out_shape=(SHAPE(PLANE, F32), share_of(SLAB), share_of(SLAB)),
+        out_shape=(SHAPE(PLANE, F32),) + (SHAPE((4, 4, 4, 16, WIDE), BF16),) * 2,
         out_specs=(VMEM, ANY, ANY),
         scratch_shapes=[
             pltpu.VMEM((3, GROUPS, SLAB, D), BF16),
             pltpu.VMEM((3,) + PLANE, BF16),
             pltpu.VMEM(PLANE, F32),
             pltpu.VMEM(PLANE, F32),
-            pltpu.VMEM((4, 4, 4, SLAB, D), BF16),
+            pltpu.VMEM((4, 4, 4, 16, D), BF16),
             pltpu.VMEM((11, 8, D), BF16),
             pltpu.VMEM((ROWS, D), F32),
             pltpu.VMEM((8, D), F32),
-            pltpu.VMEM((4, 4, 4, 2, 8, 128), BF16),
+            pltpu.VMEM((4, 4, 4, 2, 16, 128), BF16),
             pltpu.SemaphoreType.DMA((48,)),
         ],
         compiler_params=params(),
@@ -768,28 +766,6 @@
     )(ints, grad, small, sums_col, sums_ffn, gathered, hidden, grads)
 
 
-def split_kernel(place, own, other, *pieces):
-    for hop in range(4):
-        to = (place[0] + hop) & 3
-
-        def body(j):
-            pieces[hop][j] = (own[to, j].astype(F32) + other[to, j].astype(F32)).astype(BF16)
-
-        loop(4, body)
-
-
-def split(own, other, place):
-    return pl.pallas_call(
-        split_kernel,
-        name="split_shares",
-        in_specs=[SMEM, VMEM, VMEM],
-        out_shape=(SHAPE((4, 4, SLAB, D), BF16),) * 4,
-        out_specs=(VMEM,) * 4,
-        compiler_params=params(),
-        cost_estimate=cost(10**6, 10**6),
-    )(place, own, other)
-
-
 def sum_of(pieces, *index):
     value = pieces[0][index].astype(F32)
     for piece in pieces[1:]:
@@ -797,56 +773,79 @@
     return value
 
 
+def split_kernel(place, *refs):
+    for hop in range(4):
+        refs[-4 + hop][0] = sum_of(refs[:-4], (place[0] + hop) & 3, 0).astype(BF16)
+
+
+def split(inputs, place):
+    shape = inputs[0].shape
+    rest = (0,) * (len(shape) - 2)
+    return pl.pallas_call(
+        split_kernel,
+        name="split_shares",
+        grid=(4,),
+        in_specs=[SMEM]
+        + [pl.BlockSpec((4, 1) + shape[2:], lambda j: (0, j) + rest)] * len(inputs),
+        out_shape=(SHAPE(shape[1:], BF16),) * 4,
+        out_specs=(pl.BlockSpec((1,) + shape[2:], lambda j: (j,) + rest),) * 4,
+        compiler_params=params(),
+        cost_estimate=cost(10**6, 10**6),
+    )(place, *inputs)
+
+
 def second_kernel(place, *refs):
-    groups, pieces = [refs[4 * g : 4 * g + 4] for g in range(3)], refs[12:]
     for hop in range(4):
         to = (place[0] + hop) & 3
-
-        def body(j):
-            for g, group in enumerate(groups):
-                rows = slice(g * SLAB, (g + 1) * SLAB)
-                pieces[hop][j, rows, :] = sum_of(group, to, j).astype(BF16)
-
-        loop(4, body)
-
-
-def second_split(row, table, col, place):
+        for g in range(2):
+            value = sum_of(refs[4 * g : 4 * g + 4], to, 0)
+            refs[8 + hop][0, g * SLAB : (g + 1) * SLAB, :] = value.astype(BF16)
+
+
+def second_split(row, col, place):
     return pl.pallas_call(
         second_kernel,
         name="second_split",
-        in_specs=[SMEM] + [VMEM] * 12,
-        out_shape=(SHAPE((4, 3 * SLAB, D), BF16),) * 4,
-        out_specs=(VMEM,) * 4,
+        grid=(4,),
+        in_specs=[SMEM] + [pl.BlockSpec((4, 1, SLAB, D), lambda j: (0, j, 0, 0))] * 8,
+        out_shape=(SHAPE((4, 2 * SLAB, D), BF16),) * 4,
+        out_specs=(pl.BlockSpec((1, 2 * SLAB, D), lambda j: (j, 0, 0)),) * 4,
         compiler_params=params(),
         cost_estimate=cost(10**6, 10**6),
-    )(place, *row, *table, *col)
-
-
-def third_kernel(place, *refs):
+    )(place, *row, *col)
+
+
+def third_kernel(place, ffn, *refs):
+    rows, table, pieces = refs[:4], refs[4:8], refs[8:]
     for hop in range(4):
-        refs[4 + hop][...] = sum_of(refs[:4], (place[0] + hop) & 3).astype(BF16)
-
-
-def third_split(rows, place):
+        pieces[hop][...] = sum_of(rows, (place[0] + hop) & 3).astype(BF16)
+        to = (place[1] + hop) & 3
+        value = sum_of(table, to).astype(BF16)
+        pieces[4 + hop][0:16, :] = value[:, 0:D]
+        pieces[4 + hop][16:24, :] = jnp.zeros((8, D), BF16)
+        pieces[4 + hop][16:24, 0:128] = value[0:8, D:WIDE]
+        pieces[4 + hop][SLAB : 3 * SLAB, :] = ffn[to]
+
+
+def third_split(rows, table, ffn, place):
     return pl.pallas_call(
         third_kernel,
         name="third_split",
-        in_specs=[SMEM] + [VMEM] * 4,
-        out_shape=(SHAPE((3 * SLAB, D), BF16),) * 4,
-        out_specs=(VMEM,) * 4,
+        in_specs=[SMEM] + [VMEM] * 9,
+        out_shape=(SHAPE((2 * SLAB, D), BF16),) * 4 + (SHAPE((3 * SLAB, D), BF16),) * 4,
+        out_specs=(VMEM,) * 8,
         compiler_params=params(),
         cost_estimate=cost(10**6, 10**6),
-    )(place, *rows)
+    )(place, ffn, *rows, *table)
 
 
 def last_kernel(me, *refs):
-    parts, ffn, (down, tables, line), pieces, held = refs[:4], refs[4:8], refs[8:11], refs[11:15], refs[15]
-    down[...] = sum_of(ffn, slice(SLAB, 2 * SLAB))
+    rows, rest, (down, tables, line), pieces, held = refs[:4], refs[4:8], refs[8:11], refs[11:15], refs[15]
+    down[...] = sum_of(rest, slice(2 * SLAB, 3 * SLAB))
     for i in range(2):
-        rows = slice(SLAB + 8 * i, SLAB + 8 * i + 8)
-        tables[i] = sum_of(parts, rows)
-    line[...] = sum_of(parts, slice(SLAB + 16, SLAB + 24))
-    for kind, (source, start) in enumerate(((parts, 0), (parts, 2 * SLAB), (ffn, 0))):
+        tables[i] = sum_of(rest, slice(8 * i, 8 * i + 8))
+    line[...] = sum_of(rest, slice(16, 24))
+    for kind, (source, start) in enumerate(((rows, 0), (rows, SLAB), (rest, SLAB))):
         value = sum_of(source, slice(start, start + SLAB))
         for member in range(MEMBERS):
             held[member, kind] = value[6 * member : 6 * member + 6, :]
@@ -854,7 +853,7 @@
         pieces[flip][...] = held[me[0] ^ flip].astype(BF16)
 
 
-def last_split(me, rows, ffn):
+def last_split(me, rows, rest):
     return pl.pallas_call(
         last_kernel,
         name="last_split",
@@ -869,7 +868,7 @@
         scratch_shapes=[pltpu.VMEM((MEMBERS, 3, 6, D), F32)],
         compiler_params=params(),
         cost_estimate=cost(10**6, 10**6),
-    )(me, *rows, *ffn)
+    )(me, *rows, *rest)
 
 
 def outputs_kernel(me, one, two, three, four, row_qkv, row_out, col_qkv, col_out, up, held):
@@ -934,6 +933,7 @@
 
 
 STAGES = (("y", "z"), ("z", "y"), ("x", "x"))
+TABLE_STAGES = (("x", "x"), ("y", "y"), ("z", "z"))
 STRIDES = {"y": 32, "z": 8, "x": 2}
 
 
@@ -986,7 +986,7 @@
     row_heads = heads_call(False, ints, g1, gathered, saved)
     places = [place_on(axes) for axes in STAGES]
     other, row_heads = barrier((swap(other), row_heads))
-    pieces, row_heads = barrier((split(own, other, places[0]), row_heads))
+    pieces, row_heads = barrier((split((own, other), places[0]), row_heads))
     col = deliver(pieces, STAGES[0])
     g0, table_own, table_other = row_input_call(
         ints, g1, small, col_sums, ffn_sums, gathered, hidden, row_heads
@@ -995,18 +995,20 @@
     table_other, col = barrier((table_other, col))
     other, table_other, ffn = barrier((other, swap(table_other), ffn))
     ffn = lax.psum_scatter(ffn.reshape(4, 4, 2 * SLAB, D), "y", scatter_dimension=0, tiled=False)
-    table = deliver(split(table_own, table_other, places[0]), STAGES[0])
-    row = deliver(split(own, swap(other), places[0]), STAGES[0])
-    rows = deliver(second_split(row, table, col, places[1]), STAGES[1])
-    z = lax.axis_index("z")
-    ffn = deliver([take(ffn, (z + hop) % 4, 0) for hop in range(4)], ("z", "z"))
-    rows = deliver(third_split(rows, places[2]), STAGES[2])
-    return (act.reshape(tokens.shape), g0.reshape(tokens.shape)) + owned(rows, ffn)
-
-
-def owned(rows, ffn):
+    y_place, z_place = place_on(TABLE_STAGES[1]), place_on(TABLE_STAGES[2])
+    table, other = barrier((split((table_own, table_other), places[2]), swap(other)))
+    table = deliver(table, TABLE_STAGES[0])
+    row = deliver(split((own, other), places[0]), STAGES[0])
+    table = deliver(split(table, y_place), TABLE_STAGES[1])
+    rows = deliver(second_split(row, col, places[1]), STAGES[1])
+    pieces = third_split(rows, table, ffn, jnp.concatenate([places[2], z_place]))
+    rows, rest = deliver(pieces[:4], STAGES[2]), deliver(pieces[4:], TABLE_STAGES[2])
+    return (act.reshape(tokens.shape), g0.reshape(tokens.shape)) + owned(rows, rest)
+
+
+def owned(rows, rest):
     me = member().astype(jnp.int32)[None]
-    down, tables, line, *pieces = last_split(me, rows, ffn)
+    down, tables, line, *pieces = last_split(me, rows, rest)
     row_qkv, row_out, col_qkv, col_out, up = outputs(me, trade(pieces))
     sixes = line[0, :96].reshape(6, 16).T
     row_sums, col_sums, ffn_sums = sixes[0:5], sixes[5:10], sixes[10:13]

time: 322 us -> 313 us (0.972)
  waiting for transfers between devices: 97.4 us -> 81.5 us
  starting transfers between devices: 30.2 us -> 35.4 us
    ppermute x18 -> x21, waiting for transfers between devices: 44.1 us -> 28.2 us  [deliver(): came.append(lax.ppermute(pieces[hop], AXES, pairs))]
    ppermute x18 -> x21, starting transfers between devices: 25.3 us -> 30.1 us  [deliver(): came.append(lax.ppermute(pieces[hop], AXES, pairs))]
    unnamed x40 -> x48, local copies, waits for them, and re-layouts: 4.9 us -> 7.67 us
    pallas_call x4 -> x5, Pallas kernels: 18.9 us -> 20.6 us  [the longest x4 16.3 us: split(): pl.pallas_call(split_kernel, name='split_shares', grid=(4,), in_specs=[SM...]
  transfers between devices with their start and end apart: 30 -> 33, of which waited for: 14 -> 11; matrix products, arithmetic and copies ran while one was open for 4% -> 3% of each run, Pallas kernels for 24% -> 24%
where the time goes in v2:
time: 313 us; the launch traced here: 309 us
  Pallas kernels  123 us (39%)
  waiting for transfers between devices  81.5 us (26%)
  starting transfers between devices  35.4 us (11%)
  blocking collectives  31.4 us (10%)
  between operations  16.1 us (5%)
  local copies, waits for them, and re-layouts  15.8 us (5%)
  other arithmetic  5.32 us (2%)
    all_gather x1, waiting for transfers between devices, gather(): gathered = lax.all_gather(packed, AXES, axis=0, tiled=False)  50.8 us
    pallas_call x1, Pallas kernels, forward_call(): pl.pallas_call(forward_kernel, name='forward', in_specs=[SMEM, VMEM, VMEM...  41.7 us
    all_gather x1, blocking collectives, gather(): lines = lax.all_gather(line, AXES, axis=0, tiled=False).astype(F32)  31.4 us
    ppermute x21, starting transfers between devices, deliver(): came.append(lax.ppermute(pieces[hop], AXES, pairs))  30.1 us
    ppermute x21, waiting for transfers between devices, deliver(): came.append(lax.ppermute(pieces[hop], AXES, pairs))  28.2 us
    pallas_call x2, Pallas kernels, heads_call(): pl.pallas_call(lambda *refs: heads_kernel(column, *refs), name='column_he...  19 us
    pallas_call x4, Pallas kernels, split(): pl.pallas_call(split_kernel, name='split_shares', grid=(4,), in_specs=[SM...  16.3 us
    pallas_call x1, Pallas kernels, column_call(): pl.pallas_call(column_kernel, name='column_weights', in_specs=[SMEM, VMEM...  13.9 us
  transfers between devices with their start and end apart: 33, of which 11 were waited for; matrix products, arithmetic and copies ran while one was open for 3% of the time, Pallas kernels for 24%

profile of v2, /device:TPU:24, one launch (start us, length us, event | category | flops | bytes accessed | tf_op | source)
XLA Modules:
  0.0 308.8 jit_solution(12285431915109612015)
XLA Ops:
  9.1 1.6 collective-permute-start.1
  17.7 2.2 concatenate.22
  20.7 31.4 %all-gather.2 = bf16[128,1,128]{2,1,0:T(2,128)(2,1)S(1)} all-gather(bf16[1,1,128]{2,1,0:T(2,128)(2,1)S(1)} %fusion.1), channel_id=2, replica_groups=mesh['y'=4,'z'=4,'x'=4,'c'=2] {'y','z','x','c'}, dimensions={0}, use_global_device_ids=true | all-gather | bytes 33024 | tf_op jit(solution)/shard_map/all_gather | solution.py:969
  55.0 50.8 %all-gather.5.cloned.1.call-done = bf16[14336,768]{1,0:T(8,128)(2,1)} async-done(((bf16[112,768]{1,0:T(8,128)(2,1)}), bf16[14336,768]{1,0:T(8,128)(2,1)}) %all-gather.5.cloned.1.call-update) | async-done | bytes 22020112 | tf_op jit(solution)/shard_map/all_gather | solution.py:966
  105.8 41.7 %forward.1 = (bf16[512,768]{1,0:T(8,128)(2,1)}, f32[512,768]{1,0:T(8,128)}, bf16[10,512,768]{2,1,0:T(8,128)(2,1)}, f32[2,512,768]{2,1,0:T(8,128)}, bf16[8,16,48,768]{3,2,1,0:T(8,128)(2,1)}, /*index=5*/f32[8,768]{1,0:T(8,128)}) custom-call(s32[4]{0:T(128)} %pad_add_fusion.ints.refs_0_, bf16[512,768]{1,0:T(8,128)(2,1)} %bitcast.88, bf16[512,768]{1,0:T(8,128)(2,1)} %bitcast.89, ...), custom_call_target="tpu_custom_call" | custom-call | flops 24000000000 | bytes 50000000 | tf_op jit(solution)/shard_map/forward/pallas_call | solution.py:645
  147.8 11.2 %column_heads.1.grads_in = bf16[3,512,768]{2,1,0:T(8,128)(2,1)} custom-call(s32[4]{0:T(128)} %pad_add_fusion.ints.refs_0_, f32[512,768]{1,0:T(8,128)} %get-tuple-element.91.refs_1_.grad_in, bf16[32,4,112,768]{3,2,1,0:T(8,128)(2,1)} %bitcast.73, bf16[10,512,768]{2,1,0:T(8,128)(2,1)} %get-tuple-element.92.refs_3_.saved), custom_call_target="tpu_custom_call" | custom-call | flops 10000000000 | bytes 10000000 | tf_op jit(solution)/shard_map/column_heads/pallas_call | solution.py:679
  159.0 13.9 %column_weights.1 = (f32[512,768]{1,0:T(8,128)}, bf16[4,4,4,24,768]{4,3,2,1,0:T(8,128)(2,1)}, bf16[4,4,4,24,768]{4,3,2,1,0:T(8,128)(2,1)}, f32[8,768]{1,0:T(8,128)}) custom-call(s32[4]{0:T(128)} %pad_add_fusion.ints.refs_0_, f32[512,768]{1,0:T(8,128)} %get-tuple-element.91.refs_1_.grad_in, f32[16,768]{1,0:T(8,128)} %pad.9.small, ...), custom_call_target="tpu_custom_call" | custom-call | flops 10000000000 | bytes 10000000 | tf_op jit(solution)/shard_map/column_weights/pallas_call | solution.py:703
  173.3 7.7 %row_heads.1.grads_in = bf16[3,512,768]{2,1,0:T(8,128)(2,1)} custom-call(s32[4]{0:T(128)} %pad_add_fusion.ints.refs_0_, f32[512,768]{1,0:T(8,128)} %get-tuple-element.94.refs_1_.grad_in, bf16[32,4,112,768]{3,2,1,0:T(8,128)(2,1)} %bitcast.75, bf16[10,512,768]{2,1,0:T(8,128)(2,1)} %get-tuple-element.92.refs_3_.saved), custom_call_target="tpu_custom_call" | custom-call | flops 10000000000 | bytes 10000000 | tf_op jit(solution)/shard_map/row_heads/pallas_call | solution.py:679
  181.1 4.4 %split_shares.4 = (bf16[4,4,24,768]{3,2,1,0:T(8,128)(2,1)}, bf16[4,4,24,768]{3,2,1,0:T(8,128)(2,1)}, bf16[4,4,24,768]{3,2,1,0:T(8,128)(2,1)}, bf16[4,4,24,768]{3,2,1,0:T(8,128)(2,1)}) custom-call(s32[1]{0:T(128)} %bitcast.29.place, bf16[4,4,4,24,768]{4,3,2,1,0:T(8,128)(2,1)} %get-tuple-element.97.refs_0_, ...), custom_call_target="tpu_custom_call" | custom-call | flops 1000000 | bytes 1000000 | tf_op jit(solution)/shard_map/split_shares/pallas_call | solution.py:784
  185.9 2.4 collective-permute-start.5
  188.4 13.3 %row_input.1 = (f32[512,768]{1,0:T(8,128)}, bf16[4,4,4,16,896]{4,3,2,1,0:T(8,128)(2,1)}, bf16[4,4,4,16,896]{4,3,2,1,0:T(8,128)(2,1)}) custom-call(s32[4]{0:T(128)} %pad_add_fusion.ints.refs_0_, f32[512,768]{1,0:T(8,128)} %get-tuple-element.94.refs_1_.grad_in, f32[16,768]{1,0:T(8,128)} %pad.9.small, f32[8,768]{1,0:T(8,128)} %get-tuple-element.95.sums_col, ...), custom_call_target="tpu_custom_call" | custom-call | flops 20000000000 | bytes 10000000 | tf_op jit(solution)/shard_map/row_input/pallas_call | solution.py:746
  201.8 2.1 collective-permute-done.6.refs_7_
  205.4 8.8 %row_weights.1 = (bf16[4,4,4,24,768]{4,3,2,1,0:T(8,128)(2,1)}, bf16[4,4,4,24,768]{4,3,2,1,0:T(8,128)(2,1)}) custom-call(s32[4]{0:T(128)} %pad_add_fusion.ints.refs_0_, f32[512,768]{1,0:T(8,128)} %get-tuple-element.94.refs_1_.grad_in, bf16[10,512,768]{2,1,0:T(8,128)(2,1)} %get-tuple-element.92.refs_3_.saved, bf16[3,512,768]{2,1,0:T(8,128)(2,1)} %row_heads.1.grads_in), custom_call_target="tpu_custom_call" | custom-call | flops 1000000 | bytes 100000 | tf_op jit(solution)/shard_map/row_weights/pallas_call | solution.py:726
  215.6 4.0 %split_shares.5 = (bf16[4,4,16,896]{3,2,1,0:T(8,128)(2,1)}, bf16[4,4,16,896]{3,2,1,0:T(8,128)(2,1)}, bf16[4,4,16,896]{3,2,1,0:T(8,128)(2,1)}, bf16[4,4,16,896]{3,2,1,0:T(8,128)(2,1)}) custom-call(s32[1]{0:T(128)} %bitcast.32.place, bf16[4,4,4,16,896]{4,3,2,1,0:T(8,128)(2,1)} %get-tuple-element.117.refs_0_, bf16[4,4,4,16,896]{4,3,2,1,0:T(8,128)(2,1)} %copy-done), custom_call_target="tpu_custom_call" | custom-call | flops 1000000 | bytes 1000000 | tf_op jit(solution)/shard_map/split_shares/pallas_call | solution.py:784
  219.6 4.4 %split_shares.6 = (bf16[4,4,24,768]{3,2,1,0:T(8,128)(2,1)}, bf16[4,4,24,768]{3,2,1,0:T(8,128)(2,1)}, bf16[4,4,24,768]{3,2,1,0:T(8,128)(2,1)}, bf16[4,4,24,768]{3,2,1,0:T(8,128)(2,1)}) custom-call(s32[1]{0:T(128)} %bitcast.29.place, bf16[4,4,4,24,768]{4,3,2,1,0:T(8,128)(2,1)} %get-tuple-element.116.refs_0_, ...), custom_call_target="tpu_custom_call" | custom-call | flops 1000000 | bytes 1000000 | tf_op jit(solution)/shard_map/split_shares/pallas_call | solution.py:784
  228.3 2.8 collective-permute-start.16
  231.1 9.2 %collective-permute-done.9.refs_1_ = bf16[4,4,24,768]{3,2,1,0:T(8,128)(2,1)S(1)} collective-permute-done((bf16[4,4,24,768]{3,2,1,0:T(8,128)(2,1)}, bf16[4,4,24,768]{3,2,1,0:T(8,128)(2,1)S(1)}, u32[]{:S(2)}, u32[]{:S(2)}) %collective-permute-start.9) | collective-permute-done | bytes 589856 | tf_op jit(solution)/shard_map/ppermute | solution.py:953
  240.3 2.7 collective-permute-start.17
  243.0 5.0 %collective-permute-done.11.refs_3_ = bf16[4,4,24,768]{3,2,1,0:T(8,128)(2,1)S(1)} collective-permute-done((bf16[4,4,24,768]{3,2,1,0:T(8,128)(2,1)}, bf16[4,4,24,768]{3,2,1,0:T(8,128)(2,1)S(1)}, u32[]{:S(2)}, u32[]{:S(2)}) %collective-permute-start.11) | collective-permute-done | bytes 589856 | tf_op jit(solution)/shard_map/ppermute | solution.py:953
  248.8 4.2 %second_split.1 = (bf16[4,48,768]{2,1,0:T(8,128)(2,1)}, bf16[4,48,768]{2,1,0:T(8,128)(2,1)}, bf16[4,48,768]{2,1,0:T(8,128)(2,1)}, bf16[4,48,768]{2,1,0:T(8,128)(2,1)}) custom-call(s32[1]{0:T(128)} %bitcast.37.place, bf16[4,4,24,768]{3,2,1,0:T(8,128)(2,1)} %get-tuple-element.125.refs_0_, bf16[4,4,24,768]{3,2,1,0:T(8,128)(2,1)} %copy-done.4, ...), custom_call_target="tpu_custom_call" | custom-call | flops 1000000 | bytes 1000000 | tf_op jit(solution)/shard_map/second_split/pallas_call | solution.py:806
  253.1 1.6 collective-permute-start.12
  254.7 2.8 collective-permute-start.13
  258.9 3.5 %split_shares.7 = (bf16[4,16,896]{2,1,0:T(8,128)(2,1)}, bf16[4,16,896]{2,1,0:T(8,128)(2,1)}, bf16[4,16,896]{2,1,0:T(8,128)(2,1)}, bf16[4,16,896]{2,1,0:T(8,128)(2,1)}) custom-call(s32[1]{0:T(128)} %bitcast.38.place, bf16[4,4,16,896]{3,2,1,0:T(8,128)(2,1)} %get-tuple-element.137.refs_0_, bf16[4,4,16,896]{3,2,1,0:T(8,128)(2,1)} %collective-permute-done.15.refs_1_, ...), custom_call_target="tpu_custom_call" | custom-call | flops 1000000 | bytes 1000000 | tf_op jit(solution)/shard_map/split_shares/pallas_call | solution.py:784
  264.3 3.1 %collective-permute-done.18.refs_5_ = bf16[4,16,896]{2,1,0:T(8,128)(2,1)S(1)} collective-permute-done((bf16[4,16,896]{2,1,0:T(8,128)(2,1)}, bf16[4,16,896]{2,1,0:T(8,128)(2,1)S(1)}, u32[]{:S(2)}, u32[]{:S(2)}) %collective-permute-start.18) | collective-permute-done | bytes 114720 | tf_op jit(solution)/shard_map/ppermute | solution.py:953
  268.0 2.4 collective-permute-done.19.refs_6_
  270.5 3.2 %collective-permute-done.20.refs_7_ = bf16[4,16,896]{2,1,0:T(8,128)(2,1)S(1)} collective-permute-done((bf16[4,16,896]{2,1,0:T(8,128)(2,1)}, bf16[4,16,896]{2,1,0:T(8,128)(2,1)S(1)}, u32[]{:S(2)}, u32[]{:S(2)}) %collective-permute-start.20) | collective-permute-done | bytes 114720 | tf_op jit(solution)/shard_map/ppermute | solution.py:953
  274.6 2.4 third_split.1
  277.1 2.2 collective-permute-start.21
  280.7 1.8 collective-permute-start.26
  282.6 2.7 collective-permute-start.22
  286.7 1.9 collective-permute-done.22.refs_2_
  290.6 2.0 last_split.1
  (128 shorter events, 39.0 us)
Async XLA Ops:
  7.2 98.6 %all-gather.5.cloned.1.call-start = ((), (), s32[]{:S(2)}) async-start(), calls=%async_computation.4 | async-start | bytes 22192128 | tf_op jit(solution)/shard_map/all_gather | solution.py:966
  9.1 4.0 %collective-permute-start.1 = (bf16[3,6,768]{2,1,0:T(8,128)(2,1)S(1)}, bf16[3,6,768]{2,1,0:T(8,128)(2,1)S(1)}, u32[]{:S(2)}, u32[]{:S(2)}) collective-permute-start(bf16[3,6,768]{2,1,0:T(8,128)(2,1)S(1)} %get-tuple-element.215), channel_id=1, source_target_pairs={{0,2},{1,3},{2,0},{3,1},{4,6},{5,7},{6,4},{7,5},{8,10},{9,11},{10,... | collective-permute-start | bytes 82952 | tf_op jit(solution)/shard_map/ppermute | solution.py:915
  10.6 3.4 %collective-permute-start = (bf16[3,6,768]{2,1,0:T(8,128)(2,1)S(1)}, bf16[3,6,768]{2,1,0:T(8,128)(2,1)S(1)}, u32[]{:S(2)}, u32[]{:S(2)}) collective-permute-start(bf16[3,6,768]{2,1,0:T(8,128)(2,1)S(1)} %get-tuple-element.216), channel_id=1, source_target_pairs={{0,3},{1,2},{2,1},{3,0},{4,7},{5,6},{6,5},{7,4},{8,11},{9,10},{10,... | collective-permute-start | bytes 82952 | tf_op jit(solution)/shard_map/ppermute | solution.py:915
  15.7 198.6 %reduce-scatter.3.cloned.1.call-start = ((), (), s32[]{:S(2)}) async-start(), calls=%async_computation.2 | async-start | bytes 10616832 | tf_op jit(solution)/shard_map/reduce_scatter | solution.py:932
  147.6 120.5 %reduce-scatter.5.cloned.1.call-start = ((), (), s32[]{:S(2)}) async-start(), calls=%async_computation.3 | async-start | bytes 1474560 | tf_op jit(solution)/shard_map/reduce_scatter | solution.py:997
  172.9 8.1 %collective-permute-start.3 = (bf16[4,4,4,24,768]{4,3,2,1,0:T(8,128)(2,1)}, bf16[4,4,4,24,768]{4,3,2,1,0:T(8,128)(2,1)}, u32[]{:S(2)}, u32[]{:S(2)}) collective-permute-start(bf16[4,4,4,24,768]{4,3,2,1,0:T(8,128)(2,1)} %get-tuple-element.98), channel_id=1, source_target_pairs={{0,1},{1,0},{2,3},{3,2},{4,5},{5,4},{6,7},{7,6},{8,9},{9,8},{10,11... | collective-permute-start | bytes 7077896 | tf_op jit(solution)/shard_map/ppermute | solution.py:928
  185.5 16.2 %collective-permute-start.4 = (bf16[4,4,24,768]{3,2,1,0:T(8,128)(2,1)}, bf16[4,4,24,768]{3,2,1,0:T(8,128)(2,1)S(1)}, u32[]{:S(2)}, u32[]{:S(2)}) collective-permute-start(bf16[4,4,24,768]{3,2,1,0:T(8,128)(2,1)} %get-tuple-element.110), channel_id=1, source_target_pairs={{0,32},{1,9},{2,34},{3,11},{4,36},{5,13},{6,38},{7,15},{8,40},{9,1... | collective-permute-start | bytes 1769480 | tf_op jit(solution)/shard_map/ppermute | solution.py:953
  185.9 15.8 %collective-permute-start.5 = (bf16[4,4,24,768]{3,2,1,0:T(8,128)(2,1)}, bf16[4,4,24,768]{3,2,1,0:T(8,128)(2,1)S(1)}, u32[]{:S(2)}, u32[]{:S(2)}) collective-permute-start(bf16[4,4,24,768]{3,2,1,0:T(8,128)(2,1)} %get-tuple-element.111), channel_id=1, source_target_pairs={{0,64},{1,17},{2,66},{3,19},{4,68},{5,21},{6,70},{7,23},{8,72},{9,... | collective-permute-start | bytes 1769480 | tf_op jit(solution)/shard_map/ppermute | solution.py:953
  188.4 15.5 %collective-permute-start.6 = (bf16[4,4,24,768]{3,2,1,0:T(8,128)(2,1)}, bf16[4,4,24,768]{3,2,1,0:T(8,128)(2,1)S(1)}, u32[]{:S(2)}, u32[]{:S(2)}) collective-permute-start(bf16[4,4,24,768]{3,2,1,0:T(8,128)(2,1)} %get-tuple-element.112), channel_id=1, source_target_pairs={{0,96},{1,25},{2,98},{3,27},{4,100},{5,29},{6,102},{7,31},{8,104},... | collective-permute-start | bytes 1769480 | tf_op jit(solution)/shard_map/ppermute | solution.py:953
  204.7 9.6 %collective-permute-start.7 = (bf16[4,4,4,16,896]{4,3,2,1,0:T(8,128)(2,1)}, bf16[4,4,4,16,896]{4,3,2,1,0:T(8,128)(2,1)S(1)}, u32[]{:S(2)}, u32[]{:S(2)}) collective-permute-start(bf16[4,4,4,16,896]{4,3,2,1,0:T(8,128)(2,1)} %get-tuple-element.113), channel_id=1, source_target_pairs={{0,1},{1,0},{2,3},{3,2},{4,5},{5,4},{6,7},{7,6},{8,9},{9,8},{10,11... | collective-permute-start | bytes 5505032 | tf_op jit(solution)/shard_map/ppermute | solution.py:928
  214.3 5.3 %collective-permute-start.8 = (bf16[4,4,4,24,768]{4,3,2,1,0:T(8,128)(2,1)}, bf16[4,4,4,24,768]{4,3,2,1,0:T(8,128)(2,1)}, u32[]{:S(2)}, u32[]{:S(2)}) collective-permute-start(bf16[4,4,4,24,768]{4,3,2,1,0:T(8,128)(2,1)} %get-tuple-element.123), channel_id=1, source_target_pairs={{0,1},{1,0},{2,3},{3,2},{4,5},{5,4},{6,7},{7,6},{8,9},{9,8},{10,11... | collective-permute-start | bytes 7077896 | tf_op jit(solution)/shard_map/ppermute | solution.py:928
  224.0 16.3 %collective-permute-start.9 = (bf16[4,4,24,768]{3,2,1,0:T(8,128)(2,1)}, bf16[4,4,24,768]{3,2,1,0:T(8,128)(2,1)S(1)}, u32[]{:S(2)}, u32[]{:S(2)}) collective-permute-start(bf16[4,4,24,768]{3,2,1,0:T(8,128)(2,1)} %get-tuple-element.126), channel_id=1, source_target_pairs={{0,32},{1,9},{2,34},{3,11},{4,36},{5,13},{6,38},{7,15},{8,40},{9,1... | collective-permute-start | bytes 1769480 | tf_op jit(solution)/shard_map/ppermute | solution.py:953
  225.5 17.4 %collective-permute-start.10 = (bf16[4,4,24,768]{3,2,1,0:T(8,128)(2,1)}, bf16[4,4,24,768]{3,2,1,0:T(8,128)(2,1)S(1)}, u32[]{:S(2)}, u32[]{:S(2)}) collective-permute-start(bf16[4,4,24,768]{3,2,1,0:T(8,128)(2,1)} %get-tuple-element.127), channel_id=1, source_target_pairs={{0,64},{1,17},{2,66},{3,19},{4,68},{5,21},{6,70},{7,23},{8,72},{9,... | collective-permute-start | bytes 1769480 | tf_op jit(solution)/shard_map/ppermute | solution.py:953
  226.9 21.1 %collective-permute-start.11 = (bf16[4,4,24,768]{3,2,1,0:T(8,128)(2,1)}, bf16[4,4,24,768]{3,2,1,0:T(8,128)(2,1)S(1)}, u32[]{:S(2)}, u32[]{:S(2)}) collective-permute-start(bf16[4,4,24,768]{3,2,1,0:T(8,128)(2,1)} %get-tuple-element.128), channel_id=1, source_target_pairs={{0,96},{1,25},{2,98},{3,27},{4,100},{5,29},{6,102},{7,31},{8,104},... | collective-permute-start | bytes 1769480 | tf_op jit(solution)/shard_map/ppermute | solution.py:953
  226.9 30.6 %collective-permute-start.15 = (bf16[4,4,16,896]{3,2,1,0:T(8,128)(2,1)}, bf16[4,4,16,896]{3,2,1,0:T(8,128)(2,1)}, u32[]{:S(2)}, u32[]{:S(2)}) collective-permute-start(bf16[4,4,16,896]{3,2,1,0:T(8,128)(2,1)} %get-tuple-element.138), channel_id=1, source_target_pairs={{0,2},{1,3},{2,4},{3,5},{4,6},{5,7},{6,0},{7,1},{8,10},{9,11},{10,... | collective-permute-start | bytes 1376264 | tf_op jit(solution)/shard_map/ppermute | solution.py:953
  228.3 30.6 %collective-permute-start.16 = (bf16[4,4,16,896]{3,2,1,0:T(8,128)(2,1)}, bf16[4,4,16,896]{3,2,1,0:T(8,128)(2,1)}, u32[]{:S(2)}, u32[]{:S(2)}) collective-permute-start(bf16[4,4,16,896]{3,2,1,0:T(8,128)(2,1)} %get-tuple-element.139), channel_id=1, source_target_pairs={{0,4},{1,5},{2,6},{3,7},{4,0},{5,1},{6,2},{7,3},{8,12},{9,13},{10,... | collective-permute-start | bytes 1376264 | tf_op jit(solution)/shard_map/ppermute | solution.py:953
  240.3 18.6 %collective-permute-start.17 = (bf16[4,4,16,896]{3,2,1,0:T(8,128)(2,1)}, bf16[4,4,16,896]{3,2,1,0:T(8,128)(2,1)}, u32[]{:S(2)}, u32[]{:S(2)}) collective-permute-start(bf16[4,4,16,896]{3,2,1,0:T(8,128)(2,1)} %get-tuple-element.140), channel_id=1, source_target_pairs={{0,6},{1,7},{2,0},{3,1},{4,2},{5,3},{6,4},{7,5},{8,14},{9,15},{10,... | collective-permute-start | bytes 1376264 | tf_op jit(solution)/shard_map/ppermute | solution.py:953
  253.1 20.6 %collective-permute-start.12 = (bf16[4,48,768]{2,1,0:T(8,128)(2,1)}, bf16[4,48,768]{2,1,0:T(8,128)(2,1)S(1)}, u32[]{:S(2)}, u32[]{:S(2)}) collective-permute-start(bf16[4,48,768]{2,1,0:T(8,128)(2,1)} %get-tuple-element.134), channel_id=1, source_target_pairs={{0,8},{1,33},{2,10},{3,35},{4,12},{5,37},{6,14},{7,39},{8,16},{9,4... | collective-permute-start | bytes 884744 | tf_op jit(solution)/shard_map/ppermute | solution.py:953
  254.7 19.0 %collective-permute-start.13 = (bf16[4,48,768]{2,1,0:T(8,128)(2,1)}, bf16[4,48,768]{2,1,0:T(8,128)(2,1)S(1)}, u32[]{:S(2)}, u32[]{:S(2)}) collective-permute-start(bf16[4,48,768]{2,1,0:T(8,128)(2,1)} %get-tuple-element.135), channel_id=1, source_target_pairs={{0,16},{1,65},{2,18},{3,67},{4,20},{5,69},{6,22},{7,71},{8,24},{9,... | collective-permute-start | bytes 884744 | tf_op jit(solution)/shard_map/ppermute | solution.py:953
  257.5 16.2 %collective-permute-start.14 = (bf16[4,48,768]{2,1,0:T(8,128)(2,1)}, bf16[4,48,768]{2,1,0:T(8,128)(2,1)S(1)}, u32[]{:S(2)}, u32[]{:S(2)}) collective-permute-start(bf16[4,48,768]{2,1,0:T(8,128)(2,1)} %get-tuple-element.136), channel_id=1, source_target_pairs={{0,24},{1,97},{2,26},{3,99},{4,28},{5,101},{6,30},{7,103},{8,0},{9... | collective-permute-start | bytes 884744 | tf_op jit(solution)/shard_map/ppermute | solution.py:953
  262.4 5.0 %collective-permute-start.18 = (bf16[4,16,896]{2,1,0:T(8,128)(2,1)}, bf16[4,16,896]{2,1,0:T(8,128)(2,1)S(1)}, u32[]{:S(2)}, u32[]{:S(2)}) collective-permute-start(bf16[4,16,896]{2,1,0:T(8,128)(2,1)} %get-tuple-element.142), channel_id=1, source_target_pairs={{0,32},{1,33},{2,34},{3,35},{4,36},{5,37},{6,38},{7,39},{8,40},{9,... | collective-permute-start | bytes 344072 | tf_op jit(solution)/shard_map/ppermute | solution.py:953
  263.9 6.5 %collective-permute-start.19 = (bf16[4,16,896]{2,1,0:T(8,128)(2,1)}, bf16[4,16,896]{2,1,0:T(8,128)(2,1)S(1)}, u32[]{:S(2)}, u32[]{:S(2)}) collective-permute-start(bf16[4,16,896]{2,1,0:T(8,128)(2,1)} %get-tuple-element.143), channel_id=1, source_target_pairs={{0,64},{1,65},{2,66},{3,67},{4,68},{5,69},{6,70},{7,71},{8,72},{9,... | collective-permute-start | bytes 344072 | tf_op jit(solution)/shard_map/ppermute | solution.py:953
  267.5 6.2 %collective-permute-start.20 = (bf16[4,16,896]{2,1,0:T(8,128)(2,1)}, bf16[4,16,896]{2,1,0:T(8,128)(2,1)S(1)}, u32[]{:S(2)}, u32[]{:S(2)}) collective-permute-start(bf16[4,16,896]{2,1,0:T(8,128)(2,1)} %get-tuple-element.144), channel_id=1, source_target_pairs={{0,96},{1,97},{2,98},{3,99},{4,100},{5,101},{6,102},{7,103},{8,104... | collective-permute-start | bytes 344072 | tf_op jit(solution)/shard_map/ppermute | solution.py:953
  277.1 8.2 %collective-permute-start.21 = (bf16[48,768]{1,0:T(8,128)(2,1)}, bf16[48,768]{1,0:T(8,128)(2,1)S(1)}, u32[]{:S(2)}, u32[]{:S(2)}) collective-permute-start(bf16[48,768]{1,0:T(8,128)(2,1)} %get-tuple-element.146), channel_id=1, source_target_pairs={{0,2},{1,3},{2,4},{3,5},{4,6},{5,7},{6,0},{7,1},{8,10},{9,11},{10,... | collective-permute-start | bytes 221192 | tf_op jit(solution)/shard_map/ppermute | solution.py:953
  279.3 10.6 %collective-permute-start.24 = (bf16[72,768]{1,0:T(8,128)(2,1)}, bf16[72,768]{1,0:T(8,128)(2,1)S(1)}, u32[]{:S(2)}, u32[]{:S(2)}) collective-permute-start(bf16[72,768]{1,0:T(8,128)(2,1)} %get-tuple-element.150), channel_id=1, source_target_pairs={{0,8},{1,9},{2,10},{3,11},{4,12},{5,13},{6,14},{7,15},{8,16},{9,17... | collective-permute-start | bytes 331784 | tf_op jit(solution)/shard_map/ppermute | solution.py:953
  279.9 9.9 %collective-permute-start.25 = (bf16[72,768]{1,0:T(8,128)(2,1)}, bf16[72,768]{1,0:T(8,128)(2,1)S(1)}, u32[]{:S(2)}, u32[]{:S(2)}) collective-permute-start(bf16[72,768]{1,0:T(8,128)(2,1)} %get-tuple-element.151), channel_id=1, source_target_pairs={{0,16},{1,17},{2,18},{3,19},{4,20},{5,21},{6,22},{7,23},{8,24},{9,... | collective-permute-start | bytes 331784 | tf_op jit(solution)/shard_map/ppermute | solution.py:953
  280.7 9.1 %collective-permute-start.26 = (bf16[72,768]{1,0:T(8,128)(2,1)}, bf16[72,768]{1,0:T(8,128)(2,1)S(1)}, u32[]{:S(2)}, u32[]{:S(2)}) collective-permute-start(bf16[72,768]{1,0:T(8,128)(2,1)} %get-tuple-element.152), channel_id=1, source_target_pairs={{0,24},{1,25},{2,26},{3,27},{4,28},{5,29},{6,30},{7,31},{8,0},{9,1... | collective-permute-start | bytes 331784 | tf_op jit(solution)/shard_map/ppermute | solution.py:953
  282.6 6.1 %collective-permute-start.22 = (bf16[48,768]{1,0:T(8,128)(2,1)}, bf16[48,768]{1,0:T(8,128)(2,1)S(1)}, u32[]{:S(2)}, u32[]{:S(2)}) collective-permute-start(bf16[48,768]{1,0:T(8,128)(2,1)} %get-tuple-element.147), channel_id=1, source_target_pairs={{0,4},{1,5},{2,6},{3,7},{4,0},{5,1},{6,2},{7,3},{8,12},{9,13},{10,... | collective-permute-start | bytes 221192 | tf_op jit(solution)/shard_map/ppermute | solution.py:953
  285.3 4.6 %collective-permute-start.23 = (bf16[48,768]{1,0:T(8,128)(2,1)}, bf16[48,768]{1,0:T(8,128)(2,1)S(1)}, u32[]{:S(2)}, u32[]{:S(2)}) collective-permute-start(bf16[48,768]{1,0:T(8,128)(2,1)} %get-tuple-element.148), channel_id=1, source_target_pairs={{0,6},{1,7},{2,0},{3,1},{4,2},{5,3},{6,4},{7,5},{8,14},{9,15},{10,... | collective-permute-start | bytes 221192 | tf_op jit(solution)/shard_map/ppermute | solution.py:953
  295.4 4.7 %collective-permute-start.27 = (bf16[3,6,768]{2,1,0:T(8,128)(2,1)}, bf16[3,6,768]{2,1,0:T(8,128)(2,1)S(1)}, u32[]{:S(2)}, u32[]{:S(2)}) collective-permute-start(bf16[3,6,768]{2,1,0:T(8,128)(2,1)} %get-tuple-element.155), channel_id=1, source_target_pairs={{0,1},{1,0},{2,3},{3,2},{4,5},{5,4},{6,7},{7,6},{8,9},{9,8},{10,11... | collective-permute-start | bytes 82952 | tf_op jit(solution)/shard_map/ppermute | solution.py:915
  295.4 4.7 %collective-permute-start.28 = (bf16[3,6,768]{2,1,0:T(8,128)(2,1)}, bf16[3,6,768]{2,1,0:T(8,128)(2,1)S(1)}, u32[]{:S(2)}, u32[]{:S(2)}) collective-permute-start(bf16[3,6,768]{2,1,0:T(8,128)(2,1)} %get-tuple-element.156), channel_id=1, source_target_pairs={{0,2},{1,3},{2,0},{3,1},{4,6},{5,7},{6,4},{7,5},{8,10},{9,11},{10,... | collective-permute-start | bytes 82952 | tf_op jit(solution)/shard_map/ppermute | solution.py:915
  295.8 4.3 %collective-permute-start.29 = (bf16[3,6,768]{2,1,0:T(8,128)(2,1)}, bf16[3,6,768]{2,1,0:T(8,128)(2,1)S(1)}, u32[]{:S(2)}, u32[]{:S(2)}) collective-permute-start(bf16[3,6,768]{2,1,0:T(8,128)(2,1)} %get-tuple-element.157), channel_id=1, source_target_pairs={{0,3},{1,2},{2,1},{3,0},{4,7},{5,6},{6,5},{7,4},{8,11},{9,10},{10,... | collective-permute-start | bytes 82952 | tf_op jit(solution)/shard_map/ppermute | solution.py:915
  (23 other events, 45.8 us)
Sparse Core Ops, SparseCore 0:
  15.8 89.9 all-gather.4
  147.7 56.8 reduce-scatter.2
  214.6 30.2 reduce-scatter.4

commit v3 on v2

--- a/solution.py
+++ b/solution.py
@@ -210,12 +210,6 @@
             ref[plane, rows, :] = value.astype(BF16)
 
     loop(2, body)
-
-
-def by_halves(grads, which, index, value):
-    value = value.astype(BF16).reshape(8, 2, SLAB, D)
-    for half in range(2):
-        grads[which, pl.ds(16 * half + 8 * index, 8)] = value[:, half]
 
 
 class Copies:
@@ -326,7 +320,7 @@
         bias = up_bias[pl.ds(f, 1), :]
 
         def body(index):
-            rows = chunk(index, 256)
+            rows = chunk(index, 512)
             z = dot(a3[rows, :], up) + bias
             cdf = 0.5 * (1.0 + lax.erf(z * math.sqrt(0.5)))
             slope = cdf + z * (jnp.exp(-0.5 * z * z) * (1.0 / math.sqrt(2.0 * math.pi)))
@@ -347,17 +341,15 @@
                 y[rows, :] += more
                 da[rows, :] += more_da
 
-        loop(2, body)
+        loop(1, body)
         sums[pl.ds(f, 1), :] = total(wide[1].astype(F32))
 
-        def back(index):
-            cols = chunk(index, 384)
-            value = dot_tn(wide[0, :, cols], gy[...]).astype(BF16).reshape(2, 8, SLAB, D)
-            for k in range(8):
-                grads[4 + f, pl.ds(4 * k + 2 * index, 2)] = value[:, k]
-            by_halves(grads, f, index, dot_tn(a3[:, cols], wide[1]))
-
-        loop(2, back)
+        value = dot_tn(wide[0], gy[...]).astype(BF16).reshape(4, 8, SLAB, D)
+        for k in range(8):
+            grads[4 + f, 4 * k : 4 * k + 4] = value[:, k]
+        value = dot_tn(a3[...], wide[1]).astype(BF16).reshape(16, 2, SLAB, D)
+        for half in range(2):
+            grads[f, 16 * half : 16 * half + 16] = value[:, half]
         for copy in ffn_sends(f):
             copy.start()
 
@@ -399,12 +391,10 @@
         copy.wait()
 
 
-def heads_kernel(column, ints, grad_in, gathered, saved, grads_out, weight, act, sems):
-    first, planes = (24, (Q2, K2, V2)) if column else (0, (Q1, K1, V1))
-    heads = ColHeads() if column else RowHeads(ints[0])
+def row_heads_kernel(ints, grad_in, gathered, saved, grads_out, weight, act, sems):
     copies = Copies(sems)
-    load = copies.start(gathered.at[:, 3, first : first + SLAB, :], weight.at[0])
-    act_loads = [copies.start(saved.at[plane], act.at[i]) for i, plane in enumerate(planes)]
+    load = copies.start(gathered.at[:, 3, 0:SLAB, :], weight.at[0])
+    act_loads = [copies.start(saved.at[plane], act.at[i]) for i, plane in enumerate((Q1, K1, V1))]
     load.wait()
 
     def mixed_back(index):
@@ -414,7 +404,7 @@
     loop(2, mixed_back)
     for copy in act_loads:
         copy.wait()
-    attend_back(heads, act, 0, 1, 2, 3)
+    attend_back(RowHeads(ints[0]), act, 0, 1, 2, 3)
     stores = [copies.start(act.at[i], grads_out.at[i]) for i in range(3)]
     for copy in stores:
         copy.wait()
@@ -442,13 +432,13 @@
             copy.wait()
 
 
-def keep(grads, which, part, value):
-    value = value.astype(BF16).reshape(2, 4, 2, SLAB, D)
+def keep(grads, which, value):
+    value = value.astype(BF16).reshape(4, 4, 2, SLAB, D)
     for half in range(2):
-        grads[which, half, pl.ds(2 * part, 2)] = value[:, :, half]
-
-
-def weight_grads(loads, grad_in, act, out_grad, normed, mixed, grads, shares):
+        grads[which, half] = value[:, :, half]
+
+
+def weight_grads(loads, act_loads, grad_in, act, out_grad, normed, mixed, grads, shares):
     def low(index):
         rows = chunk(index, 128)
         out_grad[rows, :] = grad_in[rows, :].astype(BF16)
@@ -456,20 +446,15 @@
     loop(4, low)
     loads["mixed"].wait()
 
-    def out_back(index):
-        keep(grads, 3, index, dot_tn(mixed[:, chunk(index, 384)], out_grad[...]))
-
-    loop(2, out_back)
+    keep(grads, 3, dot_tn(mixed[...], out_grad[...]))
     shares.send(grads, 3)
-    loads["normed"].wait()
-    for i in range(3):
-        loads[i].wait()
-
-    def weight_back(index):
-        which, part = index // 2, index % 2
-        keep(grads, which, part, dot_tn(normed[:, chunk(part, 384)], act[which]))
-
-    loop(6, weight_back)
+    for copy in [loads["normed"]] + act_loads:
+        copy.wait()
+
+    def weight_back(which):
+        keep(grads, which, dot_tn(normed[...], act[which]))
+
+    loop(3, weight_back)
     for member in range(3):
         shares.send(grads, member)
 
@@ -511,20 +496,29 @@
 
 
 def column_kernel(
-    ints, grad_in, small, gathered, saved, hidden_saved, grads_in,
+    ints, grad_in, small, gathered, saved, hidden_saved,
     grad_out, own, other, sums,
     weights, act, out_grad, normed, mixed, hidden, da, grads, sems,
 ):
     copies = Copies(sems)
     shares = Shares(ints[3], copies, own, other)
+    slabs = [gathered.at[:, i, SLAB : 2 * SLAB, :] for i in range(4)]
+    out_load = copies.start(slabs[3], weights.at[3])
+    act_loads = [copies.start(saved.at[plane], act.at[i]) for i, plane in enumerate((Q2, K2, V2))]
     loads = {"mixed": copies.start(saved.at[M2], mixed), "normed": copies.start(saved.at[A2], normed)}
-    for i in range(3):
-        loads[i] = copies.start(grads_in.at[i], act.at[i])
-    loads["inputs"] = [
-        [copies.start(gathered.at[:, i, SLAB : 2 * SLAB, :], weights.at[i])] for i in range(3)
-    ]
+    loads["inputs"] = [[copies.start(slabs[i], weights.at[i])] for i in range(3)]
     loads["hidden"] = copies.start(hidden_saved.at[1], hidden)
-    weight_grads(loads, grad_in, act, out_grad, normed, mixed, grads, shares)
+    out_load.wait()
+
+    def mixed_back(index):
+        rows = chunk(index, 256)
+        act[3, rows, :] = dot_nt(grad_in[rows, :].astype(BF16), whole(weights, 3)).astype(BF16)
+
+    loop(2, mixed_back)
+    for copy in act_loads:
+        copy.wait()
+    attend_back(ColHeads(), act, 0, 1, 2, 3)
+    weight_grads(loads, [], grad_in, act, out_grad, normed, mixed, grads, shares)
     input_grads(loads, grad_in, small[GAIN + 1 : GAIN + 2, :], act, weights, hidden, da, grad_out, sums)
     shares.wait()
 
@@ -535,9 +529,8 @@
     copies = Copies(sems)
     shares = Shares(ints[3], copies, own, other)
     loads = {"mixed": copies.start(saved.at[M1], mixed), "normed": copies.start(saved.at[A1], normed)}
-    for i in range(3):
-        loads[i] = copies.start(grads_in.at[i], act.at[i])
-    weight_grads(loads, grad_in, act, out_grad, normed, mixed, grads, shares)
+    act_loads = [copies.start(grads_in.at[i], act.at[i]) for i in range(3)]
+    weight_grads(loads, act_loads, grad_in, act, out_grad, normed, mixed, grads, shares)
     shares.wait()
 
 
@@ -674,11 +667,11 @@
     )(ints, tokens, cotangent, small, up_bias, gathered)
 
 
-def heads_call(column, ints, grad, gathered, saved):
+def row_heads_call(ints, grad, gathered, saved):
     plane = (TOKENS, D)
     return pl.pallas_call(
-        lambda *refs: heads_kernel(column, *refs),
-        name="column_heads" if column else "row_heads",
+        row_heads_kernel,
+        name="row_heads",
         in_specs=[SMEM, VMEM, ANY, ANY],
         out_shape=SHAPE((3,) + plane, BF16),
         out_specs=ANY,
@@ -699,27 +692,27 @@
     return SHAPE((4, 4, 4, rows, D), BF16)
 
 
-def column_call(ints, grad, small, gathered, saved, hidden, grads):
+def column_call(ints, grad, small, gathered, saved, hidden):
     return pl.pallas_call(
         column_kernel,
-        name="column_weights",
-        in_specs=[SMEM, VMEM, VMEM, ANY, ANY, ANY, ANY],
+        name="column_back",
+        in_specs=[SMEM, VMEM, VMEM, ANY, ANY, ANY],
         out_shape=(SHAPE(PLANE, F32), share_of(SLAB), share_of(SLAB), SHAPE((8, D), F32)),
         out_specs=(VMEM, ANY, ANY, VMEM),
         scratch_shapes=[
-            pltpu.VMEM((3, GROUPS, SLAB, D), BF16),
-            pltpu.VMEM((3,) + PLANE, BF16),
+            pltpu.VMEM((4, GROUPS, SLAB, D), BF16),
+            pltpu.VMEM((4,) + PLANE, BF16),
             pltpu.VMEM(PLANE, BF16),
             pltpu.VMEM(PLANE, BF16),
             pltpu.VMEM(PLANE, BF16),
             pltpu.VMEM(PLANE, F32),
             pltpu.VMEM(PLANE, F32),
             pltpu.VMEM((4, 2, 4, 4, SLAB, D), BF16),
-            pltpu.SemaphoreType.DMA((32,)),
+            pltpu.SemaphoreType.DMA((48,)),
         ],
         compiler_params=params(),
         cost_estimate=cost(10**10, 10**7),
-    )(ints, grad, small, gathered, saved, hidden, grads)
+    )(ints, grad, small, gathered, saved, hidden)
 
 
 def row_weights_call(ints, grad, saved, grads):
@@ -840,11 +833,23 @@
 
 
 def last_kernel(me, *refs):
-    rows, rest, (down, tables, line), pieces, held = refs[:4], refs[4:8], refs[8:11], refs[11:15], refs[15]
+    rows, rest, (down, tables), small, pieces, held = refs[:4], refs[4:8], refs[8:10], refs[10:16], refs[16:20], refs[20]
     down[...] = sum_of(rest, slice(2 * SLAB, 3 * SLAB))
     for i in range(2):
         tables[i] = sum_of(rest, slice(8 * i, 8 * i + 8))
-    line[...] = sum_of(rest, slice(16, 24))
+    line = sum_of(rest, slice(16, 24), slice(0, 128))[0:1]
+    gain, shift, row_bias, col_bias, up_bias, down_bias = small
+    up_bias[...] = line[:, 96:120]
+    lines = jnp.broadcast_to(line, (16, 128))
+    value, lane = (lax.broadcasted_iota(jnp.int32, lines.shape, axis) for axis in (0, 1))
+    for j in range(6):
+        column = jnp.sum(jnp.where(lane == 16 * j + value, lines, 0.0), axis=1, keepdims=True)
+        at = slice(j, j + 1)
+        for i, first in enumerate((0, 5, 11)):
+            gain[i : i + 1, at] = column[first : first + 1]
+            shift[i : i + 1, at] = column[first + 1 : first + 2]
+        row_bias[:, at], col_bias[:, at] = column[2:5], column[7:10]
+        down_bias[:, at] = column[10:11]
     for kind, (source, start) in enumerate(((rows, 0), (rows, SLAB), (rest, SLAB))):
         value = sum_of(source, slice(start, start + SLAB))
         for member in range(MEMBERS):
@@ -861,10 +866,11 @@
         out_shape=(
             SHAPE((SLAB, D), F32),
             SHAPE((2, 8, D), F32),
-            SHAPE((8, D), F32),
         )
+        + (SHAPE((3, 6), F32),) * 4
+        + (SHAPE((1, SLAB), F32), SHAPE((1, 6), F32))
         + (SHAPE((3, 6, D), BF16),) * 4,
-        out_specs=(VMEM,) * 7,
+        out_specs=(VMEM,) * 12,
         scratch_shapes=[pltpu.VMEM((MEMBERS, 3, 6, D), F32)],
         compiler_params=params(),
         cost_estimate=cost(10**6, 10**6),
@@ -981,9 +987,8 @@
     )
     barrier = lax.optimization_barrier
     ffn = scatter_chip_rows(ffn_shares)
-    col_heads = heads_call(True, ints, g2, gathered, saved)
-    g1, own, other, col_sums = column_call(ints, g2, small, gathered, saved, hidden, col_heads)
-    row_heads = heads_call(False, ints, g1, gathered, saved)
+    g1, own, other, col_sums = column_call(ints, g2, small, gathered, saved, hidden)
+    row_heads = row_heads_call(ints, g1, gathered, saved)
     places = [place_on(axes) for axes in STAGES]
     other, row_heads = barrier((swap(other), row_heads))
     pieces, row_heads = barrier((split((own, other), places[0]), row_heads))
@@ -992,8 +997,8 @@
         ints, g1, small, col_sums, ffn_sums, gathered, hidden, row_heads
     )
     own, other = row_weights_call(ints, g1, saved, row_heads)
-    table_other, col = barrier((table_other, col))
-    other, table_other, ffn = barrier((other, swap(table_other), ffn))
+    table_other, col, ffn = barrier((table_other, col, ffn))
+    other, table_other = barrier((other, swap(table_other)))
     ffn = lax.psum_scatter(ffn.reshape(4, 4, 2 * SLAB, D), "y", scatter_dimension=0, tiled=False)
     y_place, z_place = place_on(TABLE_STAGES[1]), place_on(TABLE_STAGES[2])
     table, other = barrier((split((table_own, table_other), places[2]), swap(other)))
@@ -1008,25 +1013,21 @@
 
 def owned(rows, rest):
     me = member().astype(jnp.int32)[None]
-    down, tables, line, *pieces = last_split(me, rows, rest)
+    down, tables, gain, shift, row_bias, col_bias, up_bias, down_bias, *pieces = last_split(me, rows, rest)
     row_qkv, row_out, col_qkv, col_out, up = outputs(me, trade(pieces))
-    sixes = line[0, :96].reshape(6, 16).T
-    row_sums, col_sums, ffn_sums = sixes[0:5], sixes[5:10], sixes[10:13]
-    gain = jnp.stack([row_sums[0], col_sums[0], ffn_sums[1]])
-    shift_grad = jnp.stack([row_sums[1], col_sums[1], ffn_sums[2]])
     return (
         gain,
-        shift_grad,
+        shift,
         row_qkv,
         row_out,
-        row_sums[2:5],
+        row_bias,
         col_qkv,
         col_out,
-        col_sums[2:5],
+        col_bias,
         up,
-        line[0, 96:120],
+        up_bias[0],
         down,
-        ffn_sums[0],
+        down_bias[0],
         tables,
     )
 

time: 313 us -> 306 us (0.978)
  waiting for transfers between devices: 81.5 us -> 91.6 us
  Pallas kernels: 123 us -> 115 us
  local copies, waits for them, and re-layouts: 15.8 us -> 9.03 us
    reduce_scatter x1, waiting for transfers between devices: 0.02 us -> 5.38 us  [scatter_chip_rows(): lax.psum_scatter(shares, ('x', 'c'), scatter_dimension=0, tiled=False)]
    pallas_call x3 -> x2, Pallas kernels: 32.9 us -> 28.2 us  [the longest x1 20.5 us: column_call(): pl.pallas_call(column_kernel, name='column_back', in_specs=[SMEM, VMEM, V...]
    unnamed x48 -> x44, local copies, waits for them, and re-layouts: 7.67 us -> 3.67 us
  transfers between devices with their start and end apart: 33 -> 33, of which waited for: 11 -> 13; matrix products, arithmetic and copies ran while one was open for 3% -> 2% of each run, Pallas kernels for 24% -> 23%
where the time goes in v3:
time: 306 us; the launch traced here: 302 us
  Pallas kernels  115 us (38%)
  waiting for transfers between devices  91.6 us (30%)
  starting transfers between devices  33.5 us (11%)
  blocking collectives  31.4 us (10%)
  between operations  16 us (5%)
  local copies, waits for them, and re-layouts  9.03 us (3%)
  other arithmetic  5.17 us (2%)
    all_gather x1, waiting for transfers between devices, gather(): gathered = lax.all_gather(packed, AXES, axis=0, tiled=False)  50.8 us
    pallas_call x1, Pallas kernels, forward_call(): pl.pallas_call(forward_kernel, name='forward', in_specs=[SMEM, VMEM, VMEM...  39 us
    all_gather x1, blocking collectives, gather(): lines = lax.all_gather(line, AXES, axis=0, tiled=False).astype(F32)  31.4 us
    ppermute x21, waiting for transfers between devices, deliver(): came.append(lax.ppermute(pieces[hop], AXES, pairs))  30.3 us
    ppermute x21, starting transfers between devices, deliver(): came.append(lax.ppermute(pieces[hop], AXES, pairs))  28.3 us
    pallas_call x1, Pallas kernels, column_call(): pl.pallas_call(column_kernel, name='column_back', in_specs=[SMEM, VMEM, V...  20.5 us
    pallas_call x4, Pallas kernels, split(): pl.pallas_call(split_kernel, name='split_shares', grid=(4,), in_specs=[SM...  16.4 us
    pallas_call x1, Pallas kernels, row_input_call(): pl.pallas_call(row_input_kernel, name='row_input', in_specs=[SMEM, VMEM,...  13.3 us
  transfers between devices with their start and end apart: 33, of which 13 were waited for; matrix products, arithmetic and copies ran while one was open for 2% of the time, Pallas kernels for 23%

profile of v3, /device:TPU:24, one launch (start us, length us, event | category | flops | bytes accessed | tf_op | source)
XLA Modules:
  0.0 302.0 jit_solution(8404192136170856283)
XLA Ops:
  17.7 2.2 concatenate.22
  20.7 31.4 %all-gather.2 = bf16[128,1,128]{2,1,0:T(2,128)(2,1)S(1)} all-gather(bf16[1,1,128]{2,1,0:T(2,128)(2,1)S(1)} %fusion.1), channel_id=2, replica_groups=mesh['y'=4,'z'=4,'x'=4,'c'=2] {'y','z','x','c'}, dimensions={0}, use_global_device_ids=true | all-gather | bytes 33024 | tf_op jit(solution)/shard_map/all_gather | solution.py:975
  55.0 50.8 %all-gather.5.cloned.1.call-done = bf16[14336,768]{1,0:T(8,128)(2,1)} async-done(((bf16[112,768]{1,0:T(8,128)(2,1)}), bf16[14336,768]{1,0:T(8,128)(2,1)}) %all-gather.5.cloned.1.call-update) | async-done | bytes 22020112 | tf_op jit(solution)/shard_map/all_gather | solution.py:972
  105.8 39.0 %forward.1 = (bf16[512,768]{1,0:T(8,128)(2,1)}, f32[512,768]{1,0:T(8,128)}, bf16[10,512,768]{2,1,0:T(8,128)(2,1)}, f32[2,512,768]{2,1,0:T(8,128)}, bf16[8,16,48,768]{3,2,1,0:T(8,128)(2,1)}, /*index=5*/f32[8,768]{1,0:T(8,128)}) custom-call(s32[4]{0:T(128)} %pad_add_fusion.ints, bf16[512,768]{1,0:T(8,128)(2,1)} %bitcast.84, bf16[512,768]{1,0:T(8,128)(2,1)} %bitcast.85, ...), custom_call_target="tpu_custom_call" | custom-call | flops 24000000000 | bytes 50000000 | tf_op jit(solution)/shard_map/forward/pallas_call | solution.py:638
  145.0 20.5 %column_back.1 = (f32[512,768]{1,0:T(8,128)}, bf16[4,4,4,24,768]{4,3,2,1,0:T(8,128)(2,1)}, bf16[4,4,4,24,768]{4,3,2,1,0:T(8,128)(2,1)}, f32[8,768]{1,0:T(8,128)}) custom-call(s32[4]{0:T(128)} %pad_add_fusion.ints, f32[512,768]{1,0:T(8,128)} %get-tuple-element.96.grad_in, f32[16,768]{1,0:T(8,128)} %pad.9.small, bf16[32,4,112,768]{3,2,1,0:T(8,128)(2,1)} %bitcast.81, ...), custom_call_target="tpu_custom_call" | custom-call | flops 10000000000 | bytes 10000000 | tf_op jit(solution)/shard_map/column_back/pallas_call | solution.py:696
  165.9 7.7 %row_heads.1.grads_in = bf16[3,512,768]{2,1,0:T(8,128)(2,1)} custom-call(s32[4]{0:T(128)} %pad_add_fusion.ints, f32[512,768]{1,0:T(8,128)} %get-tuple-element.99.grad_in, bf16[32,4,112,768]{3,2,1,0:T(8,128)(2,1)} %bitcast.82, bf16[10,512,768]{2,1,0:T(8,128)(2,1)} %get-tuple-element.97.saved), custom_call_target="tpu_custom_call" | custom-call | flops 10000000000 | bytes 10000000 | tf_op jit(solution)/shard_map/row_heads/pallas_call | solution.py:672
  173.6 4.4 %split_shares.4 = (bf16[4,4,24,768]{3,2,1,0:T(8,128)(2,1)}, bf16[4,4,24,768]{3,2,1,0:T(8,128)(2,1)}, bf16[4,4,24,768]{3,2,1,0:T(8,128)(2,1)}, bf16[4,4,24,768]{3,2,1,0:T(8,128)(2,1)}) custom-call(s32[1]{0:T(128)} %bitcast.29.place, bf16[4,4,4,24,768]{4,3,2,1,0:T(8,128)(2,1)} %get-tuple-element.102.refs_0_, ...), custom_call_target="tpu_custom_call" | custom-call | flops 1000000 | bytes 1000000 | tf_op jit(solution)/shard_map/split_shares/pallas_call | solution.py:777
  178.5 2.4 collective-permute-start.5
  180.9 13.3 %row_input.1 = (f32[512,768]{1,0:T(8,128)}, bf16[4,4,4,16,896]{4,3,2,1,0:T(8,128)(2,1)}, bf16[4,4,4,16,896]{4,3,2,1,0:T(8,128)(2,1)}) custom-call(s32[4]{0:T(128)} %pad_add_fusion.ints, f32[512,768]{1,0:T(8,128)} %get-tuple-element.99.grad_in, f32[16,768]{1,0:T(8,128)} %pad.9.small, f32[8,768]{1,0:T(8,128)} %get-tuple-element.100.sums_col, ...), custom_call_target="tpu_custom_call" | custom-call | flops 20000000000 | bytes 10000000 | tf_op jit(solution)/shard_map/row_input/pallas_call | solution.py:739
  194.3 2.1 collective-permute-done.6.refs_7_
  196.4 5.4 %reduce-scatter.3.cloned.1.call-done = bf16[1,16,48,768]{3,2,1,0:T(8,128)(2,1)} async-done(((bf16[8,16,48,768]{3,2,1,0:T(8,128)(2,1)}), bf16[1,16,48,768]{3,2,1,0:T(8,128)(2,1)}) %reduce-scatter.3.cloned.1.call-update) | async-done | bytes 1179664 | tf_op jit(solution)/shard_map/reduce_scatter | solution.py:938
  201.8 8.1 %row_weights.1 = (bf16[4,4,4,24,768]{4,3,2,1,0:T(8,128)(2,1)}, bf16[4,4,4,24,768]{4,3,2,1,0:T(8,128)(2,1)}) custom-call(s32[4]{0:T(128)} %pad_add_fusion.ints, f32[512,768]{1,0:T(8,128)} %get-tuple-element.99.grad_in, bf16[10,512,768]{2,1,0:T(8,128)(2,1)} %get-tuple-element.97.saved, bf16[3,512,768]{2,1,0:T(8,128)(2,1)} %row_heads.1.grads_in), custom_call_target="tpu_custom_call" | custom-call | flops 1000000 | bytes 100000 | tf_op jit(solution)/shard_map/row_weights/pallas_call | solution.py:719
  211.2 4.0 %split_shares.5 = (bf16[4,4,16,896]{3,2,1,0:T(8,128)(2,1)}, bf16[4,4,16,896]{3,2,1,0:T(8,128)(2,1)}, bf16[4,4,16,896]{3,2,1,0:T(8,128)(2,1)}, bf16[4,4,16,896]{3,2,1,0:T(8,128)(2,1)}) custom-call(s32[1]{0:T(128)} %bitcast.32.place, bf16[4,4,4,16,896]{4,3,2,1,0:T(8,128)(2,1)} %get-tuple-element.120.refs_0_, bf16[4,4,4,16,896]{4,3,2,1,0:T(8,128)(2,1)} %copy-done), custom_call_target="tpu_custom_call" | custom-call | flops 1000000 | bytes 1000000 | tf_op jit(solution)/shard_map/split_shares/pallas_call | solution.py:777
  215.3 4.4 %split_shares.6 = (bf16[4,4,24,768]{3,2,1,0:T(8,128)(2,1)}, bf16[4,4,24,768]{3,2,1,0:T(8,128)(2,1)}, bf16[4,4,24,768]{3,2,1,0:T(8,128)(2,1)}, bf16[4,4,24,768]{3,2,1,0:T(8,128)(2,1)}) custom-call(s32[1]{0:T(128)} %bitcast.29.place, bf16[4,4,4,24,768]{4,3,2,1,0:T(8,128)(2,1)} %get-tuple-element.119.refs_0_, ...), custom_call_target="tpu_custom_call" | custom-call | flops 1000000 | bytes 1000000 | tf_op jit(solution)/shard_map/split_shares/pallas_call | solution.py:777
  220.2 2.4 collective-permute-start.10
  223.1 1.9 collective-permute-start.16
  224.9 11.2 %collective-permute-done.9.refs_1_ = bf16[4,4,24,768]{3,2,1,0:T(8,128)(2,1)S(1)} collective-permute-done((bf16[4,4,24,768]{3,2,1,0:T(8,128)(2,1)}, bf16[4,4,24,768]{3,2,1,0:T(8,128)(2,1)S(1)}, u32[]{:S(2)}, u32[]{:S(2)}) %collective-permute-start.9) | collective-permute-done | bytes 589856 | tf_op jit(solution)/shard_map/ppermute | solution.py:959
  236.2 2.7 collective-permute-start.17
  238.9 5.0 %collective-permute-done.11.refs_3_ = bf16[4,4,24,768]{3,2,1,0:T(8,128)(2,1)S(1)} collective-permute-done((bf16[4,4,24,768]{3,2,1,0:T(8,128)(2,1)}, bf16[4,4,24,768]{3,2,1,0:T(8,128)(2,1)S(1)}, u32[]{:S(2)}, u32[]{:S(2)}) %collective-permute-start.11) | collective-permute-done | bytes 589856 | tf_op jit(solution)/shard_map/ppermute | solution.py:959
  244.7 4.3 %second_split.1 = (bf16[4,48,768]{2,1,0:T(8,128)(2,1)}, bf16[4,48,768]{2,1,0:T(8,128)(2,1)}, bf16[4,48,768]{2,1,0:T(8,128)(2,1)}, bf16[4,48,768]{2,1,0:T(8,128)(2,1)}) custom-call(s32[1]{0:T(128)} %bitcast.37.place, bf16[4,4,24,768]{3,2,1,0:T(8,128)(2,1)} %get-tuple-element.130.refs_0_, bf16[4,4,24,768]{3,2,1,0:T(8,128)(2,1)} %copy-done.4, ...), custom_call_target="tpu_custom_call" | custom-call | flops 1000000 | bytes 1000000 | tf_op jit(solution)/shard_map/second_split/pallas_call | solution.py:799
  250.6 2.9 collective-permute-start.13
  254.9 3.5 %split_shares.7 = (bf16[4,16,896]{2,1,0:T(8,128)(2,1)}, bf16[4,16,896]{2,1,0:T(8,128)(2,1)}, bf16[4,16,896]{2,1,0:T(8,128)(2,1)}, bf16[4,16,896]{2,1,0:T(8,128)(2,1)}) custom-call(s32[1]{0:T(128)} %bitcast.38.place, bf16[4,4,16,896]{3,2,1,0:T(8,128)(2,1)} %get-tuple-element.142.refs_0_, bf16[4,4,16,896]{3,2,1,0:T(8,128)(2,1)} %collective-permute-done.15.refs_1_, ...), custom_call_target="tpu_custom_call" | custom-call | flops 1000000 | bytes 1000000 | tf_op jit(solution)/shard_map/split_shares/pallas_call | solution.py:777
  260.3 3.1 %collective-permute-done.18.refs_5_ = bf16[4,16,896]{2,1,0:T(8,128)(2,1)S(1)} collective-permute-done((bf16[4,16,896]{2,1,0:T(8,128)(2,1)}, bf16[4,16,896]{2,1,0:T(8,128)(2,1)S(1)}, u32[]{:S(2)}, u32[]{:S(2)}) %collective-permute-start.18) | collective-permute-done | bytes 114720 | tf_op jit(solution)/shard_map/ppermute | solution.py:959
  264.0 2.4 collective-permute-done.19.refs_6_
  266.4 3.2 %collective-permute-done.20.refs_7_ = bf16[4,16,896]{2,1,0:T(8,128)(2,1)S(1)} collective-permute-done((bf16[4,16,896]{2,1,0:T(8,128)(2,1)}, bf16[4,16,896]{2,1,0:T(8,128)(2,1)S(1)}, u32[]{:S(2)}, u32[]{:S(2)}) %collective-permute-start.20) | collective-permute-done | bytes 114720 | tf_op jit(solution)/shard_map/ppermute | solution.py:959
  270.6 2.4 third_split.1
  273.1 2.2 collective-permute-start.21
  276.7 1.8 collective-permute-start.26
  278.6 2.8 collective-permute-start.22
  282.7 1.9 collective-permute-done.22.refs_2_
  286.7 2.0 last_split.1
  290.7 2.6 collective-permute-done.28.three
  (116 shorter events, 31.8 us)
Async XLA Ops:
  7.2 98.6 %all-gather.5.cloned.1.call-start = ((), (), s32[]{:S(2)}) async-start(), calls=%async_computation.4 | async-start | bytes 22192128 | tf_op jit(solution)/shard_map/all_gather | solution.py:972
  9.0 2.7 collective-permute-start.2
  9.1 4.0 %collective-permute-start.1 = (bf16[3,6,768]{2,1,0:T(8,128)(2,1)S(1)}, bf16[3,6,768]{2,1,0:T(8,128)(2,1)S(1)}, u32[]{:S(2)}, u32[]{:S(2)}) collective-permute-start(bf16[3,6,768]{2,1,0:T(8,128)(2,1)S(1)} %get-tuple-element.180), channel_id=1, source_target_pairs={{0,2},{1,3},{2,0},{3,1},{4,6},{5,7},{6,4},{7,5},{8,10},{9,11},{10,... | collective-permute-start | bytes 82952 | tf_op jit(solution)/shard_map/ppermute | solution.py:921
  10.6 3.4 %collective-permute-start = (bf16[3,6,768]{2,1,0:T(8,128)(2,1)S(1)}, bf16[3,6,768]{2,1,0:T(8,128)(2,1)S(1)}, u32[]{:S(2)}, u32[]{:S(2)}) collective-permute-start(bf16[3,6,768]{2,1,0:T(8,128)(2,1)S(1)} %get-tuple-element.181), channel_id=1, source_target_pairs={{0,3},{1,2},{2,1},{3,0},{4,7},{5,6},{6,5},{7,4},{8,11},{9,10},{10,... | collective-permute-start | bytes 82952 | tf_op jit(solution)/shard_map/ppermute | solution.py:921
  15.7 186.1 %reduce-scatter.3.cloned.1.call-start = ((), (), s32[]{:S(2)}) async-start(), calls=%async_computation.2 | async-start | bytes 10616832 | tf_op jit(solution)/shard_map/reduce_scatter | solution.py:938
  144.8 119.2 %reduce-scatter.5.cloned.1.call-start = ((), (), s32[]{:S(2)}) async-start(), calls=%async_computation.3 | async-start | bytes 1474560 | tf_op jit(solution)/shard_map/reduce_scatter | solution.py:1002
  165.5 8.1 %collective-permute-start.3 = (bf16[4,4,4,24,768]{4,3,2,1,0:T(8,128)(2,1)}, bf16[4,4,4,24,768]{4,3,2,1,0:T(8,128)(2,1)}, u32[]{:S(2)}, u32[]{:S(2)}) collective-permute-start(bf16[4,4,4,24,768]{4,3,2,1,0:T(8,128)(2,1)} %get-tuple-element.103), channel_id=1, source_target_pairs={{0,1},{1,0},{2,3},{3,2},{4,5},{5,4},{6,7},{7,6},{8,9},{9,8},{10,11... | collective-permute-start | bytes 7077896 | tf_op jit(solution)/shard_map/ppermute | solution.py:934
  178.0 16.3 %collective-permute-start.4 = (bf16[4,4,24,768]{3,2,1,0:T(8,128)(2,1)}, bf16[4,4,24,768]{3,2,1,0:T(8,128)(2,1)S(1)}, u32[]{:S(2)}, u32[]{:S(2)}) collective-permute-start(bf16[4,4,24,768]{3,2,1,0:T(8,128)(2,1)} %get-tuple-element.114), channel_id=1, source_target_pairs={{0,32},{1,9},{2,34},{3,11},{4,36},{5,13},{6,38},{7,15},{8,40},{9,1... | collective-permute-start | bytes 1769480 | tf_op jit(solution)/shard_map/ppermute | solution.py:959
  178.5 15.8 %collective-permute-start.5 = (bf16[4,4,24,768]{3,2,1,0:T(8,128)(2,1)}, bf16[4,4,24,768]{3,2,1,0:T(8,128)(2,1)S(1)}, u32[]{:S(2)}, u32[]{:S(2)}) collective-permute-start(bf16[4,4,24,768]{3,2,1,0:T(8,128)(2,1)} %get-tuple-element.115), channel_id=1, source_target_pairs={{0,64},{1,17},{2,66},{3,19},{4,68},{5,21},{6,70},{7,23},{8,72},{9,... | collective-permute-start | bytes 1769480 | tf_op jit(solution)/shard_map/ppermute | solution.py:959
  180.9 15.5 %collective-permute-start.6 = (bf16[4,4,24,768]{3,2,1,0:T(8,128)(2,1)}, bf16[4,4,24,768]{3,2,1,0:T(8,128)(2,1)S(1)}, u32[]{:S(2)}, u32[]{:S(2)}) collective-permute-start(bf16[4,4,24,768]{3,2,1,0:T(8,128)(2,1)} %get-tuple-element.116), channel_id=1, source_target_pairs={{0,96},{1,25},{2,98},{3,27},{4,100},{5,29},{6,102},{7,31},{8,104},... | collective-permute-start | bytes 1769480 | tf_op jit(solution)/shard_map/ppermute | solution.py:959
  201.8 8.1 %collective-permute-start.7 = (bf16[4,4,4,16,896]{4,3,2,1,0:T(8,128)(2,1)}, bf16[4,4,4,16,896]{4,3,2,1,0:T(8,128)(2,1)S(1)}, u32[]{:S(2)}, u32[]{:S(2)}) collective-permute-start(bf16[4,4,4,16,896]{4,3,2,1,0:T(8,128)(2,1)} %get-tuple-element.122), channel_id=1, source_target_pairs={{0,1},{1,0},{2,3},{3,2},{4,5},{5,4},{6,7},{7,6},{8,9},{9,8},{10,11... | collective-permute-start | bytes 5505032 | tf_op jit(solution)/shard_map/ppermute | solution.py:934
  210.0 5.3 %collective-permute-start.8 = (bf16[4,4,4,24,768]{4,3,2,1,0:T(8,128)(2,1)}, bf16[4,4,4,24,768]{4,3,2,1,0:T(8,128)(2,1)}, u32[]{:S(2)}, u32[]{:S(2)}) collective-permute-start(bf16[4,4,4,24,768]{4,3,2,1,0:T(8,128)(2,1)} %get-tuple-element.128), channel_id=1, source_target_pairs={{0,1},{1,0},{2,3},{3,2},{4,5},{5,4},{6,7},{7,6},{8,9},{9,8},{10,11... | collective-permute-start | bytes 7077896 | tf_op jit(solution)/shard_map/ppermute | solution.py:934
  219.7 16.5 %collective-permute-start.9 = (bf16[4,4,24,768]{3,2,1,0:T(8,128)(2,1)}, bf16[4,4,24,768]{3,2,1,0:T(8,128)(2,1)S(1)}, u32[]{:S(2)}, u32[]{:S(2)}) collective-permute-start(bf16[4,4,24,768]{3,2,1,0:T(8,128)(2,1)} %get-tuple-element.131), channel_id=1, source_target_pairs={{0,32},{1,9},{2,34},{3,11},{4,36},{5,13},{6,38},{7,15},{8,40},{9,1... | collective-permute-start | bytes 1769480 | tf_op jit(solution)/shard_map/ppermute | solution.py:959
  220.2 18.7 %collective-permute-start.10 = (bf16[4,4,24,768]{3,2,1,0:T(8,128)(2,1)}, bf16[4,4,24,768]{3,2,1,0:T(8,128)(2,1)S(1)}, u32[]{:S(2)}, u32[]{:S(2)}) collective-permute-start(bf16[4,4,24,768]{3,2,1,0:T(8,128)(2,1)} %get-tuple-element.132), channel_id=1, source_target_pairs={{0,64},{1,17},{2,66},{3,19},{4,68},{5,21},{6,70},{7,23},{8,72},{9,... | collective-permute-start | bytes 1769480 | tf_op jit(solution)/shard_map/ppermute | solution.py:959
  222.6 21.3 %collective-permute-start.11 = (bf16[4,4,24,768]{3,2,1,0:T(8,128)(2,1)}, bf16[4,4,24,768]{3,2,1,0:T(8,128)(2,1)S(1)}, u32[]{:S(2)}, u32[]{:S(2)}) collective-permute-start(bf16[4,4,24,768]{3,2,1,0:T(8,128)(2,1)} %get-tuple-element.133), channel_id=1, source_target_pairs={{0,96},{1,25},{2,98},{3,27},{4,100},{5,29},{6,102},{7,31},{8,104},... | collective-permute-start | bytes 1769480 | tf_op jit(solution)/shard_map/ppermute | solution.py:959
  222.6 30.9 %collective-permute-start.15 = (bf16[4,4,16,896]{3,2,1,0:T(8,128)(2,1)}, bf16[4,4,16,896]{3,2,1,0:T(8,128)(2,1)}, u32[]{:S(2)}, u32[]{:S(2)}) collective-permute-start(bf16[4,4,16,896]{3,2,1,0:T(8,128)(2,1)} %get-tuple-element.143), channel_id=1, source_target_pairs={{0,2},{1,3},{2,4},{3,5},{4,6},{5,7},{6,0},{7,1},{8,10},{9,11},{10,... | collective-permute-start | bytes 1376264 | tf_op jit(solution)/shard_map/ppermute | solution.py:959
  223.1 31.8 %collective-permute-start.16 = (bf16[4,4,16,896]{3,2,1,0:T(8,128)(2,1)}, bf16[4,4,16,896]{3,2,1,0:T(8,128)(2,1)}, u32[]{:S(2)}, u32[]{:S(2)}) collective-permute-start(bf16[4,4,16,896]{3,2,1,0:T(8,128)(2,1)} %get-tuple-element.144), channel_id=1, source_target_pairs={{0,4},{1,5},{2,6},{3,7},{4,0},{5,1},{6,2},{7,3},{8,12},{9,13},{10,... | collective-permute-start | bytes 1376264 | tf_op jit(solution)/shard_map/ppermute | solution.py:959
  236.2 18.7 %collective-permute-start.17 = (bf16[4,4,16,896]{3,2,1,0:T(8,128)(2,1)}, bf16[4,4,16,896]{3,2,1,0:T(8,128)(2,1)}, u32[]{:S(2)}, u32[]{:S(2)}) collective-permute-start(bf16[4,4,16,896]{3,2,1,0:T(8,128)(2,1)} %get-tuple-element.145), channel_id=1, source_target_pairs={{0,6},{1,7},{2,0},{3,1},{4,2},{5,3},{6,4},{7,5},{8,14},{9,15},{10,... | collective-permute-start | bytes 1376264 | tf_op jit(solution)/shard_map/ppermute | solution.py:959
  249.0 20.7 %collective-permute-start.12 = (bf16[4,48,768]{2,1,0:T(8,128)(2,1)}, bf16[4,48,768]{2,1,0:T(8,128)(2,1)S(1)}, u32[]{:S(2)}, u32[]{:S(2)}) collective-permute-start(bf16[4,48,768]{2,1,0:T(8,128)(2,1)} %get-tuple-element.139), channel_id=1, source_target_pairs={{0,8},{1,33},{2,10},{3,35},{4,12},{5,37},{6,14},{7,39},{8,16},{9,4... | collective-permute-start | bytes 884744 | tf_op jit(solution)/shard_map/ppermute | solution.py:959
  250.6 19.0 %collective-permute-start.13 = (bf16[4,48,768]{2,1,0:T(8,128)(2,1)}, bf16[4,48,768]{2,1,0:T(8,128)(2,1)S(1)}, u32[]{:S(2)}, u32[]{:S(2)}) collective-permute-start(bf16[4,48,768]{2,1,0:T(8,128)(2,1)} %get-tuple-element.140), channel_id=1, source_target_pairs={{0,16},{1,65},{2,18},{3,67},{4,20},{5,69},{6,22},{7,71},{8,24},{9,... | collective-permute-start | bytes 884744 | tf_op jit(solution)/shard_map/ppermute | solution.py:959
  253.5 16.2 %collective-permute-start.14 = (bf16[4,48,768]{2,1,0:T(8,128)(2,1)}, bf16[4,48,768]{2,1,0:T(8,128)(2,1)S(1)}, u32[]{:S(2)}, u32[]{:S(2)}) collective-permute-start(bf16[4,48,768]{2,1,0:T(8,128)(2,1)} %get-tuple-element.141), channel_id=1, source_target_pairs={{0,24},{1,97},{2,26},{3,99},{4,28},{5,101},{6,30},{7,103},{8,0},{9... | collective-permute-start | bytes 884744 | tf_op jit(solution)/shard_map/ppermute | solution.py:959
  258.4 5.1 %collective-permute-start.18 = (bf16[4,16,896]{2,1,0:T(8,128)(2,1)}, bf16[4,16,896]{2,1,0:T(8,128)(2,1)S(1)}, u32[]{:S(2)}, u32[]{:S(2)}) collective-permute-start(bf16[4,16,896]{2,1,0:T(8,128)(2,1)} %get-tuple-element.147), channel_id=1, source_target_pairs={{0,32},{1,33},{2,34},{3,35},{4,36},{5,37},{6,38},{7,39},{8,40},{9,... | collective-permute-start | bytes 344072 | tf_op jit(solution)/shard_map/ppermute | solution.py:959
  259.9 6.5 %collective-permute-start.19 = (bf16[4,16,896]{2,1,0:T(8,128)(2,1)}, bf16[4,16,896]{2,1,0:T(8,128)(2,1)S(1)}, u32[]{:S(2)}, u32[]{:S(2)}) collective-permute-start(bf16[4,16,896]{2,1,0:T(8,128)(2,1)} %get-tuple-element.148), channel_id=1, source_target_pairs={{0,64},{1,65},{2,66},{3,67},{4,68},{5,69},{6,70},{7,71},{8,72},{9,... | collective-permute-start | bytes 344072 | tf_op jit(solution)/shard_map/ppermute | solution.py:959
  263.4 6.2 %collective-permute-start.20 = (bf16[4,16,896]{2,1,0:T(8,128)(2,1)}, bf16[4,16,896]{2,1,0:T(8,128)(2,1)S(1)}, u32[]{:S(2)}, u32[]{:S(2)}) collective-permute-start(bf16[4,16,896]{2,1,0:T(8,128)(2,1)} %get-tuple-element.149), channel_id=1, source_target_pairs={{0,96},{1,97},{2,98},{3,99},{4,100},{5,101},{6,102},{7,103},{8,104... | collective-permute-start | bytes 344072 | tf_op jit(solution)/shard_map/ppermute | solution.py:959
  273.1 8.3 %collective-permute-start.21 = (bf16[48,768]{1,0:T(8,128)(2,1)}, bf16[48,768]{1,0:T(8,128)(2,1)S(1)}, u32[]{:S(2)}, u32[]{:S(2)}) collective-permute-start(bf16[48,768]{1,0:T(8,128)(2,1)} %get-tuple-element.151), channel_id=1, source_target_pairs={{0,2},{1,3},{2,4},{3,5},{4,6},{5,7},{6,0},{7,1},{8,10},{9,11},{10,... | collective-permute-start | bytes 221192 | tf_op jit(solution)/shard_map/ppermute | solution.py:959
  275.2 10.7 %collective-permute-start.24 = (bf16[72,768]{1,0:T(8,128)(2,1)}, bf16[72,768]{1,0:T(8,128)(2,1)S(1)}, u32[]{:S(2)}, u32[]{:S(2)}) collective-permute-start(bf16[72,768]{1,0:T(8,128)(2,1)} %get-tuple-element.155), channel_id=1, source_target_pairs={{0,8},{1,9},{2,10},{3,11},{4,12},{5,13},{6,14},{7,15},{8,16},{9,17... | collective-permute-start | bytes 331784 | tf_op jit(solution)/shard_map/ppermute | solution.py:959
  275.9 10.1 %collective-permute-start.25 = (bf16[72,768]{1,0:T(8,128)(2,1)}, bf16[72,768]{1,0:T(8,128)(2,1)S(1)}, u32[]{:S(2)}, u32[]{:S(2)}) collective-permute-start(bf16[72,768]{1,0:T(8,128)(2,1)} %get-tuple-element.156), channel_id=1, source_target_pairs={{0,16},{1,17},{2,18},{3,19},{4,20},{5,21},{6,22},{7,23},{8,24},{9,... | collective-permute-start | bytes 331784 | tf_op jit(solution)/shard_map/ppermute | solution.py:959
  276.7 9.2 %collective-permute-start.26 = (bf16[72,768]{1,0:T(8,128)(2,1)}, bf16[72,768]{1,0:T(8,128)(2,1)S(1)}, u32[]{:S(2)}, u32[]{:S(2)}) collective-permute-start(bf16[72,768]{1,0:T(8,128)(2,1)} %get-tuple-element.157), channel_id=1, source_target_pairs={{0,24},{1,25},{2,26},{3,27},{4,28},{5,29},{6,30},{7,31},{8,0},{9,1... | collective-permute-start | bytes 331784 | tf_op jit(solution)/shard_map/ppermute | solution.py:959
  278.6 6.1 %collective-permute-start.22 = (bf16[48,768]{1,0:T(8,128)(2,1)}, bf16[48,768]{1,0:T(8,128)(2,1)S(1)}, u32[]{:S(2)}, u32[]{:S(2)}) collective-permute-start(bf16[48,768]{1,0:T(8,128)(2,1)} %get-tuple-element.152), channel_id=1, source_target_pairs={{0,4},{1,5},{2,6},{3,7},{4,0},{5,1},{6,2},{7,3},{8,12},{9,13},{10,... | collective-permute-start | bytes 221192 | tf_op jit(solution)/shard_map/ppermute | solution.py:959
  281.4 4.6 %collective-permute-start.23 = (bf16[48,768]{1,0:T(8,128)(2,1)}, bf16[48,768]{1,0:T(8,128)(2,1)S(1)}, u32[]{:S(2)}, u32[]{:S(2)}) collective-permute-start(bf16[48,768]{1,0:T(8,128)(2,1)} %get-tuple-element.153), channel_id=1, source_target_pairs={{0,6},{1,7},{2,0},{3,1},{4,2},{5,3},{6,4},{7,5},{8,14},{9,15},{10,... | collective-permute-start | bytes 221192 | tf_op jit(solution)/shard_map/ppermute | solution.py:959
  288.8 4.5 %collective-permute-start.28 = (bf16[3,6,768]{2,1,0:T(8,128)(2,1)}, bf16[3,6,768]{2,1,0:T(8,128)(2,1)S(1)}, u32[]{:S(2)}, u32[]{:S(2)}) collective-permute-start(bf16[3,6,768]{2,1,0:T(8,128)(2,1)} %get-tuple-element.162), channel_id=1, source_target_pairs={{0,2},{1,3},{2,0},{3,1},{4,6},{5,7},{6,4},{7,5},{8,10},{9,11},{10,... | collective-permute-start | bytes 82952 | tf_op jit(solution)/shard_map/ppermute | solution.py:921
  289.2 4.1 %collective-permute-start.29 = (bf16[3,6,768]{2,1,0:T(8,128)(2,1)}, bf16[3,6,768]{2,1,0:T(8,128)(2,1)S(1)}, u32[]{:S(2)}, u32[]{:S(2)}) collective-permute-start(bf16[3,6,768]{2,1,0:T(8,128)(2,1)} %get-tuple-element.163), channel_id=1, source_target_pairs={{0,3},{1,2},{2,1},{3,0},{4,7},{5,6},{6,5},{7,4},{8,11},{9,10},{10,... | collective-permute-start | bytes 82952 | tf_op jit(solution)/shard_map/ppermute | solution.py:921
  (23 other events, 62.4 us)
Sparse Core Ops, SparseCore 0:
  15.8 89.9 all-gather.4
  144.9 56.8 reduce-scatter.2
  210.8 30.0 reduce-scatter.4

commit v4 on v3

--- a/solution.py
+++ b/solution.py
@@ -459,7 +459,7 @@
         shares.send(grads, member)
 
 
-def input_grads(loads, grad_in, gain, act, weights, hidden, da, grad_out, sums, lines=None):
+def input_grads(loads, grad_in, gain, act, weights, hidden, da, grad_out, sums, lines=None, loaded=None):
     for i in range(3):
         for copy in loads["inputs"][i]:
             copy.wait()
@@ -469,6 +469,8 @@
             value = dot_nt(act[i, rows, :], whole(weights, i))
             da[rows, :] = value if i == 0 else da[rows, :] + value
 
+        if i == 2 and loaded is not None:
+            loaded()
         loop(2, input_back)
     loads["hidden"].wait()
 
@@ -569,9 +571,15 @@
         )
     loads["hidden"] = copies.start(hidden_saved.at[0], hidden)
     zeros[...] = jnp.zeros_like(zeros)
-    fills = [copies.start(zeros, out.at[:, :, :, :, 0:D]) for out in (own, other)]
+    fills = []
+
+    def fill():
+        fills.extend(copies.start(zeros, out.at[:, :, :, :, 0:D]) for out in (own, other))
+
     gain = small[GAIN : GAIN + 1, :]
-    col_lines = input_grads(loads, grad_in, gain, act, weights, hidden, da, grad_out, sums, lines)
+    col_lines = input_grads(
+        loads, grad_in, gain, act, weights, hidden, da, grad_out, sums, lines, fill
+    )
     packed = small_lines(sums, sums_col, sums_ffn).astype(F32).reshape(4, 4, 4, 2, 1, 128)
     owned_lines[...] = jnp.broadcast_to(packed, owned_lines.shape).astype(BF16)
     for copy in fills:
@@ -808,11 +816,11 @@
     )(place, *row, *col)
 
 
-def third_kernel(place, ffn, *refs):
+def third_kernel(place, table_place, ffn, *refs):
     rows, table, pieces = refs[:4], refs[4:8], refs[8:]
     for hop in range(4):
         pieces[hop][...] = sum_of(rows, (place[0] + hop) & 3).astype(BF16)
-        to = (place[1] + hop) & 3
+        to = (table_place[0] + hop) & 3
         value = sum_of(table, to).astype(BF16)
         pieces[4 + hop][0:16, :] = value[:, 0:D]
         pieces[4 + hop][16:24, :] = jnp.zeros((8, D), BF16)
@@ -820,16 +828,16 @@
         pieces[4 + hop][SLAB : 3 * SLAB, :] = ffn[to]
 
 
-def third_split(rows, table, ffn, place):
+def third_split(rows, table, ffn, place, table_place):
     return pl.pallas_call(
         third_kernel,
         name="third_split",
-        in_specs=[SMEM] + [VMEM] * 9,
+        in_specs=[SMEM] * 2 + [VMEM] * 9,
         out_shape=(SHAPE((2 * SLAB, D), BF16),) * 4 + (SHAPE((3 * SLAB, D), BF16),) * 4,
         out_specs=(VMEM,) * 8,
         compiler_params=params(),
         cost_estimate=cost(10**6, 10**6),
-    )(place, ffn, *rows, *table)
+    )(place, table_place, ffn, *rows, *table)
 
 
 def last_kernel(me, *refs):
@@ -997,8 +1005,8 @@
         ints, g1, small, col_sums, ffn_sums, gathered, hidden, row_heads
     )
     own, other = row_weights_call(ints, g1, saved, row_heads)
-    table_other, col, ffn = barrier((table_other, col, ffn))
-    other, table_other = barrier((other, swap(table_other)))
+    table_other, col = barrier((table_other, col))
+    other, table_other, ffn = barrier((other, swap(table_other), ffn))
     ffn = lax.psum_scatter(ffn.reshape(4, 4, 2 * SLAB, D), "y", scatter_dimension=0, tiled=False)
     y_place, z_place = place_on(TABLE_STAGES[1]), place_on(TABLE_STAGES[2])
     table, other = barrier((split((table_own, table_other), places[2]), swap(other)))
@@ -1006,7 +1014,7 @@
     row = deliver(split((own, other), places[0]), STAGES[0])
     table = deliver(split(table, y_place), TABLE_STAGES[1])
     rows = deliver(second_split(row, col, places[1]), STAGES[1])
-    pieces = third_split(rows, table, ffn, jnp.concatenate([places[2], z_place]))
+    pieces = third_split(rows, table, ffn, places[2], z_place)
     rows, rest = deliver(pieces[:4], STAGES[2]), deliver(pieces[4:], TABLE_STAGES[2])
     return (act.reshape(tokens.shape), g0.reshape(tokens.shape)) + owned(rows, rest)
 

time: 306 us -> 302 us (0.987)
  waiting for transfers between devices: 91.6 us -> 86 us
    reduce_scatter x1, waiting for transfers between devices: 5.38 us -> 0.02 us  [scatter_chip_rows(): lax.psum_scatter(shares, ('x', 'c'), scatter_dimension=0, tiled=False)]
  transfers between devices with their start and end apart: 33 -> 33, of which waited for: 13 -> 12; matrix products, arithmetic and copies ran while one was open for 2% -> 2% of each run, Pallas kernels for 23% -> 23%
where the time goes in v4:
time: 302 us; the launch traced here: 298 us
  Pallas kernels  114 us (38%)
  waiting for transfers between devices  86 us (28%)
  starting transfers between devices  35.9 us (12%)
  blocking collectives  31.4 us (10%)
  between operations  16 us (5%)
  local copies, waits for them, and re-layouts  9.87 us (3%)
  other arithmetic  4.58 us (2%)
    all_gather x1, waiting for transfers between devices, gather(): gathered = lax.all_gather(packed, AXES, axis=0, tiled=False)  50.8 us
    pallas_call x1, Pallas kernels, forward_call(): pl.pallas_call(forward_kernel, name='forward', in_specs=[SMEM, VMEM, VMEM...  39 us
    all_gather x1, blocking collectives, gather(): lines = lax.all_gather(line, AXES, axis=0, tiled=False).astype(F32)  31.4 us
    ppermute x21, starting transfers between devices, deliver(): came.append(lax.ppermute(pieces[hop], AXES, pairs))  30.7 us
    ppermute x21, waiting for transfers between devices, deliver(): came.append(lax.ppermute(pieces[hop], AXES, pairs))  30.1 us
    pallas_call x1, Pallas kernels, column_call(): pl.pallas_call(column_kernel, name='column_back', in_specs=[SMEM, VMEM, V...  20.5 us
    pallas_call x4, Pallas kernels, split(): pl.pallas_call(split_kernel, name='split_shares', grid=(4,), in_specs=[SM...  16.4 us
    pallas_call x1, Pallas kernels, row_input_call(): pl.pallas_call(row_input_kernel, name='row_input', in_specs=[SMEM, VMEM,...  12.2 us
  transfers between devices with their start and end apart: 33, of which 12 were waited for; matrix products, arithmetic and copies ran while one was open for 2% of the time, Pallas kernels for 23%

profile of v4, /device:TPU:24, one launch (start us, length us, event | category | flops | bytes accessed | tf_op | source)
XLA Modules:
  0.0 298.1 jit_solution(7338389987435407446)
XLA Ops:
  17.7 2.2 concatenate.19
  20.7 31.4 %all-gather.2 = bf16[128,1,128]{2,1,0:T(2,128)(2,1)S(1)} all-gather(bf16[1,1,128]{2,1,0:T(2,128)(2,1)S(1)} %fusion.1), channel_id=2, replica_groups=mesh['y'=4,'z'=4,'x'=4,'c'=2] {'y','z','x','c'}, dimensions={0}, use_global_device_ids=true | all-gather | bytes 33024 | tf_op jit(solution)/shard_map/all_gather | solution.py:983
  55.0 50.8 %all-gather.5.cloned.1.call-done = bf16[14336,768]{1,0:T(8,128)(2,1)} async-done(((bf16[112,768]{1,0:T(8,128)(2,1)}), bf16[14336,768]{1,0:T(8,128)(2,1)}) %all-gather.5.cloned.1.call-update) | async-done | bytes 22020112 | tf_op jit(solution)/shard_map/all_gather | solution.py:980
  105.8 39.0 %forward.1 = (bf16[512,768]{1,0:T(8,128)(2,1)}, f32[512,768]{1,0:T(8,128)}, bf16[10,512,768]{2,1,0:T(8,128)(2,1)}, f32[2,512,768]{2,1,0:T(8,128)}, bf16[8,16,48,768]{3,2,1,0:T(8,128)(2,1)}, /*index=5*/f32[8,768]{1,0:T(8,128)}) custom-call(s32[4]{0:T(128)} %pad_add_fusion.ints, bf16[512,768]{1,0:T(8,128)(2,1)} %bitcast.84, bf16[512,768]{1,0:T(8,128)(2,1)} %bitcast.85, ...), custom_call_target="tpu_custom_call" | custom-call | flops 24000000000 | bytes 50000000 | tf_op jit(solution)/shard_map/forward/pallas_call | solution.py:646
  145.0 20.5 %column_back.1 = (f32[512,768]{1,0:T(8,128)}, bf16[4,4,4,24,768]{4,3,2,1,0:T(8,128)(2,1)}, bf16[4,4,4,24,768]{4,3,2,1,0:T(8,128)(2,1)}, f32[8,768]{1,0:T(8,128)}) custom-call(s32[4]{0:T(128)} %pad_add_fusion.ints, f32[512,768]{1,0:T(8,128)} %get-tuple-element.96.grad_in, f32[16,768]{1,0:T(8,128)} %pad.9.small, bf16[32,4,112,768]{3,2,1,0:T(8,128)(2,1)} %bitcast.81, ...), custom_call_target="tpu_custom_call" | custom-call | flops 10000000000 | bytes 10000000 | tf_op jit(solution)/shard_map/column_back/pallas_call | solution.py:704
  165.9 7.7 %row_heads.1.grads_in = bf16[3,512,768]{2,1,0:T(8,128)(2,1)} custom-call(s32[4]{0:T(128)} %pad_add_fusion.ints, f32[512,768]{1,0:T(8,128)} %get-tuple-element.99.grad_in, bf16[32,4,112,768]{3,2,1,0:T(8,128)(2,1)} %bitcast.82, bf16[10,512,768]{2,1,0:T(8,128)(2,1)} %get-tuple-element.97.saved), custom_call_target="tpu_custom_call" | custom-call | flops 10000000000 | bytes 10000000 | tf_op jit(solution)/shard_map/row_heads/pallas_call | solution.py:680
  173.6 4.4 %split_shares.4 = (bf16[4,4,24,768]{3,2,1,0:T(8,128)(2,1)}, bf16[4,4,24,768]{3,2,1,0:T(8,128)(2,1)}, bf16[4,4,24,768]{3,2,1,0:T(8,128)(2,1)}, bf16[4,4,24,768]{3,2,1,0:T(8,128)(2,1)}) custom-call(s32[1]{0:T(128)} %bitcast.29.place, bf16[4,4,4,24,768]{4,3,2,1,0:T(8,128)(2,1)} %get-tuple-element.102.refs_0_, ...), custom_call_target="tpu_custom_call" | custom-call | flops 1000000 | bytes 1000000 | tf_op jit(solution)/shard_map/split_shares/pallas_call | solution.py:785
  178.5 2.4 collective-permute-start.5
  180.9 12.2 %row_input.1 = (f32[512,768]{1,0:T(8,128)}, bf16[4,4,4,16,896]{4,3,2,1,0:T(8,128)(2,1)}, bf16[4,4,4,16,896]{4,3,2,1,0:T(8,128)(2,1)}) custom-call(s32[4]{0:T(128)} %pad_add_fusion.ints, f32[512,768]{1,0:T(8,128)} %get-tuple-element.99.grad_in, f32[16,768]{1,0:T(8,128)} %pad.9.small, f32[8,768]{1,0:T(8,128)} %get-tuple-element.100.sums_col, ...), custom_call_target="tpu_custom_call" | custom-call | flops 20000000000 | bytes 10000000 | tf_op jit(solution)/shard_map/row_input/pallas_call | solution.py:747
  193.2 3.2 %collective-permute-done.6.refs_7_ = bf16[4,4,24,768]{3,2,1,0:T(8,128)(2,1)S(1)} collective-permute-done((bf16[4,4,24,768]{3,2,1,0:T(8,128)(2,1)}, bf16[4,4,24,768]{3,2,1,0:T(8,128)(2,1)S(1)}, u32[]{:S(2)}, u32[]{:S(2)}) %collective-permute-start.6) | collective-permute-done | bytes 589856 | tf_op jit(solution)/shard_map/ppermute | solution.py:967
  197.2 8.2 %row_weights.1 = (bf16[4,4,4,24,768]{4,3,2,1,0:T(8,128)(2,1)}, bf16[4,4,4,24,768]{4,3,2,1,0:T(8,128)(2,1)}) custom-call(s32[4]{0:T(128)} %pad_add_fusion.ints, f32[512,768]{1,0:T(8,128)} %get-tuple-element.99.grad_in, bf16[10,512,768]{2,1,0:T(8,128)(2,1)} %get-tuple-element.97.saved, bf16[3,512,768]{2,1,0:T(8,128)(2,1)} %row_heads.1.grads_in), custom_call_target="tpu_custom_call" | custom-call | flops 1000000 | bytes 100000 | tf_op jit(solution)/shard_map/row_weights/pallas_call | solution.py:727
  206.8 4.0 %split_shares.5 = (bf16[4,4,16,896]{3,2,1,0:T(8,128)(2,1)}, bf16[4,4,16,896]{3,2,1,0:T(8,128)(2,1)}, bf16[4,4,16,896]{3,2,1,0:T(8,128)(2,1)}, bf16[4,4,16,896]{3,2,1,0:T(8,128)(2,1)}) custom-call(s32[1]{0:T(128)} %bitcast.32.place, bf16[4,4,4,16,896]{4,3,2,1,0:T(8,128)(2,1)} %get-tuple-element.122.refs_0_, bf16[4,4,4,16,896]{4,3,2,1,0:T(8,128)(2,1)} %copy-done), custom_call_target="tpu_custom_call" | custom-call | flops 1000000 | bytes 1000000 | tf_op jit(solution)/shard_map/split_shares/pallas_call | solution.py:785
  210.8 4.4 %split_shares.6 = (bf16[4,4,24,768]{3,2,1,0:T(8,128)(2,1)}, bf16[4,4,24,768]{3,2,1,0:T(8,128)(2,1)}, bf16[4,4,24,768]{3,2,1,0:T(8,128)(2,1)}, bf16[4,4,24,768]{3,2,1,0:T(8,128)(2,1)}) custom-call(s32[1]{0:T(128)} %bitcast.29.place, bf16[4,4,4,24,768]{4,3,2,1,0:T(8,128)(2,1)} %get-tuple-element.121.refs_0_, ...), custom_call_target="tpu_custom_call" | custom-call | flops 1000000 | bytes 1000000 | tf_op jit(solution)/shard_map/split_shares/pallas_call | solution.py:785
  216.7 1.6 collective-permute-start.10
  220.2 2.7 collective-permute-start.16
  222.9 9.5 %collective-permute-done.9.refs_1_ = bf16[4,4,24,768]{3,2,1,0:T(8,128)(2,1)S(1)} collective-permute-done((bf16[4,4,24,768]{3,2,1,0:T(8,128)(2,1)}, bf16[4,4,24,768]{3,2,1,0:T(8,128)(2,1)S(1)}, u32[]{:S(2)}, u32[]{:S(2)}) %collective-permute-start.9) | collective-permute-done | bytes 589856 | tf_op jit(solution)/shard_map/ppermute | solution.py:967
  232.4 2.7 collective-permute-start.17
  235.1 5.0 %collective-permute-done.11.refs_3_ = bf16[4,4,24,768]{3,2,1,0:T(8,128)(2,1)S(1)} collective-permute-done((bf16[4,4,24,768]{3,2,1,0:T(8,128)(2,1)}, bf16[4,4,24,768]{3,2,1,0:T(8,128)(2,1)S(1)}, u32[]{:S(2)}, u32[]{:S(2)}) %collective-permute-start.11) | collective-permute-done | bytes 589856 | tf_op jit(solution)/shard_map/ppermute | solution.py:967
  240.9 4.3 %second_split.1 = (bf16[4,48,768]{2,1,0:T(8,128)(2,1)}, bf16[4,48,768]{2,1,0:T(8,128)(2,1)}, bf16[4,48,768]{2,1,0:T(8,128)(2,1)}, bf16[4,48,768]{2,1,0:T(8,128)(2,1)}) custom-call(s32[1]{0:T(128)} %bitcast.37.place, bf16[4,4,24,768]{3,2,1,0:T(8,128)(2,1)} %get-tuple-element.130.refs_0_, bf16[4,4,24,768]{3,2,1,0:T(8,128)(2,1)} %copy-done.4, ...), custom_call_target="tpu_custom_call" | custom-call | flops 1000000 | bytes 1000000 | tf_op jit(solution)/shard_map/second_split/pallas_call | solution.py:807
  245.2 1.6 collective-permute-start.12
  246.8 2.9 collective-permute-start.13
  251.0 3.5 %split_shares.7 = (bf16[4,16,896]{2,1,0:T(8,128)(2,1)}, bf16[4,16,896]{2,1,0:T(8,128)(2,1)}, bf16[4,16,896]{2,1,0:T(8,128)(2,1)}, bf16[4,16,896]{2,1,0:T(8,128)(2,1)}) custom-call(s32[1]{0:T(128)} %bitcast.38.place, bf16[4,4,16,896]{3,2,1,0:T(8,128)(2,1)} %get-tuple-element.142.refs_0_, bf16[4,4,16,896]{3,2,1,0:T(8,128)(2,1)} %collective-permute-done.15.refs_1_, ...), custom_call_target="tpu_custom_call" | custom-call | flops 1000000 | bytes 1000000 | tf_op jit(solution)/shard_map/split_shares/pallas_call | solution.py:785
  256.5 3.1 %collective-permute-done.18.refs_5_ = bf16[4,16,896]{2,1,0:T(8,128)(2,1)S(1)} collective-permute-done((bf16[4,16,896]{2,1,0:T(8,128)(2,1)}, bf16[4,16,896]{2,1,0:T(8,128)(2,1)S(1)}, u32[]{:S(2)}, u32[]{:S(2)}) %collective-permute-start.18) | collective-permute-done | bytes 114720 | tf_op jit(solution)/shard_map/ppermute | solution.py:967
  259.6 3.0 %collective-permute-done.19.refs_6_ = bf16[4,16,896]{2,1,0:T(8,128)(2,1)S(1)} collective-permute-done((bf16[4,16,896]{2,1,0:T(8,128)(2,1)}, bf16[4,16,896]{2,1,0:T(8,128)(2,1)S(1)}, u32[]{:S(2)}, u32[]{:S(2)}) %collective-permute-start.19) | collective-permute-done | bytes 114720 | tf_op jit(solution)/shard_map/ppermute | solution.py:967
  262.6 3.2 %collective-permute-done.20.refs_7_ = bf16[4,16,896]{2,1,0:T(8,128)(2,1)S(1)} collective-permute-done((bf16[4,16,896]{2,1,0:T(8,128)(2,1)}, bf16[4,16,896]{2,1,0:T(8,128)(2,1)S(1)}, u32[]{:S(2)}, u32[]{:S(2)}) %collective-permute-start.20) | collective-permute-done | bytes 114720 | tf_op jit(solution)/shard_map/ppermute | solution.py:967
  266.8 2.4 third_split.1
  269.2 2.2 collective-permute-start.21
  272.9 1.8 collective-permute-start.26
  274.8 2.7 collective-permute-start.22
  278.9 1.9 collective-permute-done.22.refs_2_
  282.8 2.0 last_split.1
  286.7 2.6 collective-permute-done.28.three
  (115 shorter events, 32.8 us)
Async XLA Ops:
  7.2 98.6 %all-gather.5.cloned.1.call-start = ((), (), s32[]{:S(2)}) async-start(), calls=%async_computation.4 | async-start | bytes 22192128 | tf_op jit(solution)/shard_map/all_gather | solution.py:980
  9.0 2.7 collective-permute-start.2
  9.1 4.0 %collective-permute-start.1 = (bf16[3,6,768]{2,1,0:T(8,128)(2,1)S(1)}, bf16[3,6,768]{2,1,0:T(8,128)(2,1)S(1)}, u32[]{:S(2)}, u32[]{:S(2)}) collective-permute-start(bf16[3,6,768]{2,1,0:T(8,128)(2,1)S(1)} %get-tuple-element.180), channel_id=1, source_target_pairs={{0,2},{1,3},{2,0},{3,1},{4,6},{5,7},{6,4},{7,5},{8,10},{9,11},{10,... | collective-permute-start | bytes 82952 | tf_op jit(solution)/shard_map/ppermute | solution.py:929
  10.6 3.4 %collective-permute-start = (bf16[3,6,768]{2,1,0:T(8,128)(2,1)S(1)}, bf16[3,6,768]{2,1,0:T(8,128)(2,1)S(1)}, u32[]{:S(2)}, u32[]{:S(2)}) collective-permute-start(bf16[3,6,768]{2,1,0:T(8,128)(2,1)S(1)} %get-tuple-element.181), channel_id=1, source_target_pairs={{0,3},{1,2},{2,1},{3,0},{4,7},{5,6},{6,5},{7,4},{8,11},{9,10},{10,... | collective-permute-start | bytes 82952 | tf_op jit(solution)/shard_map/ppermute | solution.py:929
  15.7 189.8 %reduce-scatter.3.cloned.1.call-start = ((), (), s32[]{:S(2)}) async-start(), calls=%async_computation.2 | async-start | bytes 10616832 | tf_op jit(solution)/shard_map/reduce_scatter | solution.py:946
  144.8 114.8 %reduce-scatter.5.cloned.1.call-start = ((), (), s32[]{:S(2)}) async-start(), calls=%async_computation.3 | async-start | bytes 1474560 | tf_op jit(solution)/shard_map/reduce_scatter | solution.py:1010
  165.5 8.1 %collective-permute-start.3 = (bf16[4,4,4,24,768]{4,3,2,1,0:T(8,128)(2,1)}, bf16[4,4,4,24,768]{4,3,2,1,0:T(8,128)(2,1)}, u32[]{:S(2)}, u32[]{:S(2)}) collective-permute-start(bf16[4,4,4,24,768]{4,3,2,1,0:T(8,128)(2,1)} %get-tuple-element.103), channel_id=1, source_target_pairs={{0,1},{1,0},{2,3},{3,2},{4,5},{5,4},{6,7},{7,6},{8,9},{9,8},{10,11... | collective-permute-start | bytes 7077896 | tf_op jit(solution)/shard_map/ppermute | solution.py:942
  178.0 15.2 %collective-permute-start.4 = (bf16[4,4,24,768]{3,2,1,0:T(8,128)(2,1)}, bf16[4,4,24,768]{3,2,1,0:T(8,128)(2,1)S(1)}, u32[]{:S(2)}, u32[]{:S(2)}) collective-permute-start(bf16[4,4,24,768]{3,2,1,0:T(8,128)(2,1)} %get-tuple-element.115), channel_id=1, source_target_pairs={{0,32},{1,9},{2,34},{3,11},{4,36},{5,13},{6,38},{7,15},{8,40},{9,1... | collective-permute-start | bytes 1769480 | tf_op jit(solution)/shard_map/ppermute | solution.py:967
  178.5 14.7 %collective-permute-start.5 = (bf16[4,4,24,768]{3,2,1,0:T(8,128)(2,1)}, bf16[4,4,24,768]{3,2,1,0:T(8,128)(2,1)S(1)}, u32[]{:S(2)}, u32[]{:S(2)}) collective-permute-start(bf16[4,4,24,768]{3,2,1,0:T(8,128)(2,1)} %get-tuple-element.116), channel_id=1, source_target_pairs={{0,64},{1,17},{2,66},{3,19},{4,68},{5,21},{6,70},{7,23},{8,72},{9,... | collective-permute-start | bytes 1769480 | tf_op jit(solution)/shard_map/ppermute | solution.py:967
  180.9 15.5 %collective-permute-start.6 = (bf16[4,4,24,768]{3,2,1,0:T(8,128)(2,1)}, bf16[4,4,24,768]{3,2,1,0:T(8,128)(2,1)S(1)}, u32[]{:S(2)}, u32[]{:S(2)}) collective-permute-start(bf16[4,4,24,768]{3,2,1,0:T(8,128)(2,1)} %get-tuple-element.117), channel_id=1, source_target_pairs={{0,96},{1,25},{2,98},{3,27},{4,100},{5,29},{6,102},{7,31},{8,104},... | collective-permute-start | bytes 1769480 | tf_op jit(solution)/shard_map/ppermute | solution.py:967
  197.2 8.2 %collective-permute-start.7 = (bf16[4,4,4,16,896]{4,3,2,1,0:T(8,128)(2,1)}, bf16[4,4,4,16,896]{4,3,2,1,0:T(8,128)(2,1)S(1)}, u32[]{:S(2)}, u32[]{:S(2)}) collective-permute-start(bf16[4,4,4,16,896]{4,3,2,1,0:T(8,128)(2,1)} %get-tuple-element.118), channel_id=1, source_target_pairs={{0,1},{1,0},{2,3},{3,2},{4,5},{5,4},{6,7},{7,6},{8,9},{9,8},{10,11... | collective-permute-start | bytes 5505032 | tf_op jit(solution)/shard_map/ppermute | solution.py:942
  205.5 5.3 %collective-permute-start.8 = (bf16[4,4,4,24,768]{4,3,2,1,0:T(8,128)(2,1)}, bf16[4,4,4,24,768]{4,3,2,1,0:T(8,128)(2,1)}, u32[]{:S(2)}, u32[]{:S(2)}) collective-permute-start(bf16[4,4,4,24,768]{4,3,2,1,0:T(8,128)(2,1)} %get-tuple-element.128), channel_id=1, source_target_pairs={{0,1},{1,0},{2,3},{3,2},{4,5},{5,4},{6,7},{7,6},{8,9},{9,8},{10,11... | collective-permute-start | bytes 7077896 | tf_op jit(solution)/shard_map/ppermute | solution.py:942
  215.3 17.1 %collective-permute-start.9 = (bf16[4,4,24,768]{3,2,1,0:T(8,128)(2,1)}, bf16[4,4,24,768]{3,2,1,0:T(8,128)(2,1)S(1)}, u32[]{:S(2)}, u32[]{:S(2)}) collective-permute-start(bf16[4,4,24,768]{3,2,1,0:T(8,128)(2,1)} %get-tuple-element.131), channel_id=1, source_target_pairs={{0,32},{1,9},{2,34},{3,11},{4,36},{5,13},{6,38},{7,15},{8,40},{9,1... | collective-permute-start | bytes 1769480 | tf_op jit(solution)/shard_map/ppermute | solution.py:967
  216.7 18.3 %collective-permute-start.10 = (bf16[4,4,24,768]{3,2,1,0:T(8,128)(2,1)}, bf16[4,4,24,768]{3,2,1,0:T(8,128)(2,1)S(1)}, u32[]{:S(2)}, u32[]{:S(2)}) collective-permute-start(bf16[4,4,24,768]{3,2,1,0:T(8,128)(2,1)} %get-tuple-element.132), channel_id=1, source_target_pairs={{0,64},{1,17},{2,66},{3,19},{4,68},{5,21},{6,70},{7,23},{8,72},{9,... | collective-permute-start | bytes 1769480 | tf_op jit(solution)/shard_map/ppermute | solution.py:967
  218.3 21.7 %collective-permute-start.11 = (bf16[4,4,24,768]{3,2,1,0:T(8,128)(2,1)}, bf16[4,4,24,768]{3,2,1,0:T(8,128)(2,1)S(1)}, u32[]{:S(2)}, u32[]{:S(2)}) collective-permute-start(bf16[4,4,24,768]{3,2,1,0:T(8,128)(2,1)} %get-tuple-element.133), channel_id=1, source_target_pairs={{0,96},{1,25},{2,98},{3,27},{4,100},{5,29},{6,102},{7,31},{8,104},... | collective-permute-start | bytes 1769480 | tf_op jit(solution)/shard_map/ppermute | solution.py:967
  218.8 30.9 %collective-permute-start.15 = (bf16[4,4,16,896]{3,2,1,0:T(8,128)(2,1)}, bf16[4,4,16,896]{3,2,1,0:T(8,128)(2,1)}, u32[]{:S(2)}, u32[]{:S(2)}) collective-permute-start(bf16[4,4,16,896]{3,2,1,0:T(8,128)(2,1)} %get-tuple-element.143), channel_id=1, source_target_pairs={{0,2},{1,3},{2,4},{3,5},{4,6},{5,7},{6,0},{7,1},{8,10},{9,11},{10,... | collective-permute-start | bytes 1376264 | tf_op jit(solution)/shard_map/ppermute | solution.py:967
  220.2 30.8 %collective-permute-start.16 = (bf16[4,4,16,896]{3,2,1,0:T(8,128)(2,1)}, bf16[4,4,16,896]{3,2,1,0:T(8,128)(2,1)}, u32[]{:S(2)}, u32[]{:S(2)}) collective-permute-start(bf16[4,4,16,896]{3,2,1,0:T(8,128)(2,1)} %get-tuple-element.144), channel_id=1, source_target_pairs={{0,4},{1,5},{2,6},{3,7},{4,0},{5,1},{6,2},{7,3},{8,12},{9,13},{10,... | collective-permute-start | bytes 1376264 | tf_op jit(solution)/shard_map/ppermute | solution.py:967
  232.4 18.7 %collective-permute-start.17 = (bf16[4,4,16,896]{3,2,1,0:T(8,128)(2,1)}, bf16[4,4,16,896]{3,2,1,0:T(8,128)(2,1)}, u32[]{:S(2)}, u32[]{:S(2)}) collective-permute-start(bf16[4,4,16,896]{3,2,1,0:T(8,128)(2,1)} %get-tuple-element.145), channel_id=1, source_target_pairs={{0,6},{1,7},{2,0},{3,1},{4,2},{5,3},{6,4},{7,5},{8,14},{9,15},{10,... | collective-permute-start | bytes 1376264 | tf_op jit(solution)/shard_map/ppermute | solution.py:967
  245.2 20.6 %collective-permute-start.12 = (bf16[4,48,768]{2,1,0:T(8,128)(2,1)}, bf16[4,48,768]{2,1,0:T(8,128)(2,1)S(1)}, u32[]{:S(2)}, u32[]{:S(2)}) collective-permute-start(bf16[4,48,768]{2,1,0:T(8,128)(2,1)} %get-tuple-element.139), channel_id=1, source_target_pairs={{0,8},{1,33},{2,10},{3,35},{4,12},{5,37},{6,14},{7,39},{8,16},{9,4... | collective-permute-start | bytes 884744 | tf_op jit(solution)/shard_map/ppermute | solution.py:967
  246.8 19.0 %collective-permute-start.13 = (bf16[4,48,768]{2,1,0:T(8,128)(2,1)}, bf16[4,48,768]{2,1,0:T(8,128)(2,1)S(1)}, u32[]{:S(2)}, u32[]{:S(2)}) collective-permute-start(bf16[4,48,768]{2,1,0:T(8,128)(2,1)} %get-tuple-element.140), channel_id=1, source_target_pairs={{0,16},{1,65},{2,18},{3,67},{4,20},{5,69},{6,22},{7,71},{8,24},{9,... | collective-permute-start | bytes 884744 | tf_op jit(solution)/shard_map/ppermute | solution.py:967
  249.7 16.2 %collective-permute-start.14 = (bf16[4,48,768]{2,1,0:T(8,128)(2,1)}, bf16[4,48,768]{2,1,0:T(8,128)(2,1)S(1)}, u32[]{:S(2)}, u32[]{:S(2)}) collective-permute-start(bf16[4,48,768]{2,1,0:T(8,128)(2,1)} %get-tuple-element.141), channel_id=1, source_target_pairs={{0,24},{1,97},{2,26},{3,99},{4,28},{5,101},{6,30},{7,103},{8,0},{9... | collective-permute-start | bytes 884744 | tf_op jit(solution)/shard_map/ppermute | solution.py:967
  254.5 5.1 %collective-permute-start.18 = (bf16[4,16,896]{2,1,0:T(8,128)(2,1)}, bf16[4,16,896]{2,1,0:T(8,128)(2,1)S(1)}, u32[]{:S(2)}, u32[]{:S(2)}) collective-permute-start(bf16[4,16,896]{2,1,0:T(8,128)(2,1)} %get-tuple-element.147), channel_id=1, source_target_pairs={{0,32},{1,33},{2,34},{3,35},{4,36},{5,37},{6,38},{7,39},{8,40},{9,... | collective-permute-start | bytes 344072 | tf_op jit(solution)/shard_map/ppermute | solution.py:967
  256.1 6.5 %collective-permute-start.19 = (bf16[4,16,896]{2,1,0:T(8,128)(2,1)}, bf16[4,16,896]{2,1,0:T(8,128)(2,1)S(1)}, u32[]{:S(2)}, u32[]{:S(2)}) collective-permute-start(bf16[4,16,896]{2,1,0:T(8,128)(2,1)} %get-tuple-element.148), channel_id=1, source_target_pairs={{0,64},{1,65},{2,66},{3,67},{4,68},{5,69},{6,70},{7,71},{8,72},{9,... | collective-permute-start | bytes 344072 | tf_op jit(solution)/shard_map/ppermute | solution.py:967
  259.6 6.2 %collective-permute-start.20 = (bf16[4,16,896]{2,1,0:T(8,128)(2,1)}, bf16[4,16,896]{2,1,0:T(8,128)(2,1)S(1)}, u32[]{:S(2)}, u32[]{:S(2)}) collective-permute-start(bf16[4,16,896]{2,1,0:T(8,128)(2,1)} %get-tuple-element.149), channel_id=1, source_target_pairs={{0,96},{1,97},{2,98},{3,99},{4,100},{5,101},{6,102},{7,103},{8,104... | collective-permute-start | bytes 344072 | tf_op jit(solution)/shard_map/ppermute | solution.py:967
  269.2 8.2 %collective-permute-start.21 = (bf16[48,768]{1,0:T(8,128)(2,1)}, bf16[48,768]{1,0:T(8,128)(2,1)S(1)}, u32[]{:S(2)}, u32[]{:S(2)}) collective-permute-start(bf16[48,768]{1,0:T(8,128)(2,1)} %get-tuple-element.151), channel_id=1, source_target_pairs={{0,2},{1,3},{2,4},{3,5},{4,6},{5,7},{6,0},{7,1},{8,10},{9,11},{10,... | collective-permute-start | bytes 221192 | tf_op jit(solution)/shard_map/ppermute | solution.py:967
  271.4 10.6 %collective-permute-start.24 = (bf16[72,768]{1,0:T(8,128)(2,1)}, bf16[72,768]{1,0:T(8,128)(2,1)S(1)}, u32[]{:S(2)}, u32[]{:S(2)}) collective-permute-start(bf16[72,768]{1,0:T(8,128)(2,1)} %get-tuple-element.155), channel_id=1, source_target_pairs={{0,8},{1,9},{2,10},{3,11},{4,12},{5,13},{6,14},{7,15},{8,16},{9,17... | collective-permute-start | bytes 331784 | tf_op jit(solution)/shard_map/ppermute | solution.py:967
  272.1 9.9 %collective-permute-start.25 = (bf16[72,768]{1,0:T(8,128)(2,1)}, bf16[72,768]{1,0:T(8,128)(2,1)S(1)}, u32[]{:S(2)}, u32[]{:S(2)}) collective-permute-start(bf16[72,768]{1,0:T(8,128)(2,1)} %get-tuple-element.156), channel_id=1, source_target_pairs={{0,16},{1,17},{2,18},{3,19},{4,20},{5,21},{6,22},{7,23},{8,24},{9,... | collective-permute-start | bytes 331784 | tf_op jit(solution)/shard_map/ppermute | solution.py:967
  272.9 9.1 %collective-permute-start.26 = (bf16[72,768]{1,0:T(8,128)(2,1)}, bf16[72,768]{1,0:T(8,128)(2,1)S(1)}, u32[]{:S(2)}, u32[]{:S(2)}) collective-permute-start(bf16[72,768]{1,0:T(8,128)(2,1)} %get-tuple-element.157), channel_id=1, source_target_pairs={{0,24},{1,25},{2,26},{3,27},{4,28},{5,29},{6,30},{7,31},{8,0},{9,1... | collective-permute-start | bytes 331784 | tf_op jit(solution)/shard_map/ppermute | solution.py:967
  274.8 6.1 %collective-permute-start.22 = (bf16[48,768]{1,0:T(8,128)(2,1)}, bf16[48,768]{1,0:T(8,128)(2,1)S(1)}, u32[]{:S(2)}, u32[]{:S(2)}) collective-permute-start(bf16[48,768]{1,0:T(8,128)(2,1)} %get-tuple-element.152), channel_id=1, source_target_pairs={{0,4},{1,5},{2,6},{3,7},{4,0},{5,1},{6,2},{7,3},{8,12},{9,13},{10,... | collective-permute-start | bytes 221192 | tf_op jit(solution)/shard_map/ppermute | solution.py:967
  277.4 4.6 %collective-permute-start.23 = (bf16[48,768]{1,0:T(8,128)(2,1)}, bf16[48,768]{1,0:T(8,128)(2,1)S(1)}, u32[]{:S(2)}, u32[]{:S(2)}) collective-permute-start(bf16[48,768]{1,0:T(8,128)(2,1)} %get-tuple-element.153), channel_id=1, source_target_pairs={{0,6},{1,7},{2,0},{3,1},{4,2},{5,3},{6,4},{7,5},{8,14},{9,15},{10,... | collective-permute-start | bytes 221192 | tf_op jit(solution)/shard_map/ppermute | solution.py:967
  284.9 4.5 %collective-permute-start.28 = (bf16[3,6,768]{2,1,0:T(8,128)(2,1)}, bf16[3,6,768]{2,1,0:T(8,128)(2,1)S(1)}, u32[]{:S(2)}, u32[]{:S(2)}) collective-permute-start(bf16[3,6,768]{2,1,0:T(8,128)(2,1)} %get-tuple-element.162), channel_id=1, source_target_pairs={{0,2},{1,3},{2,0},{3,1},{4,6},{5,7},{6,4},{7,5},{8,10},{9,11},{10,... | collective-permute-start | bytes 82952 | tf_op jit(solution)/shard_map/ppermute | solution.py:929
  285.3 4.1 %collective-permute-start.29 = (bf16[3,6,768]{2,1,0:T(8,128)(2,1)}, bf16[3,6,768]{2,1,0:T(8,128)(2,1)S(1)}, u32[]{:S(2)}, u32[]{:S(2)}) collective-permute-start(bf16[3,6,768]{2,1,0:T(8,128)(2,1)} %get-tuple-element.163), channel_id=1, source_target_pairs={{0,3},{1,2},{2,1},{3,0},{4,7},{5,6},{6,5},{7,4},{8,11},{9,10},{10,... | collective-permute-start | bytes 82952 | tf_op jit(solution)/shard_map/ppermute | solution.py:929
  (23 other events, 49.2 us)
Sparse Core Ops, SparseCore 0:
  15.8 89.9 all-gather.4
  144.9 56.8 reduce-scatter.2
  206.3 30.8 reduce-scatter.4

commit v5 on v4

--- a/solution.py
+++ b/solution.py
@@ -633,8 +633,8 @@
 SHAPE = jax.ShapeDtypeStruct
 
 
-def params():
-    return pltpu.CompilerParams(vmem_limit_bytes=62 * 1024 * 1024)
+def params(mebibytes=62):
+    return pltpu.CompilerParams(vmem_limit_bytes=mebibytes * 1024 * 1024)
 
 
 def cost(flops, traffic):
@@ -776,21 +776,25 @@
 
 def split_kernel(place, *refs):
     for hop in range(4):
-        refs[-4 + hop][0] = sum_of(refs[:-4], (place[0] + hop) & 3, 0).astype(BF16)
+        to = (place[0] + hop) & 3
+        for j in range(refs[-1].shape[0]):
+            refs[-4 + hop][j] = sum_of(refs[:-4], to, j).astype(BF16)
 
 
 def split(inputs, place):
     shape = inputs[0].shape
     rest = (0,) * (len(shape) - 2)
+    large = len(shape) == 5
+    in_block = pl.BlockSpec((4, 1) + shape[2:], lambda j: (0, j) + rest) if large else VMEM
+    out_block = pl.BlockSpec((1,) + shape[2:], lambda j: (j,) + rest) if large else VMEM
     return pl.pallas_call(
         split_kernel,
         name="split_shares",
-        grid=(4,),
-        in_specs=[SMEM]
-        + [pl.BlockSpec((4, 1) + shape[2:], lambda j: (0, j) + rest)] * len(inputs),
+        grid=(4,) if large else (),
+        in_specs=[SMEM] + [in_block] * len(inputs),
         out_shape=(SHAPE(shape[1:], BF16),) * 4,
-        out_specs=(pl.BlockSpec((1,) + shape[2:], lambda j: (j,) + rest),) * 4,
-        compiler_params=params(),
+        out_specs=(out_block,) * 4,
+        compiler_params=params(62 if large else 6),
         cost_estimate=cost(10**6, 10**6),
     )(place, *inputs)
 
@@ -798,20 +802,23 @@
 def second_kernel(place, *refs):
     for hop in range(4):
         to = (place[0] + hop) & 3
-        for g in range(2):
-            value = sum_of(refs[4 * g : 4 * g + 4], to, 0)
-            refs[8 + hop][0, g * SLAB : (g + 1) * SLAB, :] = value.astype(BF16)
+
+        def body(j):
+            for g in range(2):
+                value = sum_of(refs[4 * g : 4 * g + 4], to, j)
+                refs[8 + hop][j, g * SLAB : (g + 1) * SLAB, :] = value.astype(BF16)
+
+        loop(4, body)
 
 
 def second_split(row, col, place):
     return pl.pallas_call(
         second_kernel,
         name="second_split",
-        grid=(4,),
-        in_specs=[SMEM] + [pl.BlockSpec((4, 1, SLAB, D), lambda j: (0, j, 0, 0))] * 8,
+        in_specs=[SMEM] + [VMEM] * 8,
         out_shape=(SHAPE((4, 2 * SLAB, D), BF16),) * 4,
-        out_specs=(pl.BlockSpec((1, 2 * SLAB, D), lambda j: (j, 0, 0)),) * 4,
-        compiler_params=params(),
+        out_specs=(VMEM,) * 4,
+        compiler_params=params(10),
         cost_estimate=cost(10**6, 10**6),
     )(place, *row, *col)
 
@@ -835,7 +842,7 @@
         in_specs=[SMEM] * 2 + [VMEM] * 9,
         out_shape=(SHAPE((2 * SLAB, D), BF16),) * 4 + (SHAPE((3 * SLAB, D), BF16),) * 4,
         out_specs=(VMEM,) * 8,
-        compiler_params=params(),
+        compiler_params=params(6),
         cost_estimate=cost(10**6, 10**6),
     )(place, table_place, ffn, *rows, *table)
 
@@ -880,7 +887,7 @@
         + (SHAPE((3, 6, D), BF16),) * 4,
         out_specs=(VMEM,) * 12,
         scratch_shapes=[pltpu.VMEM((MEMBERS, 3, 6, D), F32)],
-        compiler_params=params(),
+        compiler_params=params(6),
         cost_estimate=cost(10**6, 10**6),
     )(me, *rows, *rest)
 
@@ -909,7 +916,7 @@
         ),
         out_specs=(VMEM,) * 5,
         scratch_shapes=[pltpu.VMEM((MEMBERS, 3, 6, D), F32)],
-        compiler_params=params(),
+        compiler_params=params(6),
         cost_estimate=cost(10**6, 10**6),
     )(me, *pieces)
 

time: 302 us -> 292 us (0.967)
  Pallas kernels: 114 us -> 107 us
    pallas_call x5, Pallas kernels: 20.6 us -> 17.2 us  [the longest x4 14.5 us: split(): pl.pallas_call(split_kernel, name='split_shares', grid=(4,) if large else...]
  transfers between devices with their start and end apart: 33 -> 33, of which waited for: 12 -> 14; matrix products, arithmetic and copies ran while one was open for 2% -> 2% of each run, Pallas kernels for 23% -> 23%
where the time goes in v5:
time: 292 us; the launch traced here: 288 us
  Pallas kernels  107 us (37%)
  waiting for transfers between devices  85.2 us (29%)
  starting transfers between devices  36.2 us (12%)
  blocking collectives  31.4 us (11%)
  between operations  15.9 us (5%)
  local copies, waits for them, and re-layouts  8.45 us (3%)
  other arithmetic  4.58 us (2%)
    all_gather x1, waiting for transfers between devices, gather(): gathered = lax.all_gather(packed, AXES, axis=0, tiled=False)  50.8 us
    pallas_call x1, Pallas kernels, forward_call(): pl.pallas_call(forward_kernel, name='forward', in_specs=[SMEM, VMEM, VMEM...  39 us
    all_gather x1, blocking collectives, gather(): lines = lax.all_gather(line, AXES, axis=0, tiled=False).astype(F32)  31.4 us
    ppermute x21, starting transfers between devices, deliver(): came.append(lax.ppermute(pieces[hop], AXES, pairs))  31.1 us
    ppermute x21, waiting for transfers between devices, deliver(): came.append(lax.ppermute(pieces[hop], AXES, pairs))  28.8 us
    pallas_call x1, Pallas kernels, column_call(): pl.pallas_call(column_kernel, name='column_back', in_specs=[SMEM, VMEM, V...  20.5 us
    pallas_call x4, Pallas kernels, split(): pl.pallas_call(split_kernel, name='split_shares', grid=(4,) if large else...  14.5 us
    pallas_call x1, Pallas kernels, row_input_call(): pl.pallas_call(row_input_kernel, name='row_input', in_specs=[SMEM, VMEM,...  12.2 us
  transfers between devices with their start and end apart: 33, of which 14 were waited for; matrix products, arithmetic and copies ran while one was open for 2% of the time, Pallas kernels for 23%

profile of v5, /device:TPU:24, one launch (start us, length us, event | category | flops | bytes accessed | tf_op | source)
XLA Modules:
  0.0 288.4 jit_solution(4652567307041239676)
XLA Ops:
  9.1 1.6 collective-permute-start.1
  17.7 2.2 concatenate.19
  20.7 31.4 %all-gather.2 = bf16[128,1,128]{2,1,0:T(2,128)(2,1)S(1)} all-gather(bf16[1,1,128]{2,1,0:T(2,128)(2,1)S(1)} %fusion.1), channel_id=2, replica_groups=mesh['y'=4,'z'=4,'x'=4,'c'=2] {'y','z','x','c'}, dimensions={0}, use_global_device_ids=true | all-gather | bytes 33024 | tf_op jit(solution)/shard_map/all_gather | solution.py:990
  55.0 50.8 %all-gather.5.cloned.1.call-done = bf16[14336,768]{1,0:T(8,128)(2,1)} async-done(((bf16[112,768]{1,0:T(8,128)(2,1)}), bf16[14336,768]{1,0:T(8,128)(2,1)}) %all-gather.5.cloned.1.call-update) | async-done | bytes 22020112 | tf_op jit(solution)/shard_map/all_gather | solution.py:987
  105.8 39.0 %forward.1 = (bf16[512,768]{1,0:T(8,128)(2,1)}, f32[512,768]{1,0:T(8,128)}, bf16[10,512,768]{2,1,0:T(8,128)(2,1)}, f32[2,512,768]{2,1,0:T(8,128)}, bf16[8,16,48,768]{3,2,1,0:T(8,128)(2,1)}, /*index=5*/f32[8,768]{1,0:T(8,128)}) custom-call(s32[4]{0:T(128)} %pad_add_fusion.ints, bf16[512,768]{1,0:T(8,128)(2,1)} %bitcast.84, bf16[512,768]{1,0:T(8,128)(2,1)} %bitcast.85, ...), custom_call_target="tpu_custom_call" | custom-call | flops 24000000000 | bytes 50000000 | tf_op jit(solution)/shard_map/forward/pallas_call | solution.py:646
  145.0 20.5 %column_back.1 = (f32[512,768]{1,0:T(8,128)}, bf16[4,4,4,24,768]{4,3,2,1,0:T(8,128)(2,1)}, bf16[4,4,4,24,768]{4,3,2,1,0:T(8,128)(2,1)}, f32[8,768]{1,0:T(8,128)}) custom-call(s32[4]{0:T(128)} %pad_add_fusion.ints, f32[512,768]{1,0:T(8,128)} %get-tuple-element.96.grad_in, f32[16,768]{1,0:T(8,128)} %pad.9.small, bf16[32,4,112,768]{3,2,1,0:T(8,128)(2,1)} %bitcast.81, ...), custom_call_target="tpu_custom_call" | custom-call | flops 10000000000 | bytes 10000000 | tf_op jit(solution)/shard_map/column_back/pallas_call | solution.py:704
  165.9 7.7 %row_heads.1.grads_in = bf16[3,512,768]{2,1,0:T(8,128)(2,1)} custom-call(s32[4]{0:T(128)} %pad_add_fusion.ints, f32[512,768]{1,0:T(8,128)} %get-tuple-element.99.grad_in, bf16[32,4,112,768]{3,2,1,0:T(8,128)(2,1)} %bitcast.82, bf16[10,512,768]{2,1,0:T(8,128)(2,1)} %get-tuple-element.97.saved), custom_call_target="tpu_custom_call" | custom-call | flops 10000000000 | bytes 10000000 | tf_op jit(solution)/shard_map/row_heads/pallas_call | solution.py:680
  173.6 4.4 %split_shares.4 = (bf16[4,4,24,768]{3,2,1,0:T(8,128)(2,1)}, bf16[4,4,24,768]{3,2,1,0:T(8,128)(2,1)}, bf16[4,4,24,768]{3,2,1,0:T(8,128)(2,1)}, bf16[4,4,24,768]{3,2,1,0:T(8,128)(2,1)}) custom-call(s32[1]{0:T(128)} %bitcast.29.place, bf16[4,4,4,24,768]{4,3,2,1,0:T(8,128)(2,1)} %get-tuple-element.102.refs_0_, ...), custom_call_target="tpu_custom_call" | custom-call | flops 1000000 | bytes 1000000 | tf_op jit(solution)/shard_map/split_shares/pallas_call | solution.py:790
  178.5 2.4 collective-permute-start.5
  180.9 12.2 %row_input.1 = (f32[512,768]{1,0:T(8,128)}, bf16[4,4,4,16,896]{4,3,2,1,0:T(8,128)(2,1)}, bf16[4,4,4,16,896]{4,3,2,1,0:T(8,128)(2,1)}) custom-call(s32[4]{0:T(128)} %pad_add_fusion.ints, f32[512,768]{1,0:T(8,128)} %get-tuple-element.99.grad_in, f32[16,768]{1,0:T(8,128)} %pad.9.small, f32[8,768]{1,0:T(8,128)} %get-tuple-element.100.sums_col, ...), custom_call_target="tpu_custom_call" | custom-call | flops 20000000000 | bytes 10000000 | tf_op jit(solution)/shard_map/row_input/pallas_call | solution.py:747
  193.2 3.3 %collective-permute-done.6.refs_7_ = bf16[4,4,24,768]{3,2,1,0:T(8,128)(2,1)S(1)} collective-permute-done((bf16[4,4,24,768]{3,2,1,0:T(8,128)(2,1)}, bf16[4,4,24,768]{3,2,1,0:T(8,128)(2,1)S(1)}, u32[]{:S(2)}, u32[]{:S(2)}) %collective-permute-start.6) | collective-permute-done | bytes 589856 | tf_op jit(solution)/shard_map/ppermute | solution.py:974
  196.4 8.4 %row_weights.1 = (bf16[4,4,4,24,768]{4,3,2,1,0:T(8,128)(2,1)}, bf16[4,4,4,24,768]{4,3,2,1,0:T(8,128)(2,1)}) custom-call(s32[4]{0:T(128)} %pad_add_fusion.ints, f32[512,768]{1,0:T(8,128)} %get-tuple-element.99.grad_in, bf16[10,512,768]{2,1,0:T(8,128)(2,1)} %get-tuple-element.97.saved, bf16[3,512,768]{2,1,0:T(8,128)(2,1)} %row_heads.1.grads_in), custom_call_target="tpu_custom_call" | custom-call | flops 1000000 | bytes 100000 | tf_op jit(solution)/shard_map/row_weights/pallas_call | solution.py:727
  205.6 4.0 %split_shares.5 = (bf16[4,4,16,896]{3,2,1,0:T(8,128)(2,1)}, bf16[4,4,16,896]{3,2,1,0:T(8,128)(2,1)}, bf16[4,4,16,896]{3,2,1,0:T(8,128)(2,1)}, bf16[4,4,16,896]{3,2,1,0:T(8,128)(2,1)}) custom-call(s32[1]{0:T(128)} %bitcast.32.place, bf16[4,4,4,16,896]{4,3,2,1,0:T(8,128)(2,1)} %get-tuple-element.122.refs_0_, ...), custom_call_target="tpu_custom_call" | custom-call | flops 1000000 | bytes 1000000 | tf_op jit(solution)/shard_map/split_shares/pallas_call | solution.py:790
  210.1 4.5 %split_shares.6 = (bf16[4,4,24,768]{3,2,1,0:T(8,128)(2,1)}, bf16[4,4,24,768]{3,2,1,0:T(8,128)(2,1)}, bf16[4,4,24,768]{3,2,1,0:T(8,128)(2,1)}, bf16[4,4,24,768]{3,2,1,0:T(8,128)(2,1)}) custom-call(s32[1]{0:T(128)} %bitcast.29.place, bf16[4,4,4,24,768]{4,3,2,1,0:T(8,128)(2,1)} %get-tuple-element.121.refs_0_, ...), custom_call_target="tpu_custom_call" | custom-call | flops 1000000 | bytes 1000000 | tf_op jit(solution)/shard_map/split_shares/pallas_call | solution.py:790
  215.2 2.3 collective-permute-start.10
  218.1 1.5 collective-permute-start.15
  219.6 2.7 collective-permute-start.16
  222.3 9.2 %collective-permute-done.9.refs_1_ = bf16[4,4,24,768]{3,2,1,0:T(8,128)(2,1)S(1)} collective-permute-done((bf16[4,4,24,768]{3,2,1,0:T(8,128)(2,1)}, bf16[4,4,24,768]{3,2,1,0:T(8,128)(2,1)S(1)}, u32[]{:S(2)}, u32[]{:S(2)}) %collective-permute-start.9) | collective-permute-done | bytes 589856 | tf_op jit(solution)/shard_map/ppermute | solution.py:974
  231.5 2.7 collective-permute-start.17
  234.2 5.0 %collective-permute-done.11.refs_3_ = bf16[4,4,24,768]{3,2,1,0:T(8,128)(2,1)} collective-permute-done((bf16[4,4,24,768]{3,2,1,0:T(8,128)(2,1)}, bf16[4,4,24,768]{3,2,1,0:T(8,128)(2,1)}, u32[]{:S(2)}, u32[]{:S(2)}) %collective-permute-start.11) | collective-permute-done | bytes 589856 | tf_op jit(solution)/shard_map/ppermute | solution.py:974
  241.3 2.7 second_split.1
  245.3 2.9 collective-permute-start.13
  249.6 1.5 split_shares.7
  251.1 1.6 collective-permute-start.18
  253.4 2.5 collective-permute-done.18.refs_5_
  256.2 2.9 collective-permute-done.19.refs_6_
  259.0 2.9 %collective-permute-done.20.refs_7_ = bf16[4,16,896]{2,1,0:T(8,128)(2,1)S(1)} collective-permute-done((bf16[4,16,896]{2,1,0:T(8,128)(2,1)S(1)}, bf16[4,16,896]{2,1,0:T(8,128)(2,1)S(1)}, u32[]{:S(2)}, u32[]{:S(2)}) %collective-permute-start.20) | collective-permute-done | bytes 114720 | tf_op jit(solution)/shard_map/ppermute | solution.py:974
  263.2 2.3 collective-permute-start.21
  266.9 1.9 collective-permute-start.26
  268.8 2.7 collective-permute-start.22
  272.9 1.7 collective-permute-done.22.refs_2_
  278.5 2.4 collective-permute-done.28.three
  (83 shorter events, 28.7 us)
Async XLA Ops:
  7.2 98.6 %all-gather.5.cloned.1.call-start = ((), (), s32[]{:S(2)}) async-start(), calls=%async_computation.4 | async-start | bytes 22192128 | tf_op jit(solution)/shard_map/all_gather | solution.py:987
  9.0 2.7 collective-permute-start.2
  9.1 4.0 %collective-permute-start.1 = (bf16[3,6,768]{2,1,0:T(8,128)(2,1)S(1)}, bf16[3,6,768]{2,1,0:T(8,128)(2,1)S(1)}, u32[]{:S(2)}, u32[]{:S(2)}) collective-permute-start(bf16[3,6,768]{2,1,0:T(8,128)(2,1)S(1)} %get-tuple-element.180), channel_id=1, source_target_pairs={{0,2},{1,3},{2,0},{3,1},{4,6},{5,7},{6,4},{7,5},{8,10},{9,11},{10,... | collective-permute-start | bytes 82952 | tf_op jit(solution)/shard_map/ppermute | solution.py:936
  10.6 3.4 %collective-permute-start = (bf16[3,6,768]{2,1,0:T(8,128)(2,1)S(1)}, bf16[3,6,768]{2,1,0:T(8,128)(2,1)S(1)}, u32[]{:S(2)}, u32[]{:S(2)}) collective-permute-start(bf16[3,6,768]{2,1,0:T(8,128)(2,1)S(1)} %get-tuple-element.181), channel_id=1, source_target_pairs={{0,3},{1,2},{2,1},{3,0},{4,7},{5,6},{6,5},{7,4},{8,11},{9,10},{10,... | collective-permute-start | bytes 82952 | tf_op jit(solution)/shard_map/ppermute | solution.py:936
  15.7 189.2 %reduce-scatter.3.cloned.1.call-start = ((), (), s32[]{:S(2)}) async-start(), calls=%async_computation.2 | async-start | bytes 10616832 | tf_op jit(solution)/shard_map/reduce_scatter | solution.py:953
  144.8 111.3 %reduce-scatter.5.cloned.1.call-start = ((), (), s32[]{:S(2)}) async-start(), calls=%async_computation.3 | async-start | bytes 1474560 | tf_op jit(solution)/shard_map/reduce_scatter | solution.py:1017
  165.5 8.1 %collective-permute-start.3 = (bf16[4,4,4,24,768]{4,3,2,1,0:T(8,128)(2,1)}, bf16[4,4,4,24,768]{4,3,2,1,0:T(8,128)(2,1)}, u32[]{:S(2)}, u32[]{:S(2)}) collective-permute-start(bf16[4,4,4,24,768]{4,3,2,1,0:T(8,128)(2,1)} %get-tuple-element.103), channel_id=1, source_target_pairs={{0,1},{1,0},{2,3},{3,2},{4,5},{5,4},{6,7},{7,6},{8,9},{9,8},{10,11... | collective-permute-start | bytes 7077896 | tf_op jit(solution)/shard_map/ppermute | solution.py:949
  178.0 15.1 %collective-permute-start.4 = (bf16[4,4,24,768]{3,2,1,0:T(8,128)(2,1)}, bf16[4,4,24,768]{3,2,1,0:T(8,128)(2,1)S(1)}, u32[]{:S(2)}, u32[]{:S(2)}) collective-permute-start(bf16[4,4,24,768]{3,2,1,0:T(8,128)(2,1)} %get-tuple-element.115), channel_id=1, source_target_pairs={{0,32},{1,9},{2,34},{3,11},{4,36},{5,13},{6,38},{7,15},{8,40},{9,1... | collective-permute-start | bytes 1769480 | tf_op jit(solution)/shard_map/ppermute | solution.py:974
  178.5 14.6 %collective-permute-start.5 = (bf16[4,4,24,768]{3,2,1,0:T(8,128)(2,1)}, bf16[4,4,24,768]{3,2,1,0:T(8,128)(2,1)S(1)}, u32[]{:S(2)}, u32[]{:S(2)}) collective-permute-start(bf16[4,4,24,768]{3,2,1,0:T(8,128)(2,1)} %get-tuple-element.116), channel_id=1, source_target_pairs={{0,64},{1,17},{2,66},{3,19},{4,68},{5,21},{6,70},{7,23},{8,72},{9,... | collective-permute-start | bytes 1769480 | tf_op jit(solution)/shard_map/ppermute | solution.py:974
  180.9 15.5 %collective-permute-start.6 = (bf16[4,4,24,768]{3,2,1,0:T(8,128)(2,1)}, bf16[4,4,24,768]{3,2,1,0:T(8,128)(2,1)S(1)}, u32[]{:S(2)}, u32[]{:S(2)}) collective-permute-start(bf16[4,4,24,768]{3,2,1,0:T(8,128)(2,1)} %get-tuple-element.117), channel_id=1, source_target_pairs={{0,96},{1,25},{2,98},{3,27},{4,100},{5,29},{6,102},{7,31},{8,104},... | collective-permute-start | bytes 1769480 | tf_op jit(solution)/shard_map/ppermute | solution.py:974
  196.4 8.4 %collective-permute-start.7 = (bf16[4,4,4,16,896]{4,3,2,1,0:T(8,128)(2,1)}, bf16[4,4,4,16,896]{4,3,2,1,0:T(8,128)(2,1)}, u32[]{:S(2)}, u32[]{:S(2)}) collective-permute-start(bf16[4,4,4,16,896]{4,3,2,1,0:T(8,128)(2,1)} %get-tuple-element.118), channel_id=1, source_target_pairs={{0,1},{1,0},{2,3},{3,2},{4,5},{5,4},{6,7},{7,6},{8,9},{9,8},{10,11... | collective-permute-start | bytes 5505032 | tf_op jit(solution)/shard_map/ppermute | solution.py:949
  204.9 5.2 %collective-permute-start.8 = (bf16[4,4,4,24,768]{4,3,2,1,0:T(8,128)(2,1)}, bf16[4,4,4,24,768]{4,3,2,1,0:T(8,128)(2,1)}, u32[]{:S(2)}, u32[]{:S(2)}) collective-permute-start(bf16[4,4,4,24,768]{4,3,2,1,0:T(8,128)(2,1)} %get-tuple-element.128), channel_id=1, source_target_pairs={{0,1},{1,0},{2,3},{3,2},{4,5},{5,4},{6,7},{7,6},{8,9},{9,8},{10,11... | collective-permute-start | bytes 7077896 | tf_op jit(solution)/shard_map/ppermute | solution.py:949
  214.6 16.9 %collective-permute-start.9 = (bf16[4,4,24,768]{3,2,1,0:T(8,128)(2,1)}, bf16[4,4,24,768]{3,2,1,0:T(8,128)(2,1)S(1)}, u32[]{:S(2)}, u32[]{:S(2)}) collective-permute-start(bf16[4,4,24,768]{3,2,1,0:T(8,128)(2,1)} %get-tuple-element.131), channel_id=1, source_target_pairs={{0,32},{1,9},{2,34},{3,11},{4,36},{5,13},{6,38},{7,15},{8,40},{9,1... | collective-permute-start | bytes 1769480 | tf_op jit(solution)/shard_map/ppermute | solution.py:974
  215.2 18.9 %collective-permute-start.10 = (bf16[4,4,24,768]{3,2,1,0:T(8,128)(2,1)}, bf16[4,4,24,768]{3,2,1,0:T(8,128)(2,1)S(1)}, u32[]{:S(2)}, u32[]{:S(2)}) collective-permute-start(bf16[4,4,24,768]{3,2,1,0:T(8,128)(2,1)} %get-tuple-element.132), channel_id=1, source_target_pairs={{0,64},{1,17},{2,66},{3,19},{4,68},{5,21},{6,70},{7,23},{8,72},{9,... | collective-permute-start | bytes 1769480 | tf_op jit(solution)/shard_map/ppermute | solution.py:974
  217.6 21.6 %collective-permute-start.11 = (bf16[4,4,24,768]{3,2,1,0:T(8,128)(2,1)}, bf16[4,4,24,768]{3,2,1,0:T(8,128)(2,1)}, u32[]{:S(2)}, u32[]{:S(2)}) collective-permute-start(bf16[4,4,24,768]{3,2,1,0:T(8,128)(2,1)} %get-tuple-element.133), channel_id=1, source_target_pairs={{0,96},{1,25},{2,98},{3,27},{4,100},{5,29},{6,102},{7,31},{8,104},... | collective-permute-start | bytes 1769480 | tf_op jit(solution)/shard_map/ppermute | solution.py:974
  218.1 30.1 %collective-permute-start.15 = (bf16[4,4,16,896]{3,2,1,0:T(8,128)(2,1)}, bf16[4,4,16,896]{3,2,1,0:T(8,128)(2,1)}, u32[]{:S(2)}, u32[]{:S(2)}) collective-permute-start(bf16[4,4,16,896]{3,2,1,0:T(8,128)(2,1)} %get-tuple-element.143), channel_id=1, source_target_pairs={{0,2},{1,3},{2,4},{3,5},{4,6},{5,7},{6,0},{7,1},{8,10},{9,11},{10,... | collective-permute-start | bytes 1376264 | tf_op jit(solution)/shard_map/ppermute | solution.py:974
  219.6 30.0 %collective-permute-start.16 = (bf16[4,4,16,896]{3,2,1,0:T(8,128)(2,1)}, bf16[4,4,16,896]{3,2,1,0:T(8,128)(2,1)}, u32[]{:S(2)}, u32[]{:S(2)}) collective-permute-start(bf16[4,4,16,896]{3,2,1,0:T(8,128)(2,1)} %get-tuple-element.144), channel_id=1, source_target_pairs={{0,4},{1,5},{2,6},{3,7},{4,0},{5,1},{6,2},{7,3},{8,12},{9,13},{10,... | collective-permute-start | bytes 1376264 | tf_op jit(solution)/shard_map/ppermute | solution.py:974
  231.5 18.1 %collective-permute-start.17 = (bf16[4,4,16,896]{3,2,1,0:T(8,128)(2,1)}, bf16[4,4,16,896]{3,2,1,0:T(8,128)(2,1)}, u32[]{:S(2)}, u32[]{:S(2)}) collective-permute-start(bf16[4,4,16,896]{3,2,1,0:T(8,128)(2,1)} %get-tuple-element.145), channel_id=1, source_target_pairs={{0,6},{1,7},{2,0},{3,1},{4,2},{5,3},{6,4},{7,5},{8,14},{9,15},{10,... | collective-permute-start | bytes 1376264 | tf_op jit(solution)/shard_map/ppermute | solution.py:974
  244.1 17.9 %collective-permute-start.12 = (bf16[4,48,768]{2,1,0:T(8,128)(2,1)}, bf16[4,48,768]{2,1,0:T(8,128)(2,1)S(1)}, u32[]{:S(2)}, u32[]{:S(2)}) collective-permute-start(bf16[4,48,768]{2,1,0:T(8,128)(2,1)} %get-tuple-element.139), channel_id=1, source_target_pairs={{0,8},{1,33},{2,10},{3,35},{4,12},{5,37},{6,14},{7,39},{8,16},{9,4... | collective-permute-start | bytes 884744 | tf_op jit(solution)/shard_map/ppermute | solution.py:974
  245.3 16.7 %collective-permute-start.13 = (bf16[4,48,768]{2,1,0:T(8,128)(2,1)}, bf16[4,48,768]{2,1,0:T(8,128)(2,1)S(1)}, u32[]{:S(2)}, u32[]{:S(2)}) collective-permute-start(bf16[4,48,768]{2,1,0:T(8,128)(2,1)} %get-tuple-element.140), channel_id=1, source_target_pairs={{0,16},{1,65},{2,18},{3,67},{4,20},{5,69},{6,22},{7,71},{8,24},{9,... | collective-permute-start | bytes 884744 | tf_op jit(solution)/shard_map/ppermute | solution.py:974
  248.2 13.8 %collective-permute-start.14 = (bf16[4,48,768]{2,1,0:T(8,128)(2,1)}, bf16[4,48,768]{2,1,0:T(8,128)(2,1)S(1)}, u32[]{:S(2)}, u32[]{:S(2)}) collective-permute-start(bf16[4,48,768]{2,1,0:T(8,128)(2,1)} %get-tuple-element.141), channel_id=1, source_target_pairs={{0,24},{1,97},{2,26},{3,99},{4,28},{5,101},{6,30},{7,103},{8,0},{9... | collective-permute-start | bytes 884744 | tf_op jit(solution)/shard_map/ppermute | solution.py:974
  251.1 4.9 %collective-permute-start.18 = (bf16[4,16,896]{2,1,0:T(8,128)(2,1)S(1)}, bf16[4,16,896]{2,1,0:T(8,128)(2,1)S(1)}, u32[]{:S(2)}, u32[]{:S(2)}) collective-permute-start(bf16[4,16,896]{2,1,0:T(8,128)(2,1)S(1)} %get-tuple-element.147), channel_id=1, source_target_pairs={{0,32},{1,33},{2,34},{3,35},{4,36},{5,37},{6,38},{7,39},{8,40},{9,... | collective-permute-start | bytes 344072 | tf_op jit(solution)/shard_map/ppermute | solution.py:974
  252.7 6.3 %collective-permute-start.19 = (bf16[4,16,896]{2,1,0:T(8,128)(2,1)S(1)}, bf16[4,16,896]{2,1,0:T(8,128)(2,1)S(1)}, u32[]{:S(2)}, u32[]{:S(2)}) collective-permute-start(bf16[4,16,896]{2,1,0:T(8,128)(2,1)S(1)} %get-tuple-element.148), channel_id=1, source_target_pairs={{0,64},{1,65},{2,66},{3,67},{4,68},{5,69},{6,70},{7,71},{8,72},{9,... | collective-permute-start | bytes 344072 | tf_op jit(solution)/shard_map/ppermute | solution.py:974
  256.0 6.0 %collective-permute-start.20 = (bf16[4,16,896]{2,1,0:T(8,128)(2,1)S(1)}, bf16[4,16,896]{2,1,0:T(8,128)(2,1)S(1)}, u32[]{:S(2)}, u32[]{:S(2)}) collective-permute-start(bf16[4,16,896]{2,1,0:T(8,128)(2,1)S(1)} %get-tuple-element.149), channel_id=1, source_target_pairs={{0,96},{1,97},{2,98},{3,99},{4,100},{5,101},{6,102},{7,103},{8,104... | collective-permute-start | bytes 344072 | tf_op jit(solution)/shard_map/ppermute | solution.py:974
  263.2 8.3 %collective-permute-start.21 = (bf16[48,768]{1,0:T(8,128)(2,1)S(1)}, bf16[48,768]{1,0:T(8,128)(2,1)S(1)}, u32[]{:S(2)}, u32[]{:S(2)}) collective-permute-start(bf16[48,768]{1,0:T(8,128)(2,1)S(1)} %get-tuple-element.151), channel_id=1, source_target_pairs={{0,2},{1,3},{2,4},{3,5},{4,6},{5,7},{6,0},{7,1},{8,10},{9,11},{10,... | collective-permute-start | bytes 221192 | tf_op jit(solution)/shard_map/ppermute | solution.py:974
  265.5 10.4 %collective-permute-start.24 = (bf16[72,768]{1,0:T(8,128)(2,1)S(1)}, bf16[72,768]{1,0:T(8,128)(2,1)S(1)}, u32[]{:S(2)}, u32[]{:S(2)}) collective-permute-start(bf16[72,768]{1,0:T(8,128)(2,1)S(1)} %get-tuple-element.155), channel_id=1, source_target_pairs={{0,8},{1,9},{2,10},{3,11},{4,12},{5,13},{6,14},{7,15},{8,16},{9,17... | collective-permute-start | bytes 331784 | tf_op jit(solution)/shard_map/ppermute | solution.py:974
  266.1 9.7 %collective-permute-start.25 = (bf16[72,768]{1,0:T(8,128)(2,1)S(1)}, bf16[72,768]{1,0:T(8,128)(2,1)S(1)}, u32[]{:S(2)}, u32[]{:S(2)}) collective-permute-start(bf16[72,768]{1,0:T(8,128)(2,1)S(1)} %get-tuple-element.156), channel_id=1, source_target_pairs={{0,16},{1,17},{2,18},{3,19},{4,20},{5,21},{6,22},{7,23},{8,24},{9,... | collective-permute-start | bytes 331784 | tf_op jit(solution)/shard_map/ppermute | solution.py:974
  266.9 8.9 %collective-permute-start.26 = (bf16[72,768]{1,0:T(8,128)(2,1)S(1)}, bf16[72,768]{1,0:T(8,128)(2,1)S(1)}, u32[]{:S(2)}, u32[]{:S(2)}) collective-permute-start(bf16[72,768]{1,0:T(8,128)(2,1)S(1)} %get-tuple-element.157), channel_id=1, source_target_pairs={{0,24},{1,25},{2,26},{3,27},{4,28},{5,29},{6,30},{7,31},{8,0},{9,1... | collective-permute-start | bytes 331784 | tf_op jit(solution)/shard_map/ppermute | solution.py:974
  268.8 5.9 %collective-permute-start.22 = (bf16[48,768]{1,0:T(8,128)(2,1)S(1)}, bf16[48,768]{1,0:T(8,128)(2,1)S(1)}, u32[]{:S(2)}, u32[]{:S(2)}) collective-permute-start(bf16[48,768]{1,0:T(8,128)(2,1)S(1)} %get-tuple-element.152), channel_id=1, source_target_pairs={{0,4},{1,5},{2,6},{3,7},{4,0},{5,1},{6,2},{7,3},{8,12},{9,13},{10,... | collective-permute-start | bytes 221192 | tf_op jit(solution)/shard_map/ppermute | solution.py:974
  271.5 4.4 %collective-permute-start.23 = (bf16[48,768]{1,0:T(8,128)(2,1)S(1)}, bf16[48,768]{1,0:T(8,128)(2,1)S(1)}, u32[]{:S(2)}, u32[]{:S(2)}) collective-permute-start(bf16[48,768]{1,0:T(8,128)(2,1)S(1)} %get-tuple-element.153), channel_id=1, source_target_pairs={{0,6},{1,7},{2,0},{3,1},{4,2},{5,3},{6,4},{7,5},{8,14},{9,15},{10,... | collective-permute-start | bytes 221192 | tf_op jit(solution)/shard_map/ppermute | solution.py:974
  276.6 4.3 %collective-permute-start.28 = (bf16[3,6,768]{2,1,0:T(8,128)(2,1)S(1)}, bf16[3,6,768]{2,1,0:T(8,128)(2,1)S(1)}, u32[]{:S(2)}, u32[]{:S(2)}) collective-permute-start(bf16[3,6,768]{2,1,0:T(8,128)(2,1)S(1)} %get-tuple-element.162), channel_id=1, source_target_pairs={{0,2},{1,3},{2,0},{3,1},{4,6},{5,7},{6,4},{7,5},{8,10},{9,11},{10,... | collective-permute-start | bytes 82952 | tf_op jit(solution)/shard_map/ppermute | solution.py:936
  277.4 3.8 %collective-permute-start.29 = (bf16[3,6,768]{2,1,0:T(8,128)(2,1)S(1)}, bf16[3,6,768]{2,1,0:T(8,128)(2,1)S(1)}, u32[]{:S(2)}, u32[]{:S(2)}) collective-permute-start(bf16[3,6,768]{2,1,0:T(8,128)(2,1)S(1)} %get-tuple-element.163), channel_id=1, source_target_pairs={{0,3},{1,2},{2,1},{3,0},{4,7},{5,6},{6,5},{7,4},{8,11},{9,10},{10,... | collective-permute-start | bytes 82952 | tf_op jit(solution)/shard_map/ppermute | solution.py:936
  (7 other events, 50.8 us)
Sparse Core Ops, SparseCore 0:
  15.8 89.9 all-gather.4
  144.9 56.8 reduce-scatter.2
  205.7 30.4 reduce-scatter.4

commit v6 on v5

--- a/solution.py
+++ b/solution.py
@@ -799,14 +799,32 @@
     )(place, *inputs)
 
 
+def sum_kernel(*refs):
+    def body(j):
+        refs[-1][j] = sum_of(refs[:-1], j).astype(BF16)
+
+    loop(4, body)
+
+
+def summed(parts):
+    return pl.pallas_call(
+        sum_kernel,
+        name="column_sum",
+        in_specs=[VMEM] * 4,
+        out_shape=SHAPE(parts[0].shape, BF16),
+        out_specs=VMEM,
+        compiler_params=params(8),
+        cost_estimate=cost(10**6, 10**6),
+    )(*parts)
+
+
 def second_kernel(place, *refs):
     for hop in range(4):
         to = (place[0] + hop) & 3
 
         def body(j):
-            for g in range(2):
-                value = sum_of(refs[4 * g : 4 * g + 4], to, j)
-                refs[8 + hop][j, g * SLAB : (g + 1) * SLAB, :] = value.astype(BF16)
+            refs[5 + hop][j, 0:SLAB, :] = sum_of(refs[:4], to, j).astype(BF16)
+            refs[5 + hop][j, SLAB : 2 * SLAB, :] = refs[4][to, j]
 
         loop(4, body)
 
@@ -815,12 +833,12 @@
     return pl.pallas_call(
         second_kernel,
         name="second_split",
-        in_specs=[SMEM] + [VMEM] * 8,
+        in_specs=[SMEM] + [VMEM] * 5,
         out_shape=(SHAPE((4, 2 * SLAB, D), BF16),) * 4,
         out_specs=(VMEM,) * 4,
         compiler_params=params(10),
         cost_estimate=cost(10**6, 10**6),
-    )(place, *row, *col)
+    )(place, *row, col)
 
 
 def third_kernel(place, table_place, ffn, *refs):
@@ -1018,7 +1036,9 @@
     y_place, z_place = place_on(TABLE_STAGES[1]), place_on(TABLE_STAGES[2])
     table, other = barrier((split((table_own, table_other), places[2]), swap(other)))
     table = deliver(table, TABLE_STAGES[0])
-    row = deliver(split((own, other), places[0]), STAGES[0])
+    pieces, col = barrier((split((own, other), places[0]), col))
+    row = deliver(pieces, STAGES[0])
+    col = summed(col)
     table = deliver(split(table, y_place), TABLE_STAGES[1])
     rows = deliver(second_split(row, col, places[1]), STAGES[1])
     pieces = third_split(rows, table, ffn, places[2], z_place)

time: 292 us -> 290 us (level)
  transfers between devices with their start and end apart: 33 -> 33, of which waited for: 14 -> 13; matrix products, arithmetic and copies ran while one was open for 2% -> 2% of each run, Pallas kernels for 23% -> 23%
where the time goes in v6:
time: 290 us; the launch traced here: 288 us
  Pallas kernels  106 us (37%)
  waiting for transfers between devices  85.7 us (30%)
  starting transfers between devices  36.8 us (13%)
  blocking collectives  31.4 us (11%)
  between operations  16 us (6%)
  local copies, waits for them, and re-layouts  7.39 us (3%)
  other arithmetic  4.58 us (2%)
    all_gather x1, waiting for transfers between devices, gather(): gathered = lax.all_gather(packed, AXES, axis=0, tiled=False)  50.8 us
    pallas_call x1, Pallas kernels, forward_call(): pl.pallas_call(forward_kernel, name='forward', in_specs=[SMEM, VMEM, VMEM...  39 us
    ppermute x21, starting transfers between devices, deliver(): came.append(lax.ppermute(pieces[hop], AXES, pairs))  31.7 us
    all_gather x1, blocking collectives, gather(): lines = lax.all_gather(line, AXES, axis=0, tiled=False).astype(F32)  31.4 us
    ppermute x21, waiting for transfers between devices, deliver(): came.append(lax.ppermute(pieces[hop], AXES, pairs))  29.5 us
    pallas_call x1, Pallas kernels, column_call(): pl.pallas_call(column_kernel, name='column_back', in_specs=[SMEM, VMEM, V...  20.5 us
    pallas_call x4, Pallas kernels, split(): pl.pallas_call(split_kernel, name='split_shares', grid=(4,) if large else...  14.5 us
    pallas_call x1, Pallas kernels, row_input_call(): pl.pallas_call(row_input_kernel, name='row_input', in_specs=[SMEM, VMEM,...  12.2 us
  transfers between devices with their start and end apart: 33, of which 13 were waited for; matrix products, arithmetic and copies ran while one was open for 2% of the time, Pallas kernels for 23%

profile of v6, /device:TPU:24, one launch (start us, length us, event | category | flops | bytes accessed | tf_op | source)
XLA Modules:
  0.0 287.6 jit_solution(11924520379774627140)
XLA Ops:
  9.1 1.6 collective-permute-start.1
  17.7 2.2 concatenate.19
  20.7 31.4 %all-gather.2 = bf16[128,1,128]{2,1,0:T(2,128)(2,1)S(1)} all-gather(bf16[1,1,128]{2,1,0:T(2,128)(2,1)S(1)} %fusion.1), channel_id=2, replica_groups=mesh['y'=4,'z'=4,'x'=4,'c'=2] {'y','z','x','c'}, dimensions={0}, use_global_device_ids=true | all-gather | bytes 33024 | tf_op jit(solution)/shard_map/all_gather | solution.py:1008
  55.0 50.8 %all-gather.5.cloned.1.call-done = bf16[14336,768]{1,0:T(8,128)(2,1)} async-done(((bf16[112,768]{1,0:T(8,128)(2,1)}), bf16[14336,768]{1,0:T(8,128)(2,1)}) %all-gather.5.cloned.1.call-update) | async-done | bytes 22020112 | tf_op jit(solution)/shard_map/all_gather | solution.py:1005
  105.8 39.0 %forward.1 = (bf16[512,768]{1,0:T(8,128)(2,1)}, f32[512,768]{1,0:T(8,128)}, bf16[10,512,768]{2,1,0:T(8,128)(2,1)}, f32[2,512,768]{2,1,0:T(8,128)}, bf16[8,16,48,768]{3,2,1,0:T(8,128)(2,1)}, /*index=5*/f32[8,768]{1,0:T(8,128)}) custom-call(s32[4]{0:T(128)} %pad_add_fusion.ints, bf16[512,768]{1,0:T(8,128)(2,1)} %bitcast.84, bf16[512,768]{1,0:T(8,128)(2,1)} %bitcast.85, ...), custom_call_target="tpu_custom_call" | custom-call | flops 24000000000 | bytes 50000000 | tf_op jit(solution)/shard_map/forward/pallas_call | solution.py:646
  145.0 20.5 %column_back.1 = (f32[512,768]{1,0:T(8,128)}, bf16[4,4,4,24,768]{4,3,2,1,0:T(8,128)(2,1)}, bf16[4,4,4,24,768]{4,3,2,1,0:T(8,128)(2,1)}, f32[8,768]{1,0:T(8,128)}) custom-call(s32[4]{0:T(128)} %pad_add_fusion.ints, f32[512,768]{1,0:T(8,128)} %get-tuple-element.104.grad_in, f32[16,768]{1,0:T(8,128)} %pad.9.small, bf16[32,4,112,768]{3,2,1,0:T(8,128)(2,1)} %bitcast.81, ...), custom_call_target="tpu_custom_call" | custom-call | flops 10000000000 | bytes 10000000 | tf_op jit(solution)/shard_map/column_back/pallas_call | solution.py:704
  165.9 7.7 %row_heads.1.grads_in = bf16[3,512,768]{2,1,0:T(8,128)(2,1)} custom-call(s32[4]{0:T(128)} %pad_add_fusion.ints, f32[512,768]{1,0:T(8,128)} %get-tuple-element.107.grad_in, bf16[32,4,112,768]{3,2,1,0:T(8,128)(2,1)} %bitcast.82, bf16[10,512,768]{2,1,0:T(8,128)(2,1)} %get-tuple-element.105.saved), custom_call_target="tpu_custom_call" | custom-call | flops 10000000000 | bytes 10000000 | tf_op jit(solution)/shard_map/row_heads/pallas_call | solution.py:680
  173.6 4.4 %split_shares.4 = (bf16[4,4,24,768]{3,2,1,0:T(8,128)(2,1)}, bf16[4,4,24,768]{3,2,1,0:T(8,128)(2,1)}, bf16[4,4,24,768]{3,2,1,0:T(8,128)(2,1)}, bf16[4,4,24,768]{3,2,1,0:T(8,128)(2,1)}) custom-call(s32[1]{0:T(128)} %bitcast.29.place, bf16[4,4,4,24,768]{4,3,2,1,0:T(8,128)(2,1)} %get-tuple-element.110.refs_0_, ...), custom_call_target="tpu_custom_call" | custom-call | flops 1000000 | bytes 1000000 | tf_op jit(solution)/shard_map/split_shares/pallas_call | solution.py:790
  178.5 2.4 collective-permute-start.5
  180.9 12.2 %row_input.1 = (f32[512,768]{1,0:T(8,128)}, bf16[4,4,4,16,896]{4,3,2,1,0:T(8,128)(2,1)}, bf16[4,4,4,16,896]{4,3,2,1,0:T(8,128)(2,1)}) custom-call(s32[4]{0:T(128)} %pad_add_fusion.ints, f32[512,768]{1,0:T(8,128)} %get-tuple-element.107.grad_in, f32[16,768]{1,0:T(8,128)} %pad.9.small, f32[8,768]{1,0:T(8,128)} %get-tuple-element.108.sums_col, ...), custom_call_target="tpu_custom_call" | custom-call | flops 20000000000 | bytes 10000000 | tf_op jit(solution)/shard_map/row_input/pallas_call | solution.py:747
  193.2 3.2 %collective-permute-done.6.refs_3_ = bf16[4,4,24,768]{3,2,1,0:T(8,128)(2,1)S(1)} collective-permute-done((bf16[4,4,24,768]{3,2,1,0:T(8,128)(2,1)}, bf16[4,4,24,768]{3,2,1,0:T(8,128)(2,1)S(1)}, u32[]{:S(2)}, u32[]{:S(2)}) %collective-permute-start.6) | collective-permute-done | bytes 589856 | tf_op jit(solution)/shard_map/ppermute | solution.py:992
  196.4 8.4 %row_weights.1 = (bf16[4,4,4,24,768]{4,3,2,1,0:T(8,128)(2,1)}, bf16[4,4,4,24,768]{4,3,2,1,0:T(8,128)(2,1)}) custom-call(s32[4]{0:T(128)} %pad_add_fusion.ints, f32[512,768]{1,0:T(8,128)} %get-tuple-element.107.grad_in, bf16[10,512,768]{2,1,0:T(8,128)(2,1)} %get-tuple-element.105.saved, bf16[3,512,768]{2,1,0:T(8,128)(2,1)} %row_heads.1.grads_in), custom_call_target="tpu_custom_call" | custom-call | flops 1000000 | bytes 100000 | tf_op jit(solution)/shard_map/row_weights/pallas_call | solution.py:727
  205.6 4.0 %split_shares.5 = (bf16[4,4,16,896]{3,2,1,0:T(8,128)(2,1)}, bf16[4,4,16,896]{3,2,1,0:T(8,128)(2,1)}, bf16[4,4,16,896]{3,2,1,0:T(8,128)(2,1)}, bf16[4,4,16,896]{3,2,1,0:T(8,128)(2,1)}) custom-call(s32[1]{0:T(128)} %bitcast.32.place, bf16[4,4,4,16,896]{4,3,2,1,0:T(8,128)(2,1)} %get-tuple-element.130.refs_0_, ...), custom_call_target="tpu_custom_call" | custom-call | flops 1000000 | bytes 1000000 | tf_op jit(solution)/shard_map/split_shares/pallas_call | solution.py:790
  210.1 4.5 %split_shares.6 = (bf16[4,4,24,768]{3,2,1,0:T(8,128)(2,1)}, bf16[4,4,24,768]{3,2,1,0:T(8,128)(2,1)}, bf16[4,4,24,768]{3,2,1,0:T(8,128)(2,1)}, bf16[4,4,24,768]{3,2,1,0:T(8,128)(2,1)}) custom-call(s32[1]{0:T(128)} %bitcast.29.place, bf16[4,4,4,24,768]{4,3,2,1,0:T(8,128)(2,1)} %get-tuple-element.129.refs_0_, ...), custom_call_target="tpu_custom_call" | custom-call | flops 1000000 | bytes 1000000 | tf_op jit(solution)/shard_map/split_shares/pallas_call | solution.py:790
  215.2 2.3 collective-permute-start.10
  218.1 1.5 collective-permute-start.15
  219.6 2.7 collective-permute-start.16
  222.3 9.2 %collective-permute-done.9.refs_1_ = bf16[4,4,24,768]{3,2,1,0:T(8,128)(2,1)S(1)} collective-permute-done((bf16[4,4,24,768]{3,2,1,0:T(8,128)(2,1)}, bf16[4,4,24,768]{3,2,1,0:T(8,128)(2,1)S(1)}, u32[]{:S(2)}, u32[]{:S(2)}) %collective-permute-start.9) | collective-permute-done | bytes 589856 | tf_op jit(solution)/shard_map/ppermute | solution.py:992
  231.5 2.7 collective-permute-start.17
  235.6 3.6 %collective-permute-done.11.refs_3_ = bf16[4,4,24,768]{3,2,1,0:T(8,128)(2,1)} collective-permute-done((bf16[4,4,24,768]{3,2,1,0:T(8,128)(2,1)}, bf16[4,4,24,768]{3,2,1,0:T(8,128)(2,1)}, u32[]{:S(2)}, u32[]{:S(2)}) %collective-permute-start.11) | collective-permute-done | bytes 589856 | tf_op jit(solution)/shard_map/ppermute | solution.py:992
  240.7 4.5 %collective-permute-start.12 = (bf16[4,48,768]{2,1,0:T(8,128)(2,1)S(1)}, bf16[4,48,768]{2,1,0:T(8,128)(2,1)S(1)}, u32[]{:S(2)}, u32[]{:S(2)}) collective-permute-start(bf16[4,48,768]{2,1,0:T(8,128)(2,1)S(1)} %get-tuple-element.155), channel_id=1, source_target_pairs={{0,8},{1,33},{2,10},{3,35},{4,12},{5,37},{6,14},{7,39},{8,16},{9,4... | collective-permute-start | bytes 884744 | tf_op jit(solution)/shard_map/ppermute | solution.py:992
  245.2 2.8 collective-permute-start.13
  249.4 1.5 split_shares.7
  251.2 4.6 %collective-permute-done.18.refs_5_ = bf16[4,16,896]{2,1,0:T(8,128)(2,1)S(1)} collective-permute-done((bf16[4,16,896]{2,1,0:T(8,128)(2,1)S(1)}, bf16[4,16,896]{2,1,0:T(8,128)(2,1)S(1)}, u32[]{:S(2)}, u32[]{:S(2)}) %collective-permute-start.18) | collective-permute-done | bytes 114720 | tf_op jit(solution)/shard_map/ppermute | solution.py:992
  255.8 1.7 collective-permute-done.19.refs_6_
  257.5 4.3 %collective-permute-done.20.refs_7_ = bf16[4,16,896]{2,1,0:T(8,128)(2,1)S(1)} collective-permute-done((bf16[4,16,896]{2,1,0:T(8,128)(2,1)S(1)}, bf16[4,16,896]{2,1,0:T(8,128)(2,1)S(1)}, u32[]{:S(2)}, u32[]{:S(2)}) %collective-permute-start.20) | collective-permute-done | bytes 114720 | tf_op jit(solution)/shard_map/ppermute | solution.py:992
  263.0 2.0 collective-permute-start.21
  266.5 1.8 collective-permute-start.26
  268.3 2.6 collective-permute-start.22
  270.9 1.5 collective-permute-start.23
  272.4 1.7 collective-permute-done.22.refs_2_
  277.9 2.4 collective-permute-done.28.three
  (84 shorter events, 25.7 us)
Async XLA Ops:
  7.2 98.6 %all-gather.5.cloned.1.call-start = ((), (), s32[]{:S(2)}) async-start(), calls=%async_computation.4 | async-start | bytes 22192128 | tf_op jit(solution)/shard_map/all_gather | solution.py:1005
  9.0 2.7 collective-permute-start.2
  9.1 4.0 %collective-permute-start.1 = (bf16[3,6,768]{2,1,0:T(8,128)(2,1)S(1)}, bf16[3,6,768]{2,1,0:T(8,128)(2,1)S(1)}, u32[]{:S(2)}, u32[]{:S(2)}) collective-permute-start(bf16[3,6,768]{2,1,0:T(8,128)(2,1)S(1)} %get-tuple-element.196), channel_id=1, source_target_pairs={{0,2},{1,3},{2,0},{3,1},{4,6},{5,7},{6,4},{7,5},{8,10},{9,11},{10,... | collective-permute-start | bytes 82952 | tf_op jit(solution)/shard_map/ppermute | solution.py:954
  10.6 3.4 %collective-permute-start = (bf16[3,6,768]{2,1,0:T(8,128)(2,1)S(1)}, bf16[3,6,768]{2,1,0:T(8,128)(2,1)S(1)}, u32[]{:S(2)}, u32[]{:S(2)}) collective-permute-start(bf16[3,6,768]{2,1,0:T(8,128)(2,1)S(1)} %get-tuple-element.197), channel_id=1, source_target_pairs={{0,3},{1,2},{2,1},{3,0},{4,7},{5,6},{6,5},{7,4},{8,11},{9,10},{10,... | collective-permute-start | bytes 82952 | tf_op jit(solution)/shard_map/ppermute | solution.py:954
  15.7 189.2 %reduce-scatter.3.cloned.1.call-start = ((), (), s32[]{:S(2)}) async-start(), calls=%async_computation.2 | async-start | bytes 10616832 | tf_op jit(solution)/shard_map/reduce_scatter | solution.py:971
  144.8 111.0 %reduce-scatter.5.cloned.1.call-start = ((), (), s32[]{:S(2)}) async-start(), calls=%async_computation.3 | async-start | bytes 1474560 | tf_op jit(solution)/shard_map/reduce_scatter | solution.py:1035
  165.5 8.1 %collective-permute-start.3 = (bf16[4,4,4,24,768]{4,3,2,1,0:T(8,128)(2,1)}, bf16[4,4,4,24,768]{4,3,2,1,0:T(8,128)(2,1)}, u32[]{:S(2)}, u32[]{:S(2)}) collective-permute-start(bf16[4,4,4,24,768]{4,3,2,1,0:T(8,128)(2,1)} %get-tuple-element.111), channel_id=1, source_target_pairs={{0,1},{1,0},{2,3},{3,2},{4,5},{5,4},{6,7},{7,6},{8,9},{9,8},{10,11... | collective-permute-start | bytes 7077896 | tf_op jit(solution)/shard_map/ppermute | solution.py:967
  178.0 15.2 %collective-permute-start.4 = (bf16[4,4,24,768]{3,2,1,0:T(8,128)(2,1)}, bf16[4,4,24,768]{3,2,1,0:T(8,128)(2,1)S(1)}, u32[]{:S(2)}, u32[]{:S(2)}) collective-permute-start(bf16[4,4,24,768]{3,2,1,0:T(8,128)(2,1)} %get-tuple-element.123), channel_id=1, source_target_pairs={{0,32},{1,9},{2,34},{3,11},{4,36},{5,13},{6,38},{7,15},{8,40},{9,1... | collective-permute-start | bytes 1769480 | tf_op jit(solution)/shard_map/ppermute | solution.py:992
  178.5 14.7 %collective-permute-start.5 = (bf16[4,4,24,768]{3,2,1,0:T(8,128)(2,1)}, bf16[4,4,24,768]{3,2,1,0:T(8,128)(2,1)S(1)}, u32[]{:S(2)}, u32[]{:S(2)}) collective-permute-start(bf16[4,4,24,768]{3,2,1,0:T(8,128)(2,1)} %get-tuple-element.124), channel_id=1, source_target_pairs={{0,64},{1,17},{2,66},{3,19},{4,68},{5,21},{6,70},{7,23},{8,72},{9,... | collective-permute-start | bytes 1769480 | tf_op jit(solution)/shard_map/ppermute | solution.py:992
  180.9 15.5 %collective-permute-start.6 = (bf16[4,4,24,768]{3,2,1,0:T(8,128)(2,1)}, bf16[4,4,24,768]{3,2,1,0:T(8,128)(2,1)S(1)}, u32[]{:S(2)}, u32[]{:S(2)}) collective-permute-start(bf16[4,4,24,768]{3,2,1,0:T(8,128)(2,1)} %get-tuple-element.125), channel_id=1, source_target_pairs={{0,96},{1,25},{2,98},{3,27},{4,100},{5,29},{6,102},{7,31},{8,104},... | collective-permute-start | bytes 1769480 | tf_op jit(solution)/shard_map/ppermute | solution.py:992
  196.4 8.4 %collective-permute-start.7 = (bf16[4,4,4,16,896]{4,3,2,1,0:T(8,128)(2,1)}, bf16[4,4,4,16,896]{4,3,2,1,0:T(8,128)(2,1)}, u32[]{:S(2)}, u32[]{:S(2)}) collective-permute-start(bf16[4,4,4,16,896]{4,3,2,1,0:T(8,128)(2,1)} %get-tuple-element.126), channel_id=1, source_target_pairs={{0,1},{1,0},{2,3},{3,2},{4,5},{5,4},{6,7},{7,6},{8,9},{9,8},{10,11... | collective-permute-start | bytes 5505032 | tf_op jit(solution)/shard_map/ppermute | solution.py:967
  204.9 5.2 %collective-permute-start.8 = (bf16[4,4,4,24,768]{4,3,2,1,0:T(8,128)(2,1)}, bf16[4,4,4,24,768]{4,3,2,1,0:T(8,128)(2,1)}, u32[]{:S(2)}, u32[]{:S(2)}) collective-permute-start(bf16[4,4,4,24,768]{4,3,2,1,0:T(8,128)(2,1)} %get-tuple-element.136), channel_id=1, source_target_pairs={{0,1},{1,0},{2,3},{3,2},{4,5},{5,4},{6,7},{7,6},{8,9},{9,8},{10,11... | collective-permute-start | bytes 7077896 | tf_op jit(solution)/shard_map/ppermute | solution.py:967
  214.6 16.9 %collective-permute-start.9 = (bf16[4,4,24,768]{3,2,1,0:T(8,128)(2,1)}, bf16[4,4,24,768]{3,2,1,0:T(8,128)(2,1)S(1)}, u32[]{:S(2)}, u32[]{:S(2)}) collective-permute-start(bf16[4,4,24,768]{3,2,1,0:T(8,128)(2,1)} %get-tuple-element.147), channel_id=1, source_target_pairs={{0,32},{1,9},{2,34},{3,11},{4,36},{5,13},{6,38},{7,15},{8,40},{9,1... | collective-permute-start | bytes 1769480 | tf_op jit(solution)/shard_map/ppermute | solution.py:992
  215.2 20.3 %collective-permute-start.10 = (bf16[4,4,24,768]{3,2,1,0:T(8,128)(2,1)}, bf16[4,4,24,768]{3,2,1,0:T(8,128)(2,1)S(1)}, u32[]{:S(2)}, u32[]{:S(2)}) collective-permute-start(bf16[4,4,24,768]{3,2,1,0:T(8,128)(2,1)} %get-tuple-element.148), channel_id=1, source_target_pairs={{0,64},{1,17},{2,66},{3,19},{4,68},{5,21},{6,70},{7,23},{8,72},{9,... | collective-permute-start | bytes 1769480 | tf_op jit(solution)/shard_map/ppermute | solution.py:992
  217.6 21.6 %collective-permute-start.11 = (bf16[4,4,24,768]{3,2,1,0:T(8,128)(2,1)}, bf16[4,4,24,768]{3,2,1,0:T(8,128)(2,1)}, u32[]{:S(2)}, u32[]{:S(2)}) collective-permute-start(bf16[4,4,24,768]{3,2,1,0:T(8,128)(2,1)} %get-tuple-element.149), channel_id=1, source_target_pairs={{0,96},{1,25},{2,98},{3,27},{4,100},{5,29},{6,102},{7,31},{8,104},... | collective-permute-start | bytes 1769480 | tf_op jit(solution)/shard_map/ppermute | solution.py:992
  218.1 30.0 %collective-permute-start.15 = (bf16[4,4,16,896]{3,2,1,0:T(8,128)(2,1)}, bf16[4,4,16,896]{3,2,1,0:T(8,128)(2,1)}, u32[]{:S(2)}, u32[]{:S(2)}) collective-permute-start(bf16[4,4,16,896]{3,2,1,0:T(8,128)(2,1)} %get-tuple-element.159), channel_id=1, source_target_pairs={{0,2},{1,3},{2,4},{3,5},{4,6},{5,7},{6,0},{7,1},{8,10},{9,11},{10,... | collective-permute-start | bytes 1376264 | tf_op jit(solution)/shard_map/ppermute | solution.py:992
  219.6 29.9 %collective-permute-start.16 = (bf16[4,4,16,896]{3,2,1,0:T(8,128)(2,1)}, bf16[4,4,16,896]{3,2,1,0:T(8,128)(2,1)}, u32[]{:S(2)}, u32[]{:S(2)}) collective-permute-start(bf16[4,4,16,896]{3,2,1,0:T(8,128)(2,1)} %get-tuple-element.160), channel_id=1, source_target_pairs={{0,4},{1,5},{2,6},{3,7},{4,0},{5,1},{6,2},{7,3},{8,12},{9,13},{10,... | collective-permute-start | bytes 1376264 | tf_op jit(solution)/shard_map/ppermute | solution.py:992
  231.5 17.9 %collective-permute-start.17 = (bf16[4,4,16,896]{3,2,1,0:T(8,128)(2,1)}, bf16[4,4,16,896]{3,2,1,0:T(8,128)(2,1)}, u32[]{:S(2)}, u32[]{:S(2)}) collective-permute-start(bf16[4,4,16,896]{3,2,1,0:T(8,128)(2,1)} %get-tuple-element.161), channel_id=1, source_target_pairs={{0,6},{1,7},{2,0},{3,1},{4,2},{5,3},{6,4},{7,5},{8,14},{9,15},{10,... | collective-permute-start | bytes 1376264 | tf_op jit(solution)/shard_map/ppermute | solution.py:992
  240.7 21.2 %collective-permute-start.12 = (bf16[4,48,768]{2,1,0:T(8,128)(2,1)S(1)}, bf16[4,48,768]{2,1,0:T(8,128)(2,1)S(1)}, u32[]{:S(2)}, u32[]{:S(2)}) collective-permute-start(bf16[4,48,768]{2,1,0:T(8,128)(2,1)S(1)} %get-tuple-element.155), channel_id=1, source_target_pairs={{0,8},{1,33},{2,10},{3,35},{4,12},{5,37},{6,14},{7,39},{8,16},{9,4... | collective-permute-start | bytes 884744 | tf_op jit(solution)/shard_map/ppermute | solution.py:992
  245.2 16.7 %collective-permute-start.13 = (bf16[4,48,768]{2,1,0:T(8,128)(2,1)S(1)}, bf16[4,48,768]{2,1,0:T(8,128)(2,1)S(1)}, u32[]{:S(2)}, u32[]{:S(2)}) collective-permute-start(bf16[4,48,768]{2,1,0:T(8,128)(2,1)S(1)} %get-tuple-element.156), channel_id=1, source_target_pairs={{0,16},{1,65},{2,18},{3,67},{4,20},{5,69},{6,22},{7,71},{8,24},{9,... | collective-permute-start | bytes 884744 | tf_op jit(solution)/shard_map/ppermute | solution.py:992
  248.0 13.8 %collective-permute-start.14 = (bf16[4,48,768]{2,1,0:T(8,128)(2,1)S(1)}, bf16[4,48,768]{2,1,0:T(8,128)(2,1)S(1)}, u32[]{:S(2)}, u32[]{:S(2)}) collective-permute-start(bf16[4,48,768]{2,1,0:T(8,128)(2,1)S(1)} %get-tuple-element.157), channel_id=1, source_target_pairs={{0,24},{1,97},{2,26},{3,99},{4,28},{5,101},{6,30},{7,103},{8,0},{9... | collective-permute-start | bytes 884744 | tf_op jit(solution)/shard_map/ppermute | solution.py:992
  251.0 4.9 %collective-permute-start.18 = (bf16[4,16,896]{2,1,0:T(8,128)(2,1)S(1)}, bf16[4,16,896]{2,1,0:T(8,128)(2,1)S(1)}, u32[]{:S(2)}, u32[]{:S(2)}) collective-permute-start(bf16[4,16,896]{2,1,0:T(8,128)(2,1)S(1)} %get-tuple-element.163), channel_id=1, source_target_pairs={{0,32},{1,33},{2,34},{3,35},{4,36},{5,37},{6,38},{7,39},{8,40},{9,... | collective-permute-start | bytes 344072 | tf_op jit(solution)/shard_map/ppermute | solution.py:992
  251.2 6.3 %collective-permute-start.19 = (bf16[4,16,896]{2,1,0:T(8,128)(2,1)S(1)}, bf16[4,16,896]{2,1,0:T(8,128)(2,1)S(1)}, u32[]{:S(2)}, u32[]{:S(2)}) collective-permute-start(bf16[4,16,896]{2,1,0:T(8,128)(2,1)S(1)} %get-tuple-element.164), channel_id=1, source_target_pairs={{0,64},{1,65},{2,66},{3,67},{4,68},{5,69},{6,70},{7,71},{8,72},{9,... | collective-permute-start | bytes 344072 | tf_op jit(solution)/shard_map/ppermute | solution.py:992
  255.8 6.0 %collective-permute-start.20 = (bf16[4,16,896]{2,1,0:T(8,128)(2,1)S(1)}, bf16[4,16,896]{2,1,0:T(8,128)(2,1)S(1)}, u32[]{:S(2)}, u32[]{:S(2)}) collective-permute-start(bf16[4,16,896]{2,1,0:T(8,128)(2,1)S(1)} %get-tuple-element.165), channel_id=1, source_target_pairs={{0,96},{1,97},{2,98},{3,99},{4,100},{5,101},{6,102},{7,103},{8,104... | collective-permute-start | bytes 344072 | tf_op jit(solution)/shard_map/ppermute | solution.py:992
  263.0 7.9 %collective-permute-start.21 = (bf16[48,768]{1,0:T(8,128)(2,1)S(1)}, bf16[48,768]{1,0:T(8,128)(2,1)S(1)}, u32[]{:S(2)}, u32[]{:S(2)}) collective-permute-start(bf16[48,768]{1,0:T(8,128)(2,1)S(1)} %get-tuple-element.167), channel_id=1, source_target_pairs={{0,2},{1,3},{2,4},{3,5},{4,6},{5,7},{6,0},{7,1},{8,10},{9,11},{10,... | collective-permute-start | bytes 221192 | tf_op jit(solution)/shard_map/ppermute | solution.py:992
  265.1 10.2 %collective-permute-start.24 = (bf16[72,768]{1,0:T(8,128)(2,1)S(1)}, bf16[72,768]{1,0:T(8,128)(2,1)S(1)}, u32[]{:S(2)}, u32[]{:S(2)}) collective-permute-start(bf16[72,768]{1,0:T(8,128)(2,1)S(1)} %get-tuple-element.171), channel_id=1, source_target_pairs={{0,8},{1,9},{2,10},{3,11},{4,12},{5,13},{6,14},{7,15},{8,16},{9,17... | collective-permute-start | bytes 331784 | tf_op jit(solution)/shard_map/ppermute | solution.py:992
  265.2 10.0 %collective-permute-start.25 = (bf16[72,768]{1,0:T(8,128)(2,1)S(1)}, bf16[72,768]{1,0:T(8,128)(2,1)S(1)}, u32[]{:S(2)}, u32[]{:S(2)}) collective-permute-start(bf16[72,768]{1,0:T(8,128)(2,1)S(1)} %get-tuple-element.172), channel_id=1, source_target_pairs={{0,16},{1,17},{2,18},{3,19},{4,20},{5,21},{6,22},{7,23},{8,24},{9,... | collective-permute-start | bytes 331784 | tf_op jit(solution)/shard_map/ppermute | solution.py:992
  266.5 8.7 %collective-permute-start.26 = (bf16[72,768]{1,0:T(8,128)(2,1)S(1)}, bf16[72,768]{1,0:T(8,128)(2,1)S(1)}, u32[]{:S(2)}, u32[]{:S(2)}) collective-permute-start(bf16[72,768]{1,0:T(8,128)(2,1)S(1)} %get-tuple-element.173), channel_id=1, source_target_pairs={{0,24},{1,25},{2,26},{3,27},{4,28},{5,29},{6,30},{7,31},{8,0},{9,1... | collective-permute-start | bytes 331784 | tf_op jit(solution)/shard_map/ppermute | solution.py:992
  268.3 5.9 %collective-permute-start.22 = (bf16[48,768]{1,0:T(8,128)(2,1)S(1)}, bf16[48,768]{1,0:T(8,128)(2,1)S(1)}, u32[]{:S(2)}, u32[]{:S(2)}) collective-permute-start(bf16[48,768]{1,0:T(8,128)(2,1)S(1)} %get-tuple-element.168), channel_id=1, source_target_pairs={{0,4},{1,5},{2,6},{3,7},{4,0},{5,1},{6,2},{7,3},{8,12},{9,13},{10,... | collective-permute-start | bytes 221192 | tf_op jit(solution)/shard_map/ppermute | solution.py:992
  270.9 4.4 %collective-permute-start.23 = (bf16[48,768]{1,0:T(8,128)(2,1)S(1)}, bf16[48,768]{1,0:T(8,128)(2,1)S(1)}, u32[]{:S(2)}, u32[]{:S(2)}) collective-permute-start(bf16[48,768]{1,0:T(8,128)(2,1)S(1)} %get-tuple-element.169), channel_id=1, source_target_pairs={{0,6},{1,7},{2,0},{3,1},{4,2},{5,3},{6,4},{7,5},{8,14},{9,15},{10,... | collective-permute-start | bytes 221192 | tf_op jit(solution)/shard_map/ppermute | solution.py:992
  276.0 4.3 %collective-permute-start.28 = (bf16[3,6,768]{2,1,0:T(8,128)(2,1)S(1)}, bf16[3,6,768]{2,1,0:T(8,128)(2,1)S(1)}, u32[]{:S(2)}, u32[]{:S(2)}) collective-permute-start(bf16[3,6,768]{2,1,0:T(8,128)(2,1)S(1)} %get-tuple-element.178), channel_id=1, source_target_pairs={{0,2},{1,3},{2,0},{3,1},{4,6},{5,7},{6,4},{7,5},{8,10},{9,11},{10,... | collective-permute-start | bytes 82952 | tf_op jit(solution)/shard_map/ppermute | solution.py:954
  276.5 3.8 %collective-permute-start.29 = (bf16[3,6,768]{2,1,0:T(8,128)(2,1)S(1)}, bf16[3,6,768]{2,1,0:T(8,128)(2,1)S(1)}, u32[]{:S(2)}, u32[]{:S(2)}) collective-permute-start(bf16[3,6,768]{2,1,0:T(8,128)(2,1)S(1)} %get-tuple-element.179), channel_id=1, source_target_pairs={{0,3},{1,2},{2,1},{3,0},{4,7},{5,6},{6,5},{7,4},{8,11},{9,10},{10,... | collective-permute-start | bytes 82952 | tf_op jit(solution)/shard_map/ppermute | solution.py:954
  (7 other events, 54.6 us)
Sparse Core Ops, SparseCore 0:
  15.8 89.9 all-gather.4
  144.9 56.8 reduce-scatter.2
  205.7 30.4 reduce-scatter.4

commit v7 on v6

--- a/solution.py
+++ b/solution.py
@@ -983,7 +983,7 @@
 
 def deliver(pieces, axes):
     came = [pieces[0]]
-    for hop in range(1, 4):
+    for hop in (2, 1, 3):
         pairs = []
         for dev in range(DEVICES):
             stride = STRIDES[axes[dev % 2]]
@@ -1039,6 +1039,7 @@
     pieces, col = barrier((split((own, other), places[0]), col))
     row = deliver(pieces, STAGES[0])
     col = summed(col)
+    table, ffn = barrier((table, ffn))
     table = deliver(split(table, y_place), TABLE_STAGES[1])
     rows = deliver(second_split(row, col, places[1]), STAGES[1])
     pieces = third_split(rows, table, ffn, places[2], z_place)

time: 290 us -> 292 us (level)
  transfers between devices with their start and end apart: 33 -> 33, of which waited for: 13 -> 14; matrix products, arithmetic and copies ran while one was open for 2% -> 2% of each run, Pallas kernels for 23% -> 23%
where the time goes in v7:
time: 292 us; the launch traced here: 288 us
  Pallas kernels  106 us (36%)
  waiting for transfers between devices  86.1 us (29%)
  starting transfers between devices  37.3 us (13%)
  blocking collectives  31.4 us (11%)
  between operations  16 us (5%)
  local copies, waits for them, and re-layouts  7.4 us (3%)
  other arithmetic  4.58 us (2%)
    all_gather x1, waiting for transfers between devices, gather(): gathered = lax.all_gather(packed, AXES, axis=0, tiled=False)  50.8 us
    pallas_call x1, Pallas kernels, forward_call(): pl.pallas_call(forward_kernel, name='forward', in_specs=[SMEM, VMEM, VMEM...  39 us
    ppermute x21, starting transfers between devices, deliver(): came.append(lax.ppermute(pieces[hop], AXES, pairs))  32.4 us
    all_gather x1, blocking collectives, gather(): lines = lax.all_gather(line, AXES, axis=0, tiled=False).astype(F32)  31.4 us
    ppermute x21, waiting for transfers between devices, deliver(): came.append(lax.ppermute(pieces[hop], AXES, pairs))  29.7 us
    pallas_call x1, Pallas kernels, column_call(): pl.pallas_call(column_kernel, name='column_back', in_specs=[SMEM, VMEM, V...  20.5 us
    pallas_call x4, Pallas kernels, split(): pl.pallas_call(split_kernel, name='split_shares', grid=(4,) if large else...  14.5 us
    pallas_call x1, Pallas kernels, row_input_call(): pl.pallas_call(row_input_kernel, name='row_input', in_specs=[SMEM, VMEM,...  12.1 us
  transfers between devices with their start and end apart: 33, of which 14 were waited for; matrix products, arithmetic and copies ran while one was open for 2% of the time, Pallas kernels for 23%

profile of v7, /device:TPU:24, one launch (start us, length us, event | category | flops | bytes accessed | tf_op | source)
XLA Modules:
  0.0 288.4 jit_solution(9898959612497728384)
XLA Ops:
  9.1 1.6 collective-permute-start.1
  17.7 2.2 concatenate.19
  20.7 31.4 %all-gather.2 = bf16[128,1,128]{2,1,0:T(2,128)(2,1)S(1)} all-gather(bf16[1,1,128]{2,1,0:T(2,128)(2,1)S(1)} %fusion.1), channel_id=2, replica_groups=mesh['y'=4,'z'=4,'x'=4,'c'=2] {'y','z','x','c'}, dimensions={0}, use_global_device_ids=true | all-gather | bytes 33024 | tf_op jit(solution)/shard_map/all_gather | solution.py:1008
  55.0 50.8 %all-gather.5.cloned.1.call-done = bf16[14336,768]{1,0:T(8,128)(2,1)} async-done(((bf16[112,768]{1,0:T(8,128)(2,1)}), bf16[14336,768]{1,0:T(8,128)(2,1)}) %all-gather.5.cloned.1.call-update) | async-done | bytes 22020112 | tf_op jit(solution)/shard_map/all_gather | solution.py:1005
  105.8 39.0 %forward.1 = (bf16[512,768]{1,0:T(8,128)(2,1)}, f32[512,768]{1,0:T(8,128)}, bf16[10,512,768]{2,1,0:T(8,128)(2,1)}, f32[2,512,768]{2,1,0:T(8,128)}, bf16[8,16,48,768]{3,2,1,0:T(8,128)(2,1)}, /*index=5*/f32[8,768]{1,0:T(8,128)}) custom-call(s32[4]{0:T(128)} %pad_add_fusion.ints, bf16[512,768]{1,0:T(8,128)(2,1)} %bitcast.84, bf16[512,768]{1,0:T(8,128)(2,1)} %bitcast.85, ...), custom_call_target="tpu_custom_call" | custom-call | flops 24000000000 | bytes 50000000 | tf_op jit(solution)/shard_map/forward/pallas_call | solution.py:646
  145.0 20.5 %column_back.1 = (f32[512,768]{1,0:T(8,128)}, bf16[4,4,4,24,768]{4,3,2,1,0:T(8,128)(2,1)}, bf16[4,4,4,24,768]{4,3,2,1,0:T(8,128)(2,1)}, f32[8,768]{1,0:T(8,128)}) custom-call(s32[4]{0:T(128)} %pad_add_fusion.ints, f32[512,768]{1,0:T(8,128)} %get-tuple-element.109.grad_in, f32[16,768]{1,0:T(8,128)} %pad.9.small, bf16[32,4,112,768]{3,2,1,0:T(8,128)(2,1)} %bitcast.81, ...), custom_call_target="tpu_custom_call" | custom-call | flops 10000000000 | bytes 10000000 | tf_op jit(solution)/shard_map/column_back/pallas_call | solution.py:704
  165.9 7.7 %row_heads.1.grads_in = bf16[3,512,768]{2,1,0:T(8,128)(2,1)} custom-call(s32[4]{0:T(128)} %pad_add_fusion.ints, f32[512,768]{1,0:T(8,128)} %get-tuple-element.112.grad_in, bf16[32,4,112,768]{3,2,1,0:T(8,128)(2,1)} %bitcast.82, bf16[10,512,768]{2,1,0:T(8,128)(2,1)} %get-tuple-element.110.saved), custom_call_target="tpu_custom_call" | custom-call | flops 10000000000 | bytes 10000000 | tf_op jit(solution)/shard_map/row_heads/pallas_call | solution.py:680
  173.6 4.4 %split_shares.4 = (bf16[4,4,24,768]{3,2,1,0:T(8,128)(2,1)}, bf16[4,4,24,768]{3,2,1,0:T(8,128)(2,1)}, bf16[4,4,24,768]{3,2,1,0:T(8,128)(2,1)}, bf16[4,4,24,768]{3,2,1,0:T(8,128)(2,1)}) custom-call(s32[1]{0:T(128)} %bitcast.29.place, bf16[4,4,4,24,768]{4,3,2,1,0:T(8,128)(2,1)} %get-tuple-element.115.refs_0_, ...), custom_call_target="tpu_custom_call" | custom-call | flops 1000000 | bytes 1000000 | tf_op jit(solution)/shard_map/split_shares/pallas_call | solution.py:790
  179.4 2.1 collective-permute-start.5
  181.5 12.1 %row_input.1 = (f32[512,768]{1,0:T(8,128)}, bf16[4,4,4,16,896]{4,3,2,1,0:T(8,128)(2,1)}, bf16[4,4,4,16,896]{4,3,2,1,0:T(8,128)(2,1)}) custom-call(s32[4]{0:T(128)} %pad_add_fusion.ints, f32[512,768]{1,0:T(8,128)} %get-tuple-element.112.grad_in, f32[16,768]{1,0:T(8,128)} %pad.9.small, f32[8,768]{1,0:T(8,128)} %get-tuple-element.113.sums_col, ...), custom_call_target="tpu_custom_call" | custom-call | flops 20000000000 | bytes 10000000 | tf_op jit(solution)/shard_map/row_input/pallas_call | solution.py:747
  193.8 2.1 collective-permute-done.6.refs_3_
  196.0 8.5 %row_weights.1 = (bf16[4,4,4,24,768]{4,3,2,1,0:T(8,128)(2,1)}, bf16[4,4,4,24,768]{4,3,2,1,0:T(8,128)(2,1)}) custom-call(s32[4]{0:T(128)} %pad_add_fusion.ints, f32[512,768]{1,0:T(8,128)} %get-tuple-element.112.grad_in, bf16[10,512,768]{2,1,0:T(8,128)(2,1)} %get-tuple-element.110.saved, bf16[3,512,768]{2,1,0:T(8,128)(2,1)} %row_heads.1.grads_in), custom_call_target="tpu_custom_call" | custom-call | flops 1000000 | bytes 100000 | tf_op jit(solution)/shard_map/row_weights/pallas_call | solution.py:727
  205.0 4.0 %split_shares.5 = (bf16[4,4,16,896]{3,2,1,0:T(8,128)(2,1)}, bf16[4,4,16,896]{3,2,1,0:T(8,128)(2,1)}, bf16[4,4,16,896]{3,2,1,0:T(8,128)(2,1)}, bf16[4,4,16,896]{3,2,1,0:T(8,128)(2,1)}) custom-call(s32[1]{0:T(128)} %bitcast.32.place, bf16[4,4,4,16,896]{4,3,2,1,0:T(8,128)(2,1)} %get-tuple-element.125.refs_0_, ...), custom_call_target="tpu_custom_call" | custom-call | flops 1000000 | bytes 1000000 | tf_op jit(solution)/shard_map/split_shares/pallas_call | solution.py:790
  209.6 4.5 %split_shares.6 = (bf16[4,4,24,768]{3,2,1,0:T(8,128)(2,1)}, bf16[4,4,24,768]{3,2,1,0:T(8,128)(2,1)}, bf16[4,4,24,768]{3,2,1,0:T(8,128)(2,1)}, bf16[4,4,24,768]{3,2,1,0:T(8,128)(2,1)}) custom-call(s32[1]{0:T(128)} %bitcast.29.place, bf16[4,4,4,24,768]{4,3,2,1,0:T(8,128)(2,1)} %get-tuple-element.146.refs_0_, ...), custom_call_target="tpu_custom_call" | custom-call | flops 1000000 | bytes 1000000 | tf_op jit(solution)/shard_map/split_shares/pallas_call | solution.py:790
  215.6 1.5 collective-permute-start.13
  217.6 3.0 %collective-permute-start.9 = (bf16[4,4,16,896]{3,2,1,0:T(8,128)(2,1)}, bf16[4,4,16,896]{3,2,1,0:T(8,128)(2,1)}, u32[]{:S(2)}, u32[]{:S(2)}) collective-permute-start(bf16[4,4,16,896]{3,2,1,0:T(8,128)(2,1)} %get-tuple-element.141), channel_id=1, source_target_pairs={{0,4},{1,5},{2,6},{3,7},{4,0},{5,1},{6,2},{7,3},{8,12},{9,13},{10,... | collective-permute-start | bytes 1376264 | tf_op jit(solution)/shard_map/ppermute | solution.py:992
  221.2 10.1 %collective-permute-done.12.refs_1_ = bf16[4,4,24,768]{3,2,1,0:T(8,128)(2,1)S(1)} collective-permute-done((bf16[4,4,24,768]{3,2,1,0:T(8,128)(2,1)}, bf16[4,4,24,768]{3,2,1,0:T(8,128)(2,1)S(1)}, u32[]{:S(2)}, u32[]{:S(2)}) %collective-permute-start.12) | collective-permute-done | bytes 589856 | tf_op jit(solution)/shard_map/ppermute | solution.py:992
  231.3 2.7 collective-permute-start.11
  235.4 1.8 collective-permute-done.13.refs_2_
  237.2 4.1 %collective-permute-done.14.refs_3_ = bf16[4,4,24,768]{3,2,1,0:T(8,128)(2,1)} collective-permute-done((bf16[4,4,24,768]{3,2,1,0:T(8,128)(2,1)}, bf16[4,4,24,768]{3,2,1,0:T(8,128)(2,1)}, u32[]{:S(2)}, u32[]{:S(2)}) %collective-permute-start.14) | collective-permute-done | bytes 589856 | tf_op jit(solution)/shard_map/ppermute | solution.py:992
  242.7 3.4 %collective-permute-start.15 = (bf16[4,48,768]{2,1,0:T(8,128)(2,1)S(1)}, bf16[4,48,768]{2,1,0:T(8,128)(2,1)S(1)}, u32[]{:S(2)}, u32[]{:S(2)}) collective-permute-start(bf16[4,48,768]{2,1,0:T(8,128)(2,1)S(1)} %get-tuple-element.165), channel_id=1, source_target_pairs={{0,16},{1,65},{2,18},{3,67},{4,20},{5,69},{6,22},{7,71},{8,24},{9,... | collective-permute-start | bytes 884744 | tf_op jit(solution)/shard_map/ppermute | solution.py:992
  246.2 3.2 %collective-permute-start.17 = (bf16[4,48,768]{2,1,0:T(8,128)(2,1)S(1)}, bf16[4,48,768]{2,1,0:T(8,128)(2,1)S(1)}, u32[]{:S(2)}, u32[]{:S(2)}) collective-permute-start(bf16[4,48,768]{2,1,0:T(8,128)(2,1)S(1)} %get-tuple-element.167), channel_id=1, source_target_pairs={{0,24},{1,97},{2,26},{3,99},{4,28},{5,101},{6,30},{7,103},{8,0},{9... | collective-permute-start | bytes 884744 | tf_op jit(solution)/shard_map/ppermute | solution.py:992
  249.4 1.5 split_shares.7
  251.0 1.7 collective-permute-start.18
  254.0 3.4 %collective-permute-done.18.refs_5_ = bf16[4,16,896]{2,1,0:T(8,128)(2,1)S(1)} collective-permute-done((bf16[4,16,896]{2,1,0:T(8,128)(2,1)S(1)}, bf16[4,16,896]{2,1,0:T(8,128)(2,1)S(1)}, u32[]{:S(2)}, u32[]{:S(2)}) %collective-permute-start.18) | collective-permute-done | bytes 114720 | tf_op jit(solution)/shard_map/ppermute | solution.py:992
  257.7 5.6 %collective-permute-done.20.refs_7_ = bf16[4,16,896]{2,1,0:T(8,128)(2,1)S(1)} collective-permute-done((bf16[4,16,896]{2,1,0:T(8,128)(2,1)S(1)}, bf16[4,16,896]{2,1,0:T(8,128)(2,1)S(1)}, u32[]{:S(2)}, u32[]{:S(2)}) %collective-permute-start.20) | collective-permute-done | bytes 114720 | tf_op jit(solution)/shard_map/ppermute | solution.py:992
  264.5 2.7 collective-permute-start.21
  268.1 2.4 collective-permute-start.26
  271.0 2.7 collective-permute-start.23
  273.7 2.3 collective-permute-done.22.refs_2_
  276.9 1.8 collective-permute-start.29
  278.7 2.4 collective-permute-done.28.three
  (84 shorter events, 25.2 us)
Async XLA Ops:
  7.2 98.6 %all-gather.5.cloned.1.call-start = ((), (), s32[]{:S(2)}) async-start(), calls=%async_computation.4 | async-start | bytes 22192128 | tf_op jit(solution)/shard_map/all_gather | solution.py:1005
  9.0 2.7 collective-permute-start.2
  9.1 4.0 %collective-permute-start.1 = (bf16[3,6,768]{2,1,0:T(8,128)(2,1)S(1)}, bf16[3,6,768]{2,1,0:T(8,128)(2,1)S(1)}, u32[]{:S(2)}, u32[]{:S(2)}) collective-permute-start(bf16[3,6,768]{2,1,0:T(8,128)(2,1)S(1)} %get-tuple-element.206), channel_id=1, source_target_pairs={{0,2},{1,3},{2,0},{3,1},{4,6},{5,7},{6,4},{7,5},{8,10},{9,11},{10,... | collective-permute-start | bytes 82952 | tf_op jit(solution)/shard_map/ppermute | solution.py:954
  10.6 3.4 %collective-permute-start = (bf16[3,6,768]{2,1,0:T(8,128)(2,1)S(1)}, bf16[3,6,768]{2,1,0:T(8,128)(2,1)S(1)}, u32[]{:S(2)}, u32[]{:S(2)}) collective-permute-start(bf16[3,6,768]{2,1,0:T(8,128)(2,1)S(1)} %get-tuple-element.207), channel_id=1, source_target_pairs={{0,3},{1,2},{2,1},{3,0},{4,7},{5,6},{6,5},{7,4},{8,11},{9,10},{10,... | collective-permute-start | bytes 82952 | tf_op jit(solution)/shard_map/ppermute | solution.py:954
  15.7 188.8 %reduce-scatter.3.cloned.1.call-start = ((), (), s32[]{:S(2)}) async-start(), calls=%async_computation.2 | async-start | bytes 10616832 | tf_op jit(solution)/shard_map/reduce_scatter | solution.py:971
  144.8 104.6 %reduce-scatter.5.cloned.1.call-start = ((), (), s32[]{:S(2)}) async-start(), calls=%async_computation.3 | async-start | bytes 1474560 | tf_op jit(solution)/shard_map/reduce_scatter | solution.py:1035
  165.5 8.1 %collective-permute-start.3 = (bf16[4,4,4,24,768]{4,3,2,1,0:T(8,128)(2,1)}, bf16[4,4,4,24,768]{4,3,2,1,0:T(8,128)(2,1)}, u32[]{:S(2)}, u32[]{:S(2)}) collective-permute-start(bf16[4,4,4,24,768]{4,3,2,1,0:T(8,128)(2,1)} %get-tuple-element.116), channel_id=1, source_target_pairs={{0,1},{1,0},{2,3},{3,2},{4,5},{5,4},{6,7},{7,6},{8,9},{9,8},{10,11... | collective-permute-start | bytes 7077896 | tf_op jit(solution)/shard_map/ppermute | solution.py:967
  178.0 15.7 %collective-permute-start.4 = (bf16[4,4,24,768]{3,2,1,0:T(8,128)(2,1)}, bf16[4,4,24,768]{3,2,1,0:T(8,128)(2,1)S(1)}, u32[]{:S(2)}, u32[]{:S(2)}) collective-permute-start(bf16[4,4,24,768]{3,2,1,0:T(8,128)(2,1)} %get-tuple-element.129), channel_id=1, source_target_pairs={{0,64},{1,17},{2,66},{3,19},{4,68},{5,21},{6,70},{7,23},{8,72},{9,... | collective-permute-start | bytes 1769480 | tf_op jit(solution)/shard_map/ppermute | solution.py:992
  179.4 14.4 %collective-permute-start.5 = (bf16[4,4,24,768]{3,2,1,0:T(8,128)(2,1)}, bf16[4,4,24,768]{3,2,1,0:T(8,128)(2,1)S(1)}, u32[]{:S(2)}, u32[]{:S(2)}) collective-permute-start(bf16[4,4,24,768]{3,2,1,0:T(8,128)(2,1)} %get-tuple-element.130), channel_id=1, source_target_pairs={{0,32},{1,9},{2,34},{3,11},{4,36},{5,13},{6,38},{7,15},{8,40},{9,1... | collective-permute-start | bytes 1769480 | tf_op jit(solution)/shard_map/ppermute | solution.py:992
  181.5 14.4 %collective-permute-start.6 = (bf16[4,4,24,768]{3,2,1,0:T(8,128)(2,1)}, bf16[4,4,24,768]{3,2,1,0:T(8,128)(2,1)S(1)}, u32[]{:S(2)}, u32[]{:S(2)}) collective-permute-start(bf16[4,4,24,768]{3,2,1,0:T(8,128)(2,1)} %get-tuple-element.131), channel_id=1, source_target_pairs={{0,96},{1,25},{2,98},{3,27},{4,100},{5,29},{6,102},{7,31},{8,104},... | collective-permute-start | bytes 1769480 | tf_op jit(solution)/shard_map/ppermute | solution.py:992
  195.9 8.5 %collective-permute-start.7 = (bf16[4,4,4,16,896]{4,3,2,1,0:T(8,128)(2,1)}, bf16[4,4,4,16,896]{4,3,2,1,0:T(8,128)(2,1)}, u32[]{:S(2)}, u32[]{:S(2)}) collective-permute-start(bf16[4,4,4,16,896]{4,3,2,1,0:T(8,128)(2,1)} %get-tuple-element.132), channel_id=1, source_target_pairs={{0,1},{1,0},{2,3},{3,2},{4,5},{5,4},{6,7},{7,6},{8,9},{9,8},{10,11... | collective-permute-start | bytes 5505032 | tf_op jit(solution)/shard_map/ppermute | solution.py:967
  204.5 5.2 %collective-permute-start.8 = (bf16[4,4,4,24,768]{4,3,2,1,0:T(8,128)(2,1)}, bf16[4,4,4,24,768]{4,3,2,1,0:T(8,128)(2,1)}, u32[]{:S(2)}, u32[]{:S(2)}) collective-permute-start(bf16[4,4,4,24,768]{4,3,2,1,0:T(8,128)(2,1)} %get-tuple-element.139), channel_id=1, source_target_pairs={{0,1},{1,0},{2,3},{3,2},{4,5},{5,4},{6,7},{7,6},{8,9},{9,8},{10,11... | collective-permute-start | bytes 7077896 | tf_op jit(solution)/shard_map/ppermute | solution.py:967
  214.1 17.2 %collective-permute-start.12 = (bf16[4,4,24,768]{3,2,1,0:T(8,128)(2,1)}, bf16[4,4,24,768]{3,2,1,0:T(8,128)(2,1)S(1)}, u32[]{:S(2)}, u32[]{:S(2)}) collective-permute-start(bf16[4,4,24,768]{3,2,1,0:T(8,128)(2,1)} %get-tuple-element.157), channel_id=1, source_target_pairs={{0,64},{1,17},{2,66},{3,19},{4,68},{5,21},{6,70},{7,23},{8,72},{9,... | collective-permute-start | bytes 1769480 | tf_op jit(solution)/shard_map/ppermute | solution.py:992
  215.6 21.6 %collective-permute-start.13 = (bf16[4,4,24,768]{3,2,1,0:T(8,128)(2,1)}, bf16[4,4,24,768]{3,2,1,0:T(8,128)(2,1)S(1)}, u32[]{:S(2)}, u32[]{:S(2)}) collective-permute-start(bf16[4,4,24,768]{3,2,1,0:T(8,128)(2,1)} %get-tuple-element.158), channel_id=1, source_target_pairs={{0,32},{1,9},{2,34},{3,11},{4,36},{5,13},{6,38},{7,15},{8,40},{9,1... | collective-permute-start | bytes 1769480 | tf_op jit(solution)/shard_map/ppermute | solution.py:992
  217.1 24.1 %collective-permute-start.14 = (bf16[4,4,24,768]{3,2,1,0:T(8,128)(2,1)}, bf16[4,4,24,768]{3,2,1,0:T(8,128)(2,1)}, u32[]{:S(2)}, u32[]{:S(2)}) collective-permute-start(bf16[4,4,24,768]{3,2,1,0:T(8,128)(2,1)} %get-tuple-element.159), channel_id=1, source_target_pairs={{0,96},{1,25},{2,98},{3,27},{4,100},{5,29},{6,102},{7,31},{8,104},... | collective-permute-start | bytes 1769480 | tf_op jit(solution)/shard_map/ppermute | solution.py:992
  217.6 28.6 %collective-permute-start.9 = (bf16[4,4,16,896]{3,2,1,0:T(8,128)(2,1)}, bf16[4,4,16,896]{3,2,1,0:T(8,128)(2,1)}, u32[]{:S(2)}, u32[]{:S(2)}) collective-permute-start(bf16[4,4,16,896]{3,2,1,0:T(8,128)(2,1)} %get-tuple-element.141), channel_id=1, source_target_pairs={{0,4},{1,5},{2,6},{3,7},{4,0},{5,1},{6,2},{7,3},{8,12},{9,13},{10,... | collective-permute-start | bytes 1376264 | tf_op jit(solution)/shard_map/ppermute | solution.py:992
  220.6 28.8 %collective-permute-start.10 = (bf16[4,4,16,896]{3,2,1,0:T(8,128)(2,1)}, bf16[4,4,16,896]{3,2,1,0:T(8,128)(2,1)}, u32[]{:S(2)}, u32[]{:S(2)}) collective-permute-start(bf16[4,4,16,896]{3,2,1,0:T(8,128)(2,1)} %get-tuple-element.142), channel_id=1, source_target_pairs={{0,2},{1,3},{2,4},{3,5},{4,6},{5,7},{6,0},{7,1},{8,10},{9,11},{10,... | collective-permute-start | bytes 1376264 | tf_op jit(solution)/shard_map/ppermute | solution.py:992
  231.3 18.1 %collective-permute-start.11 = (bf16[4,4,16,896]{3,2,1,0:T(8,128)(2,1)}, bf16[4,4,16,896]{3,2,1,0:T(8,128)(2,1)}, u32[]{:S(2)}, u32[]{:S(2)}) collective-permute-start(bf16[4,4,16,896]{3,2,1,0:T(8,128)(2,1)} %get-tuple-element.143), channel_id=1, source_target_pairs={{0,6},{1,7},{2,0},{3,1},{4,2},{5,3},{6,4},{7,5},{8,14},{9,15},{10,... | collective-permute-start | bytes 1376264 | tf_op jit(solution)/shard_map/ppermute | solution.py:992
  242.7 20.6 %collective-permute-start.15 = (bf16[4,48,768]{2,1,0:T(8,128)(2,1)S(1)}, bf16[4,48,768]{2,1,0:T(8,128)(2,1)S(1)}, u32[]{:S(2)}, u32[]{:S(2)}) collective-permute-start(bf16[4,48,768]{2,1,0:T(8,128)(2,1)S(1)} %get-tuple-element.165), channel_id=1, source_target_pairs={{0,16},{1,65},{2,18},{3,67},{4,20},{5,69},{6,22},{7,71},{8,24},{9,... | collective-permute-start | bytes 884744 | tf_op jit(solution)/shard_map/ppermute | solution.py:992
  246.2 17.2 %collective-permute-start.16 = (bf16[4,48,768]{2,1,0:T(8,128)(2,1)S(1)}, bf16[4,48,768]{2,1,0:T(8,128)(2,1)S(1)}, u32[]{:S(2)}, u32[]{:S(2)}) collective-permute-start(bf16[4,48,768]{2,1,0:T(8,128)(2,1)S(1)} %get-tuple-element.166), channel_id=1, source_target_pairs={{0,8},{1,33},{2,10},{3,35},{4,12},{5,37},{6,14},{7,39},{8,16},{9,4... | collective-permute-start | bytes 884744 | tf_op jit(solution)/shard_map/ppermute | solution.py:992
  246.2 17.1 %collective-permute-start.17 = (bf16[4,48,768]{2,1,0:T(8,128)(2,1)S(1)}, bf16[4,48,768]{2,1,0:T(8,128)(2,1)S(1)}, u32[]{:S(2)}, u32[]{:S(2)}) collective-permute-start(bf16[4,48,768]{2,1,0:T(8,128)(2,1)S(1)} %get-tuple-element.167), channel_id=1, source_target_pairs={{0,24},{1,97},{2,26},{3,99},{4,28},{5,101},{6,30},{7,103},{8,0},{9... | collective-permute-start | bytes 884744 | tf_op jit(solution)/shard_map/ppermute | solution.py:992
  251.0 6.4 %collective-permute-start.18 = (bf16[4,16,896]{2,1,0:T(8,128)(2,1)S(1)}, bf16[4,16,896]{2,1,0:T(8,128)(2,1)S(1)}, u32[]{:S(2)}, u32[]{:S(2)}) collective-permute-start(bf16[4,16,896]{2,1,0:T(8,128)(2,1)S(1)} %get-tuple-element.173), channel_id=1, source_target_pairs={{0,64},{1,65},{2,66},{3,67},{4,68},{5,69},{6,70},{7,71},{8,72},{9,... | collective-permute-start | bytes 344072 | tf_op jit(solution)/shard_map/ppermute | solution.py:992
  252.7 5.0 %collective-permute-start.19 = (bf16[4,16,896]{2,1,0:T(8,128)(2,1)S(1)}, bf16[4,16,896]{2,1,0:T(8,128)(2,1)S(1)}, u32[]{:S(2)}, u32[]{:S(2)}) collective-permute-start(bf16[4,16,896]{2,1,0:T(8,128)(2,1)S(1)} %get-tuple-element.174), channel_id=1, source_target_pairs={{0,32},{1,33},{2,34},{3,35},{4,36},{5,37},{6,38},{7,39},{8,40},{9,... | collective-permute-start | bytes 344072 | tf_op jit(solution)/shard_map/ppermute | solution.py:992
  257.3 6.0 %collective-permute-start.20 = (bf16[4,16,896]{2,1,0:T(8,128)(2,1)S(1)}, bf16[4,16,896]{2,1,0:T(8,128)(2,1)S(1)}, u32[]{:S(2)}, u32[]{:S(2)}) collective-permute-start(bf16[4,16,896]{2,1,0:T(8,128)(2,1)S(1)} %get-tuple-element.175), channel_id=1, source_target_pairs={{0,96},{1,97},{2,98},{3,99},{4,100},{5,101},{6,102},{7,103},{8,104... | collective-permute-start | bytes 344072 | tf_op jit(solution)/shard_map/ppermute | solution.py:992
  264.5 6.5 %collective-permute-start.21 = (bf16[48,768]{1,0:T(8,128)(2,1)S(1)}, bf16[48,768]{1,0:T(8,128)(2,1)S(1)}, u32[]{:S(2)}, u32[]{:S(2)}) collective-permute-start(bf16[48,768]{1,0:T(8,128)(2,1)S(1)} %get-tuple-element.177), channel_id=1, source_target_pairs={{0,4},{1,5},{2,6},{3,7},{4,0},{5,1},{6,2},{7,3},{8,12},{9,13},{10,... | collective-permute-start | bytes 221192 | tf_op jit(solution)/shard_map/ppermute | solution.py:992
  267.2 8.8 %collective-permute-start.24 = (bf16[72,768]{1,0:T(8,128)(2,1)S(1)}, bf16[72,768]{1,0:T(8,128)(2,1)S(1)}, u32[]{:S(2)}, u32[]{:S(2)}) collective-permute-start(bf16[72,768]{1,0:T(8,128)(2,1)S(1)} %get-tuple-element.181), channel_id=1, source_target_pairs={{0,16},{1,17},{2,18},{3,19},{4,20},{5,21},{6,22},{7,23},{8,24},{9,... | collective-permute-start | bytes 331784 | tf_op jit(solution)/shard_map/ppermute | solution.py:992
  267.2 8.8 %collective-permute-start.25 = (bf16[72,768]{1,0:T(8,128)(2,1)S(1)}, bf16[72,768]{1,0:T(8,128)(2,1)S(1)}, u32[]{:S(2)}, u32[]{:S(2)}) collective-permute-start(bf16[72,768]{1,0:T(8,128)(2,1)S(1)} %get-tuple-element.182), channel_id=1, source_target_pairs={{0,8},{1,9},{2,10},{3,11},{4,12},{5,13},{6,14},{7,15},{8,16},{9,17... | collective-permute-start | bytes 331784 | tf_op jit(solution)/shard_map/ppermute | solution.py:992
  268.1 7.9 %collective-permute-start.26 = (bf16[72,768]{1,0:T(8,128)(2,1)S(1)}, bf16[72,768]{1,0:T(8,128)(2,1)S(1)}, u32[]{:S(2)}, u32[]{:S(2)}) collective-permute-start(bf16[72,768]{1,0:T(8,128)(2,1)S(1)} %get-tuple-element.183), channel_id=1, source_target_pairs={{0,24},{1,25},{2,26},{3,27},{4,28},{5,29},{6,30},{7,31},{8,0},{9,1... | collective-permute-start | bytes 331784 | tf_op jit(solution)/shard_map/ppermute | solution.py:992
  270.5 5.6 %collective-permute-start.22 = (bf16[48,768]{1,0:T(8,128)(2,1)S(1)}, bf16[48,768]{1,0:T(8,128)(2,1)S(1)}, u32[]{:S(2)}, u32[]{:S(2)}) collective-permute-start(bf16[48,768]{1,0:T(8,128)(2,1)S(1)} %get-tuple-element.178), channel_id=1, source_target_pairs={{0,2},{1,3},{2,4},{3,5},{4,6},{5,7},{6,0},{7,1},{8,10},{9,11},{10,... | collective-permute-start | bytes 221192 | tf_op jit(solution)/shard_map/ppermute | solution.py:992
  271.0 5.0 %collective-permute-start.23 = (bf16[48,768]{1,0:T(8,128)(2,1)S(1)}, bf16[48,768]{1,0:T(8,128)(2,1)S(1)}, u32[]{:S(2)}, u32[]{:S(2)}) collective-permute-start(bf16[48,768]{1,0:T(8,128)(2,1)S(1)} %get-tuple-element.179), channel_id=1, source_target_pairs={{0,6},{1,7},{2,0},{3,1},{4,2},{5,3},{6,4},{7,5},{8,14},{9,15},{10,... | collective-permute-start | bytes 221192 | tf_op jit(solution)/shard_map/ppermute | solution.py:992
  276.8 4.3 %collective-permute-start.28 = (bf16[3,6,768]{2,1,0:T(8,128)(2,1)S(1)}, bf16[3,6,768]{2,1,0:T(8,128)(2,1)S(1)}, u32[]{:S(2)}, u32[]{:S(2)}) collective-permute-start(bf16[3,6,768]{2,1,0:T(8,128)(2,1)S(1)} %get-tuple-element.188), channel_id=1, source_target_pairs={{0,2},{1,3},{2,0},{3,1},{4,6},{5,7},{6,4},{7,5},{8,10},{9,11},{10,... | collective-permute-start | bytes 82952 | tf_op jit(solution)/shard_map/ppermute | solution.py:954
  276.9 4.2 %collective-permute-start.29 = (bf16[3,6,768]{2,1,0:T(8,128)(2,1)S(1)}, bf16[3,6,768]{2,1,0:T(8,128)(2,1)S(1)}, u32[]{:S(2)}, u32[]{:S(2)}) collective-permute-start(bf16[3,6,768]{2,1,0:T(8,128)(2,1)S(1)} %get-tuple-element.189), channel_id=1, source_target_pairs={{0,3},{1,2},{2,1},{3,0},{4,7},{5,6},{6,5},{7,4},{8,11},{9,10},{10,... | collective-permute-start | bytes 82952 | tf_op jit(solution)/shard_map/ppermute | solution.py:954
  (7 other events, 57.0 us)
Sparse Core Ops, SparseCore 0:
  15.8 89.9 all-gather.4
  144.9 56.8 reduce-scatter.2
  205.1 29.5 reduce-scatter.4
